TPU v7x, 128 devices: a whole 4x4x4 slice. The times are simulated.
128 devices in a mesh: heads: 2 (over z_hi), slab: 64 (over z_lo, y, x, core).
Axes of the slice: x: 4, y: 4, z: 4 (z_hi: 2, z_lo: 2; z = z_hi * 2 + z_lo), core: 2. Of those that a mesh axis runs over, the one named last changes fastest.
Arguments:
- tokens: bfloat16 [64, 384, 3072], P('slab', 'heads'), may hold values from -400 to 400
- qkv_weight: bfloat16 [3072, 4608], P(None, 'heads'), may hold values from -1 to 1
- out_weight: bfloat16 [1536, 3072], P('heads'), may hold values from -0.15625 to 0.15625
- query_gain: float32 [128], replicated, may hold values from 0.6 to 4.5
- key_gain: float32 [128], replicated, may hold values from 0.6 to 4.5
- mod_shift: float32 [3072], replicated, may hold values from -3 to 3
- mod_scale: float32 [3072], replicated, may hold values from -0.5 to 1.5
- branch_gate: float32 [3072], replicated, may hold values from 1 to 3
- block_mask: int32 [64, 27], P('slab'), may hold values 0 or 1
Outputs:
- attended: bfloat16 [64, 384, 3072], P('slab', 'heads')
All inputs are finite; a program needn't handle non-finite values. No bound on the sum of `block_mask` on one device may be relied on, other than what follows from the above.
Results may differ from a plain program's by a relative error of at most 0.0095.
The roundings to bfloat16 on the way count: a program that leaves them out, or rounds other values in their place, can miss the bound.
Values may be sent and summed in bfloat16 or wider, within the bound.
No kernel may reach another device: no remote copies, remote signals or barrier semaphores. Data moves between devices by JAX's collectives and lax.ppermute only.
A program may use at most 320 MiB of HBM per device.

v0:
```python
import jax
import jax.numpy as jnp
import numpy as np
from jax import lax
from jax.experimental import pallas as pl
from jax.experimental.pallas import tpu as pltpu
from jax.sharding import PartitionSpec as P


TILE = 384
HD = 128
MASK_ROWS = 16
NEG = -1e30

HALO = (
    ((0, 0, 1), (0, 2, 4, 6)),
    ((0, 1, 0), (0, 1, 4, 5)),
    ((1, 0, 0), (0, 1, 2, 3)),
    ((0, 1, 1), (0, 4)),
    ((1, 0, 1), (0, 2)),
    ((1, 1, 0), (0, 1)),
    ((1, 1, 1), (0,)),
)
OWN_AT = [((u >> 2) & 1, (u >> 1) & 1, u & 1) for u in range(8)]
HALO_AT = [
    tuple(-1 if moved[d] else ((u >> (2 - d)) & 1) for d in range(3)) for moved, us in HALO for u in us
]


def chip_of(s):
    return ((s >> 4) & 1) * 2 + ((s >> 2) & 1)


def corner_of(s):
    return ((s >> 3) & 1) * 2 + ((s >> 1) & 1)


def slot_of(s, core, p):
    return chip_of(s) ^ p ^ (core * corner_of(s))


def u_base(s):
    ut = ((s >> 4) ^ (s >> 5) ^ 1) & 1
    uh = ((s >> 2) ^ (s >> 3) ^ 1) & 1
    uw = (s ^ (s >> 1) ^ 1) & 1
    return ut * 4 + uh * 2 + uw


def chip_mask(p):
    return ((p >> 1) << 4) | ((p & 1) << 2)


def halo_mask(core, moved):
    mask = (moved[0] << 5) | (moved[1] << 3) | (moved[2] << 1)
    if core:
        mask |= (moved[1] << 4) | (moved[2] << 2)
    return mask


def busy(s):
    return slot_of(s, s & 1, 0) < 3


def to_chip(value, p):
    pairs = [(s, s ^ chip_mask(p)) for s in range(64) if busy(s ^ chip_mask(p))]
    return lax.ppermute(value, "slab", pairs)


def from_chip(value, p):
    pairs = [(s, s ^ chip_mask(p)) for s in range(64) if busy(s)]
    return lax.ppermute(value, "slab", pairs)


def across(value):
    pairs = [(64 * g + s, 64 * (1 - g) + s) for g in range(2) for s in range(64) if busy(s)]
    return lax.ppermute(value, ("heads", "slab"), pairs)


def weight_across(value):
    pairs = [(64 * g + s, 64 * (1 - g) + (s ^ 32)) for g in range(2) for s in range(64)]
    return lax.ppermute(value, ("heads", "slab"), pairs)


def to_core(value):
    return lax.ppermute(value, "slab", [(s, s ^ 1) for s in range(64)])


def to_block(value, moved):
    pairs = [(s, s ^ halo_mask(s & 1, moved)) for s in range(64) if busy(s)]
    return lax.ppermute(value, "slab", pairs)


def to_group(value):
    return lax.ppermute(value, "heads", [(0, 1), (1, 0)])


def whole(shape):
    return pl.BlockSpec(shape, lambda *_: (0,) * len(shape), pipeline_mode=pl.Buffered(1))


def modulate(token_rows, mod_shift, mod_scale):
    token_rows = token_rows.astype(jnp.float32)
    row_mean = jnp.mean(token_rows, axis=-1, keepdims=True)
    centered = token_rows - row_mean
    variance = jnp.mean(centered * centered, axis=-1, keepdims=True)
    return (centered * lax.rsqrt(variance + 1e-06) * (1.0 + mod_scale) + mod_shift).astype(
        jnp.bfloat16
    )


def project_kernel(other, s_ref, x_ref, w_ref, qg_ref, kg_ref, mask_ref, out_ref):
    s = s_ref[0]
    rows = x_ref.shape[0]
    slot = slot_of(s, (s & 1) ^ other, pl.program_id(0))

    @pl.when(slot < 3)
    def _():
        acc = jnp.dot(x_ref[...], w_ref[...], preferred_element_type=jnp.float32).astype(jnp.bfloat16)

        def normed(part, gain):
            part = part.astype(jnp.float32)
            return part * lax.rsqrt(jnp.mean(part * part, axis=-1, keepdims=True) + 1e-06) * gain

        q = normed(acc[:, :HD], qg_ref[...]) * HD ** (-0.5)
        out_ref[0, :rows, :HD] = q.astype(jnp.bfloat16)
        out_ref[0, :rows, HD : 2 * HD] = normed(acc[:, HD : 2 * HD], kg_ref[...]).astype(jnp.bfloat16)
        out_ref[0, :rows, 2 * HD :] = acc[:, 2 * HD :]
        if out_ref.shape[1] > rows:
            out_ref[0, rows:, :] = mask_ref[...]

    @pl.when(slot >= 3)
    def _():
        out_ref[0] = jnp.zeros_like(out_ref[0])


def project(slab_at, x, weight, query_gain, key_gain, mask_rows, other, with_mask):
    rows, width = x.shape
    out_rows = rows + (MASK_ROWS if with_mask else 0)

    def weight_at(i, s_ref):
        s = s_ref[0]
        core = (s & 1) ^ other
        return (0, core * 3 + jnp.minimum(slot_of(s, core, i), 2))

    return pl.pallas_call(
        lambda *refs: project_kernel(other, *refs),
        out_shape=jax.ShapeDtypeStruct((4, out_rows, 3 * HD), jnp.bfloat16),
        grid_spec=pltpu.PrefetchScalarGridSpec(
            num_scalar_prefetch=1,
            grid=(4,),
            in_specs=[
                whole((rows, width)),
                pl.BlockSpec((width, 3 * HD), weight_at),
                whole((1, HD)),
                whole((1, HD)),
                whole((MASK_ROWS, 3 * HD)),
            ],
            out_specs=pl.BlockSpec((1, out_rows, 3 * HD), lambda i, s_ref: (i, 0, 0)),
        ),
        compiler_params=pltpu.CompilerParams(vmem_limit_bytes=7 << 20),
    )(slab_at, x, weight, query_gain, key_gain, mask_rows)


def live_tables():
    table = np.full((8, 8, HD), HD, np.int32)
    for corner in range(8):
        signs = [((corner >> (2 - d)) & 1) * 2 - 1 for d in range(3)]
        for u in range(8):
            for k, at in enumerate(OWN_AT + HALO_AT):
                steps = [at[d] - ((u >> (2 - d)) & 1) for d in range(3)]
                if min(steps) >= -1:
                    table[corner, u, k] = 13 + sum(
                        w * g * t for w, g, t in zip((9, 3, 1), signs, steps, strict=True)
                    )
    return table


def block_of(s):
    return ((s >> 5) & 1) * 4 + corner_of(s)


def part_kernel(s_ref, w_ref, out_ref, sem):
    rows = out_ref.shape[0]
    start = pl.multiple_of((s_ref[0] & 1) * rows, rows)
    copy = pltpu.make_async_copy(w_ref.at[pl.ds(start, rows)], out_ref, sem)
    copy.start()
    copy.wait()


def weight_part(slab_at, weight):
    rows, width = weight.shape
    return pl.pallas_call(
        part_kernel,
        out_shape=jax.ShapeDtypeStruct((rows // 2, width), weight.dtype),
        grid_spec=pltpu.PrefetchScalarGridSpec(
            num_scalar_prefetch=1,
            grid=(1,),
            in_specs=[pl.BlockSpec(memory_space=pl.ANY)],
            out_specs=pl.BlockSpec(memory_space=pl.ANY),
            scratch_shapes=[pltpu.SemaphoreType.DMA(())],
        ),
        compiler_params=pltpu.CompilerParams(vmem_limit_bytes=1 << 20),
        name="weight_part",
    )(slab_at, weight)


def assemble_kernel(s_ref, *refs):
    base = u_base(s_ref[0])
    half = TILE // 2
    spot_ref, q_ref, kv_ref, live_ref = refs[10:14]
    entry = lax.broadcasted_iota(jnp.int32, (HD, HD), 0)
    lane = lax.broadcasted_iota(jnp.int32, (MASK_ROWS, HD), 1)
    for at, halves in enumerate((refs[:5], refs[5:10])):
        keep_ref, core_ref, *near = halves
        pieces = [(keep_ref, 0), (core_ref, 0)] + [(ref, dc) for ref in near for dc in range(2)]
        rows = slice(at * half, (at + 1) * half)
        for r, (ref, dc) in enumerate(pieces):
            u = base ^ r
            q_ref[u, rows] = ref[dc, :half, :HD]
            kv_ref[u, rows] = ref[dc, :half, HD:]
            if at == 0:
                marked = jnp.where(lane == 13, 1.0, ref[dc, half:, :HD].astype(jnp.float32))
                pick = jnp.where(entry == spot_ref[0, pl.ds(u, 1)], 1.0, 0.0)
                live = jnp.dot(
                    marked.astype(jnp.bfloat16),
                    pick.astype(jnp.bfloat16),
                    preferred_element_type=jnp.float32,
                )
                live_ref[pl.ds(u, 1)] = live[:1].astype(jnp.int32)
    for (_, us), send in zip(HALO, refs[14:]):
        for at, u in enumerate(us):
            send[at] = kv_ref[u]


def assemble(slab_at, halves):
    shapes = [
        ((8, TILE, HD), jnp.bfloat16),
        ((8, TILE, 2 * HD), jnp.bfloat16),
        ((8, HD), jnp.int32),
    ] + [((len(us), TILE, 2 * HD), jnp.bfloat16) for _, us in HALO[:4]]
    in_specs = []
    for keep, *_ in halves:
        rows = keep.shape[1]
        in_specs += [whole((1, rows, 3 * HD))] * 2 + [whole((2, rows, 3 * HD))] * 3
    in_specs.append(pl.BlockSpec((1, 8, HD), lambda i, s_ref: (block_of(s_ref[0]), 0, 0)))
    return pl.pallas_call(
        assemble_kernel,
        out_shape=[jax.ShapeDtypeStruct(*shape) for shape in shapes],
        grid_spec=pltpu.PrefetchScalarGridSpec(
            num_scalar_prefetch=1,
            grid=(1,),
            in_specs=in_specs,
            out_specs=[whole(shape) for shape, _ in shapes],
        ),
        compiler_params=pltpu.CompilerParams(vmem_limit_bytes=16 << 20),
        name="assemble",
    )(slab_at, *halves[0], *halves[1], jnp.asarray(live_tables()))


def fold(x, op):
    return op(op(x[:, :HD], x[:, HD : 2 * HD]), x[:, 2 * HD :])


def spread_max(x):
    return jnp.broadcast_to(jnp.max(x, axis=1, keepdims=True), x.shape)


def attend(u, first, count, live_ref, q, kv_ref, s_ref, list_ref, m_ref, l_ref, acc_ref, rescale):
    n = jnp.int32(0)
    for k in range(count):
        list_ref[n] = k
        n = n + live_ref[u, first + k]

    def score(base, group):
        def step(j, _):
            top = m_ref[...]
            for i in range(group):
                at = base + j * group + i
                scores = lax.dot_general(
                    q,
                    kv_ref[list_ref[at], :, :HD],
                    (((1,), (1,)), ((), ())),
                    preferred_element_type=jnp.float32,
                )
                s_ref[at] = scores
                top = jnp.maximum(top, fold(scores, jnp.maximum))
            m_ref[...] = top
            return 0

        return step

    def weigh(base, group):
        def step(j, _):
            top = m_ref[...]
            top = jnp.concatenate([top, top, top], axis=1)
            total = l_ref[...]
            acc = acc_ref[...]
            for i in range(group):
                at = base + j * group + i
                raised = jnp.exp(s_ref[at] - top)
                total = total + fold(raised, jnp.add)
                acc = acc + jnp.dot(
                    raised.astype(jnp.bfloat16),
                    kv_ref[list_ref[at], :, HD:],
                    preferred_element_type=jnp.float32,
                )
            l_ref[...] = total
            acc_ref[...] = acc
            return 0

        return step

    def each(make):
        lax.fori_loop(0, n >> 2, make(0, 4), 0)
        lax.fori_loop(0, (n >> 1) & 1, make((n >> 2) << 2, 2), 0)
        lax.fori_loop(0, n & 1, make((n >> 1) << 1, 1), 0)

    each(score)
    rescale(spread_max(m_ref[...]))
    each(weigh)


def own_kernel(live_ref, q_ref, kv_ref, m_ref, l_ref, acc_ref, s_ref, list_ref):
    u = pl.program_id(0)
    m, l, acc = m_ref.at[0], l_ref.at[0], acc_ref.at[0]
    m[...] = jnp.full_like(m[...], NEG)

    def rescale(top):
        m[...] = top
        l[...] = jnp.zeros_like(l[...])
        acc[...] = jnp.zeros_like(acc[...])

    attend(u, 0, 8, live_ref, q_ref[0], kv_ref, s_ref, list_ref, m, l, acc, rescale)


def attend_own(live, q, kv):
    per_u = pl.BlockSpec((1, TILE, HD), lambda u, *_: (u, 0, 0))
    state = jax.ShapeDtypeStruct((8, TILE, HD), jnp.float32)
    return pl.pallas_call(
        own_kernel,
        out_shape=[state, state, state],
        grid_spec=pltpu.PrefetchScalarGridSpec(
            num_scalar_prefetch=1,
            grid=(8,),
            in_specs=[per_u, whole((8, TILE, 2 * HD))],
            out_specs=[per_u] * 3,
            scratch_shapes=[pltpu.VMEM((8, TILE, TILE), jnp.float32), pltpu.SMEM((9,), jnp.int32)],
        ),
        compiler_params=pltpu.CompilerParams(vmem_limit_bytes=14 << 20),
        name="attend_own",
    )(live, q, kv)


def halo_kernel(s_ref, live_ref, q_ref, m_in, l_in, acc_in, *refs):
    pieces, (near_ref, far_ref, kv_ref, score_ref, m_ref, l_ref, acc_ref, list_ref, sems) = refs[:7], refs[7:]

    @pl.when(pl.program_id(0) == 0)
    def _():
        at = 0
        copies = []
        for i, piece in enumerate(pieces):
            to = kv_ref.at[pl.ds(at, piece.shape[0])]
            copies.append(pltpu.make_async_copy(piece, to, sems.at[i]))
            at += piece.shape[0]
        for copy in copies:
            copy.start()
        for copy in copies:
            copy.wait()

    u = pl.program_id(0) ^ u_base(s_ref[0])
    m_ref[...] = m_in[0]

    def rescale(top):
        m_ref[...] = top
        shrink = jnp.exp(m_in[0] - top)
        l_ref[...] = l_in[0] * shrink
        acc_ref[...] = acc_in[0] * shrink

    count = len(HALO_AT)
    attend(u, 8, count, live_ref, q_ref[0], kv_ref, score_ref, list_ref, m_ref, l_ref, acc_ref, rescale)
    total = jnp.sum(l_ref[...], axis=1, keepdims=True)
    mixed = (acc_ref[...] / total).astype(jnp.bfloat16)
    near_ref[0] = mixed[: TILE // 2]
    far_ref[0] = mixed[TILE // 2 :]


def attend_halo(slab_at, live, q, state, pieces):
    per_u = pl.BlockSpec((1, TILE, HD), lambda r, s_ref, *_: (r ^ u_base(s_ref[0]), 0, 0))
    count = len(HALO_AT)
    return pl.pallas_call(
        halo_kernel,
        out_shape=[jax.ShapeDtypeStruct((8, TILE // 2, HD), jnp.bfloat16)] * 2,
        grid_spec=pltpu.PrefetchScalarGridSpec(
            num_scalar_prefetch=2,
            grid=(8,),
            in_specs=[per_u] * 4 + [pl.BlockSpec(memory_space=pl.ANY)] * len(pieces),
            out_specs=[pl.BlockSpec((1, TILE // 2, HD), lambda r, *_: (r, 0, 0))] * 2,
            scratch_shapes=[
                pltpu.VMEM((count, TILE, 2 * HD), jnp.bfloat16),
                pltpu.VMEM((count, TILE, TILE), jnp.float32),
            ]
            + [pltpu.VMEM((TILE, HD), jnp.float32)] * 3
            + [pltpu.SMEM((count + 1,), jnp.int32), pltpu.SemaphoreType.DMA((len(pieces),))],
        ),
        compiler_params=pltpu.CompilerParams(vmem_limit_bytes=24 << 20),
        name="attend_halo",
    )(slab_at, live, q, *state, *pieces)


def output_kernel(s_ref, *refs):
    same, cross, (core_ref, w_ref, wc_ref, wd_ref, gate_ref, out_ref, x_ref, xc_ref, xd_ref) = (
        refs[:4],
        refs[4:8],
        refs[8:],
    )
    s = s_ref[0]
    mine = s & 1

    @pl.when(pl.program_id(0) == 0)
    def _():
        for p in range(4):
            for core, pieces in (
                (mine, (same[p].at[0], cross[p].at[0])),
                (1 - mine, (core_ref.at[p], core_ref.at[4 + p])),
            ):
                slot = slot_of(s, core, p)
                far_ref = xc_ref if core is mine else xd_ref

                @pl.when(slot < 3)
                def _(core=core, slot=slot, pieces=pieces, far_ref=far_ref):
                    x_ref[:, pl.ds(pl.multiple_of((core * 3 + slot) * HD, HD), HD)] = pieces[0][...]
                    far_ref[:, pl.ds(pl.multiple_of(slot * HD, HD), HD)] = pieces[1][...]

    def dot(x, w):
        return jnp.dot(x[...], w[...], preferred_element_type=jnp.float32)

    near = dot(x_ref, w_ref).astype(jnp.bfloat16).astype(jnp.float32)
    far = (dot(xc_ref, wc_ref) + dot(xd_ref, wd_ref)).astype(jnp.bfloat16).astype(jnp.float32)
    out_ref[...] = (gate_ref[...] * (near + far)).astype(jnp.bfloat16)


def output(slab_at, same, cross, core, weight, weight_c, weight_d, gate):
    inner, width = weight.shape
    half = TILE // 2
    cols = 1024
    by_col = lambda rows: pl.BlockSpec((rows, cols), lambda n, s_ref: (0, n))
    return pl.pallas_call(
        output_kernel,
        out_shape=jax.ShapeDtypeStruct((half, width), jnp.bfloat16),
        grid_spec=pltpu.PrefetchScalarGridSpec(
            num_scalar_prefetch=1,
            grid=(width // cols,),
            in_specs=[whole((1, half, HD))] * 8
            + [whole((8, half, HD)), by_col(inner), by_col(inner // 2), by_col(inner // 2), by_col(1)],
            out_specs=by_col(half),
            scratch_shapes=[
                pltpu.VMEM((half, inner), jnp.bfloat16),
                pltpu.VMEM((half, inner // 2), jnp.bfloat16),
                pltpu.VMEM((half, inner // 2), jnp.bfloat16),
            ],
        ),
        compiler_params=pltpu.CompilerParams(vmem_limit_bytes=14 << 20),
        name="output",
    )(slab_at, *same, *cross, core, weight, weight_c, weight_d, gate)


def on_device(
    tokens,
    qkv_weight,
    out_weight,
    query_gain,
    key_gain,
    mod_shift,
    mod_scale,
    branch_gate,
    block_mask,
):
    slab_at = lax.axis_index("slab").astype(jnp.int32).reshape(1)
    own = modulate(tokens[0], mod_shift, mod_scale)
    far = to_group(own)
    mask_rows = jnp.pad(
        jnp.broadcast_to(block_mask.astype(jnp.bfloat16), (MASK_ROWS, 27)), ((0, 0), (0, 3 * HD - 27))
    )
    gains = (query_gain.reshape(1, HD), key_gain.reshape(1, HD))
    part = weight_part(slab_at, out_weight)
    halves = []
    x = own
    for at in range(2):
        send = project(slab_at, x, qkv_weight, *gains, mask_rows, 1, at == 0)
        if at:
            send, part = lax.optimization_barrier((send, part))
        core = to_core(send)
        keep = project(slab_at, x, qkv_weight, *gains, mask_rows, 0, at == 0)
        near = []
        for p in (1, 2, 3):
            near.append(to_chip(jnp.stack([keep[p], core[p]]), p))
        x = far
        halves.append((keep, core, *near))
    weight_c = weight_across(part)
    q, kv, live, *sends = assemble(slab_at, halves)
    halo = [to_block(piece, moved) for piece, (moved, _) in zip(sends, HALO)] + [None] * 3
    state = attend_own(live, q, kv)
    *state, over, weight_c = lax.optimization_barrier((*state, halo[2], weight_c))
    halo[2] = over
    for at, moved, us in ((4, (0, 0, 1), (0, 2)), (5, (0, 1, 0), (0, 1)), (6, (0, 1, 1), (0,))):
        halo[at] = to_block(jnp.stack([over[u] for u in us]), moved)
    weight_d = to_core(weight_c)
    mixed, crossing = attend_halo(slab_at, live, q, state, halo)
    crossed = across(crossing)
    pieces = [(mixed, crossed)]
    for p in (1, 2, 3):
        r = slice(2 * p, 2 * p + 2)
        moved = from_chip(jnp.concatenate([mixed[r], crossed[r]]), p)
        pieces.append((moved[:2], moved[2:]))
    same, cross = zip(*pieces, strict=True)
    core = to_core(jnp.stack([piece[1] for piece in same + cross]))
    gate = branch_gate.reshape(1, -1)
    return output(slab_at, same, cross, core, out_weight, weight_c, weight_d, gate)[None]


def solution(mesh):
    in_specs = (
        P("slab", "heads", None),
        P(None, "heads"),
        P("heads", None),
        P(),
        P(),
        P(),
        P(),
        P(),
        P("slab", None),
    )
    out_specs = P("slab", "heads", None)
    return jax.shard_map(
        on_device,
        mesh=mesh,
        in_specs=in_specs,
        out_specs=out_specs,
        check_vma=False,
    )
```

profile of v0, /device:TPU:17, one launch (start us, length us, event | category | flops | bytes accessed | tf_op | source)
XLA Modules:
  0.0 178.6 jit_solution(11261333838860784236)
XLA Ops:
  1.7 1.7 fusion.3
  4.0 3.7 %collective-permute-start.4 = (bf16[192,3072]{1,0:T(8,128)(2,1)S(1)}, bf16[192,3072]{1,0:T(8,128)(2,1)S(1)}, u32[]{:S(2)}, u32[]{:S(2)}) collective-permute-start(bf16[192,3072]{1,0:T(8,128)(2,1)S(1)} %fusion.6.refs_1_), channel_id=1, source_target_pairs={{0,64},{64,0},{1,65},{65,1},{2,66},{66,2},{3,67},{67,3},{4,68},{68... | collective-permute-start | bytes 3538952 | tf_op jit(solution)/shard_map/ppermute | solution.py:94
  7.7 5.0 %copy-done = bf16[3072,2304]{1,0:T(8,128)(2,1)S(1)} copy-done((bf16[3072,2304]{1,0:T(8,128)(2,1)S(1)}, bf16[3072,2304]{1,0:T(8,128)(2,1)}, u32[]{:S(2)}) %copy-start) | copy-done | bytes 14155800
  12.7 3.6 %shard_map.101 = bf16[4,208,384]{2,1,0:T(8,128)(2,1)S(1)} custom-call(s32[1]{0:T(128)} %bitcast.refs_0_.s_ref, bf16[192,3072]{1,0:T(8,128)(2,1)S(1)} %fusion.6.refs_1_, bf16[3072,2304]{1,0:T(8,128)(2,1)S(1)} %copy-done, f32[1,128]{1,0:T(1,128)S(1)} %bitcast.28, f32[1,128]{1,0:T(1,128)S(1)} %bitcast.32, bf16[16,384]{1,0:T(8,128)(2,1)S(1)} %pad.7.refs_5_), custom_call_target="tpu_custom_call" | custom-call | tf_op jit(solution)/shard_map/pallas_call | solution.py:145
  17.4 3.5 %shard_map.100.refs_0_ = bf16[4,208,384]{2,1,0:T(8,128)(2,1)S(1)} custom-call(s32[1]{0:T(128)} %bitcast.refs_0_.s_ref, bf16[192,3072]{1,0:T(8,128)(2,1)S(1)} %fusion.6.refs_1_, bf16[3072,2304]{1,0:T(8,128)(2,1)S(1)} %copy-done, f32[1,128]{1,0:T(1,128)S(1)} %bitcast.29, f32[1,128]{1,0:T(1,128)S(1)} %bitcast.33, bf16[16,384]{1,0:T(8,128)(2,1)S(1)} %pad.7.refs_5_), custom_call_target="tpu_custom_call" | custom-call | tf_op jit(solution)/shard_map/pallas_call | solution.py:145
  21.2 12.1 %collective-permute-done.4.refs_1_ = bf16[192,3072]{1,0:T(8,128)(2,1)S(1)} collective-permute-done((bf16[192,3072]{1,0:T(8,128)(2,1)S(1)}, bf16[192,3072]{1,0:T(8,128)(2,1)S(1)}, u32[]{:S(2)}, u32[]{:S(2)}) %collective-permute-start.4) | collective-permute-done | bytes 1179680 | tf_op jit(solution)/shard_map/ppermute | solution.py:94
  33.4 3.6 %shard_map.103 = bf16[4,192,384]{2,1,0:T(8,128)(2,1)S(1)} custom-call(s32[1]{0:T(128)} %bitcast.refs_0_.s_ref, bf16[192,3072]{1,0:T(8,128)(2,1)S(1)} %collective-permute-done.4.refs_1_, bf16[3072,2304]{1,0:T(8,128)(2,1)S(1)} %bitcast.24, f32[1,128]{1,0:T(1,128)S(1)} %bitcast.30, f32[1,128]{1,0:T(1,128)S(1)} %bitcast.34, bf16[16,384]{1,0:T(8,128)(2,1)S(1)} %pad.7.refs_5_), custom_call_target="tpu_custom_call" | custom-call | tf_op jit(solution)/shard_map/pallas_call | solution.py:145
  36.9 2.9 %collective-permute-start.10 = (bf16[384,3072]{1,0:T(8,128)(2,1)S(1)}, bf16[384,3072]{1,0:T(8,128)(2,1)S(1)}, u32[]{:S(2)}, u32[]{:S(2)}) collective-permute-start(bf16[384,3072]{1,0:T(8,128)(2,1)S(1)} %weight_part.1), channel_id=1, source_target_pairs={{0,96},{1,97},{2,98},{3,99},{4,100},{5,101},{6,102},{7,103},{8,104... | collective-permute-start | bytes 7077896 | tf_op jit(solution)/shard_map/ppermute | solution.py:81
  39.9 1.9 %collective-permute-start.5 = (bf16[4,192,384]{2,1,0:T(8,128)(2,1)S(1)}, bf16[4,192,384]{2,1,0:T(8,128)(2,1)S(1)}, u32[]{:S(2)}, u32[]{:S(2)}) collective-permute-start(bf16[4,192,384]{2,1,0:T(8,128)(2,1)S(1)} %shard_map.103), channel_id=1, source_target_pairs={{0,1},{1,0},{2,3},{3,2},{4,5},{5,4},{6,7},{7,6},{8,9},{9,8},{10,11... | collective-permute-start | bytes 1769480 | tf_op jit(solution)/shard_map/ppermute | solution.py:85
  43.2 5.3 %collective-permute-start.2 = (bf16[2,208,384]{2,1,0:T(8,128)(2,1)S(1)}, bf16[2,208,384]{2,1,0:T(8,128)(2,1)S(1)}, u32[]{:S(2)}, u32[]{:S(2)}) collective-permute-start(bf16[2,208,384]{2,1,0:T(8,128)(2,1)S(1)} %pad_maximum_fusion.2), channel_id=1, source_target_pairs={{0,16},{1,17},{2,18},{7,23},{8,24},{9,25},{10,26},{11,27},{13,29},... | collective-permute-start | bytes 958472 | tf_op jit(solution)/shard_map/ppermute | solution.py:66
  48.6 1.9 %collective-permute-start.3 = (bf16[2,208,384]{2,1,0:T(8,128)(2,1)S(1)}, bf16[2,208,384]{2,1,0:T(8,128)(2,1)S(1)}, u32[]{:S(2)}, u32[]{:S(2)}) collective-permute-start(bf16[2,208,384]{2,1,0:T(8,128)(2,1)S(1)} %pad_maximum_fusion.3), channel_id=1, source_target_pairs={{3,23},{4,16},{5,17},{6,18},{9,29},{11,31},{12,24},{13,25},{14,26}... | collective-permute-start | bytes 958472 | tf_op jit(solution)/shard_map/ppermute | solution.py:66
  50.5 3.6 %shard_map.102.refs_5_ = bf16[4,192,384]{2,1,0:T(8,128)(2,1)S(1)} custom-call(s32[1]{0:T(128)} %bitcast.refs_0_.s_ref, bf16[192,3072]{1,0:T(8,128)(2,1)S(1)} %collective-permute-done.4.refs_1_, bf16[3072,2304]{1,0:T(8,128)(2,1)S(1)} %bitcast.24, f32[1,128]{1,0:T(1,128)S(1)} %bitcast.31, f32[1,128]{1,0:T(1,128)S(1)} %bitcast.35, bf16[16,384]{1,0:T(8,128)(2,1)S(1)} %pad.7.refs_5_), custom_call_target="tpu_custom_call" | custom-call | tf_op jit(solution)/shard_map/pallas_call | solution.py:145
  55.7 8.1 %collective-permute-start.7 = (bf16[2,192,384]{2,1,0:T(8,128)(2,1)S(1)}, bf16[2,192,384]{2,1,0:T(8,128)(2,1)S(1)}, u32[]{:S(2)}, u32[]{:S(2)}) collective-permute-start(bf16[2,192,384]{2,1,0:T(8,128)(2,1)S(1)} %pad_maximum_fusion.5), channel_id=1, source_target_pairs={{0,16},{1,17},{2,18},{7,23},{8,24},{9,25},{10,26},{11,27},{13,29},... | collective-permute-start | bytes 884744 | tf_op jit(solution)/shard_map/ppermute | solution.py:66
  63.9 3.6 %collective-permute-start.8 = (bf16[2,192,384]{2,1,0:T(8,128)(2,1)S(1)}, bf16[2,192,384]{2,1,0:T(8,128)(2,1)S(1)}, u32[]{:S(2)}, u32[]{:S(2)}) collective-permute-start(bf16[2,192,384]{2,1,0:T(8,128)(2,1)S(1)} %pad_maximum_fusion.6), channel_id=1, source_target_pairs={{3,23},{4,16},{5,17},{6,18},{9,29},{11,31},{12,24},{13,25},{14,26}... | collective-permute-start | bytes 884744 | tf_op jit(solution)/shard_map/ppermute | solution.py:66
  67.6 2.5 %collective-permute-done.7.refs_8_ = bf16[2,192,384]{2,1,0:T(8,128)(2,1)S(1)} collective-permute-done((bf16[2,192,384]{2,1,0:T(8,128)(2,1)S(1)}, bf16[2,192,384]{2,1,0:T(8,128)(2,1)S(1)}, u32[]{:S(2)}, u32[]{:S(2)}) %collective-permute-start.7) | collective-permute-done | bytes 294944 | tf_op jit(solution)/shard_map/ppermute | solution.py:66
  70.1 6.7 %collective-permute-done.8.refs_9_ = bf16[2,192,384]{2,1,0:T(8,128)(2,1)S(1)} collective-permute-done((bf16[2,192,384]{2,1,0:T(8,128)(2,1)S(1)}, bf16[2,192,384]{2,1,0:T(8,128)(2,1)S(1)}, u32[]{:S(2)}, u32[]{:S(2)}) %collective-permute-start.8) | collective-permute-done | bytes 294944 | tf_op jit(solution)/shard_map/ppermute | solution.py:66
  77.4 1.9 %collective-permute-start.9 = (bf16[4,384,256]{2,1,0:T(8,128)(2,1)S(1)}, bf16[4,384,256]{2,1,0:T(8,128)(2,1)S(1)}, u32[]{:S(2)}, u32[]{:S(2)}) collective-permute-start(bf16[4,384,256]{2,1,0:T(8,128)(2,1)S(1)} %get-tuple-element.31), channel_id=1, source_target_pairs={{0,32},{1,33},{2,34},{3,35},{4,36},{5,37},{6,38},{7,39},{8,40},{9,... | collective-permute-start | bytes 2359304 | tf_op jit(solution)/shard_map/ppermute | solution.py:90
  79.3 1.9 %collective-permute-start.11 = (bf16[4,384,256]{2,1,0:T(8,128)(2,1)S(1)}, bf16[4,384,256]{2,1,0:T(8,128)(2,1)S(1)}, u32[]{:S(2)}, u32[]{:S(2)}) collective-permute-start(bf16[4,384,256]{2,1,0:T(8,128)(2,1)S(1)} %get-tuple-element.36), channel_id=1, source_target_pairs={{0,2},{1,7},{2,0},{3,5},{4,6},{5,3},{6,4},{7,1},{8,10},{9,15},{10,... | collective-permute-start | bytes 2359304 | tf_op jit(solution)/shard_map/ppermute | solution.py:90
  81.2 6.3 %collective-permute-start.12 = (bf16[4,384,256]{2,1,0:T(8,128)(2,1)S(1)}, bf16[4,384,256]{2,1,0:T(8,128)(2,1)S(1)}, u32[]{:S(2)}, u32[]{:S(2)}) collective-permute-start(bf16[4,384,256]{2,1,0:T(8,128)(2,1)S(1)} %get-tuple-element.37), channel_id=1, source_target_pairs={{0,8},{1,25},{2,10},{3,27},{4,12},{5,29},{6,14},{7,31},{8,0},{9,17... | collective-permute-start | bytes 2359304 | tf_op jit(solution)/shard_map/ppermute | solution.py:90
  87.5 3.5 %collective-permute-start.13 = (bf16[2,384,256]{2,1,0:T(8,128)(2,1)S(1)}, bf16[2,384,256]{2,1,0:T(8,128)(2,1)S(1)}, u32[]{:S(2)}, u32[]{:S(2)}) collective-permute-start(bf16[2,384,256]{2,1,0:T(8,128)(2,1)S(1)} %get-tuple-element.39), channel_id=1, source_target_pairs={{0,10},{1,31},{2,8},{3,29},{4,14},{5,27},{6,12},{7,25},{8,2},{9,23... | collective-permute-start | bytes 1179656 | tf_op jit(solution)/shard_map/ppermute | solution.py:90
  91.0 16.0 %attend_own.1 = (f32[8,384,128]{2,1,0:T(8,128)S(1)}, f32[8,384,128]{2,1,0:T(8,128)S(1)}, f32[8,384,128]{2,1,0:T(8,128)S(1)}) custom-call(s32[8,128]{1,0:T(8,128)S(1)} %get-tuple-element.25.live_ref, bf16[8,384,128]{2,1,0:T(8,128)(2,1)S(1)} %get-tuple-element.26.q_ref, bf16[8,384,256]{2,1,0:T(8,128)(2,1)S(1)} %get-tuple-element.27.kv_ref), custom_call_target="tpu_custom_call" | custom-call | tf_op jit(solution)/shard_map/attend_own/pallas_call | solution.py:339
  107.1 1.9 %collective-permute-start.14 = (bf16[2,384,256]{2,1,0:T(8,128)(2,1)S(1)}, bf16[2,384,256]{2,1,0:T(8,128)(2,1)S(1)}, u32[]{:S(2)}, u32[]{:S(2)}) collective-permute-start(bf16[2,384,256]{2,1,0:T(8,128)(2,1)S(1)} %pad_maximum_fusion), channel_id=1, source_target_pairs={{0,2},{1,7},{2,0},{3,5},{4,6},{5,3},{6,4},{7,1},{8,10},{9,15},{10,... | collective-permute-start | bytes 1179656 | tf_op jit(solution)/shard_map/ppermute | solution.py:90
  109.1 4.6 %collective-permute-start.15 = (bf16[2,384,256]{2,1,0:T(8,128)(2,1)S(1)}, bf16[2,384,256]{2,1,0:T(8,128)(2,1)S(1)}, u32[]{:S(2)}, u32[]{:S(2)}) collective-permute-start(bf16[2,384,256]{2,1,0:T(8,128)(2,1)S(1)} %stack.34), channel_id=1, source_target_pairs={{0,8},{1,25},{2,10},{3,27},{4,12},{5,29},{6,14},{7,31},{8,0},{9,17... | collective-permute-start | bytes 1179656 | tf_op jit(solution)/shard_map/ppermute | solution.py:90
  113.7 4.3 %collective-permute-start.16 = (bf16[1,384,256]{2,1,0:T(8,128)(2,1)S(1)}, bf16[1,384,256]{2,1,0:T(8,128)(2,1)S(1)}, u32[]{:S(2)}, u32[]{:S(2)}) collective-permute-start(bf16[1,384,256]{2,1,0:T(8,128)(2,1)S(1)} %get-tuple-element.43), channel_id=1, source_target_pairs={{0,10},{1,31},{2,8},{3,29},{4,14},{5,27},{6,12},{7,25},{8,2},{9,23... | collective-permute-start | bytes 589832 | tf_op jit(solution)/shard_map/ppermute | solution.py:90
  118.3 3.9 %collective-permute-done.16.refs_6_ = bf16[1,384,256]{2,1,0:T(8,128)(2,1)S(1)} collective-permute-done((bf16[1,384,256]{2,1,0:T(8,128)(2,1)S(1)}, bf16[1,384,256]{2,1,0:T(8,128)(2,1)S(1)}, u32[]{:S(2)}, u32[]{:S(2)}) %collective-permute-start.16) | collective-permute-done | bytes 196640 | tf_op jit(solution)/shard_map/ppermute | solution.py:90
  122.2 16.8 %attend_halo.1 = (bf16[8,192,128]{2,1,0:T(8,128)(2,1)S(1)}, bf16[8,192,128]{2,1,0:T(8,128)(2,1)S(1)}) custom-call(s32[1]{0:T(128)} %bitcast.refs_0_.s_ref, s32[8,128]{1,0:T(8,128)S(1)} %get-tuple-element.25.live_ref, bf16[8,384,128]{2,1,0:T(8,128)(2,1)S(1)} %get-tuple-element.26.q_ref, f32[8,384,128]{2,1,0:T(8,128)S(1)} %get-tuple-element.33.m_in, ...), custom_call_target="tpu_custom_call" | custom-call | tf_op jit(solution)/shard_map/attend_halo/pallas_call | solution.py:390
  139.1 2.8 %collective-permute-start.17 = (bf16[8,192,128]{2,1,0:T(8,128)(2,1)S(1)}, bf16[8,192,128]{2,1,0:T(8,128)(2,1)S(1)}, u32[]{:S(2)}, u32[]{:S(2)}) collective-permute-start(bf16[8,192,128]{2,1,0:T(8,128)(2,1)S(1)} %get-tuple-element.41), channel_id=1, source_target_pairs={{0,64},{1,65},{2,66},{3,67},{4,68},{5,69},{6,70},{7,71},{8,72},{9,... | collective-permute-start | bytes 1179656 | tf_op jit(solution)/shard_map/ppermute | solution.py:76
  142.0 10.6 %collective-permute-done.17.refs_4_ = bf16[8,192,128]{2,1,0:T(8,128)(2,1)S(1)} collective-permute-done((bf16[8,192,128]{2,1,0:T(8,128)(2,1)S(1)}, bf16[8,192,128]{2,1,0:T(8,128)(2,1)S(1)}, u32[]{:S(2)}, u32[]{:S(2)}) %collective-permute-start.17) | collective-permute-done | bytes 393248 | tf_op jit(solution)/shard_map/ppermute | solution.py:76
  154.0 5.5 %collective-permute-start.19 = (bf16[4,192,128]{2,1,0:T(8,128)(2,1)S(1)}, bf16[4,192,128]{2,1,0:T(8,128)(2,1)S(1)}, u32[]{:S(2)}, u32[]{:S(2)}) collective-permute-start(bf16[4,192,128]{2,1,0:T(8,128)(2,1)S(1)} %pad_maximum_fusion.8), channel_id=1, source_target_pairs={{0,16},{1,17},{2,18},{3,19},{4,20},{5,21},{6,22},{7,23},{8,24},{9,... | collective-permute-start | bytes 589832 | tf_op jit(solution)/shard_map/ppermute | solution.py:71
  159.6 4.0 %collective-permute-start.20 = (bf16[4,192,128]{2,1,0:T(8,128)(2,1)S(1)}, bf16[4,192,128]{2,1,0:T(8,128)(2,1)S(1)}, u32[]{:S(2)}, u32[]{:S(2)}) collective-permute-start(bf16[4,192,128]{2,1,0:T(8,128)(2,1)S(1)} %pad_maximum_fusion.9), channel_id=1, source_target_pairs={{0,20},{1,21},{2,22},{3,23},{4,16},{5,17},{6,18},{7,19},{8,28},{9,... | collective-permute-start | bytes 589832 | tf_op jit(solution)/shard_map/ppermute | solution.py:71
  164.2 7.8 %collective-permute-done.20 = bf16[4,192,128]{2,1,0:T(8,128)(2,1)S(1)} collective-permute-done((bf16[4,192,128]{2,1,0:T(8,128)(2,1)S(1)}, bf16[4,192,128]{2,1,0:T(8,128)(2,1)S(1)}, u32[]{:S(2)}, u32[]{:S(2)}) %collective-permute-start.20) | collective-permute-done | bytes 196640 | tf_op jit(solution)/shard_map/ppermute | solution.py:71
  174.2 4.4 %output.1 = bf16[192,3072]{1,0:T(8,128)(2,1)} custom-call(s32[1]{0:T(128)} %bitcast.refs_0_.s_ref, bf16[8,192,128]{2,1,0:T(8,128)(2,1)S(1)} %get-tuple-element.40.refs_0_, bf16[2,192,128]{2,1,0:T(8,128)(2,1)S(1)} %get-tuple-element.68.refs_1_, bf16[2,192,128]{2,1,0:T(8,128)(2,1)S(1)} %get-tuple-element.66.refs_2_, ...), custom_call_target="tpu_custom_call" | custom-call | tf_op jit(solution)/shard_map/output/pallas_call | solution.py:447
  (93 shorter events, 11.7 us)
Async XLA Ops:
  0.0 7.7 %copy-start.4 = (f32[128]{0:T(128)S(1)}, f32[128]{0:T(128)}, u32[]{:S(2)}) copy-start(f32[128]{0:T(128)} %param.14) | copy-start | bytes 1540
  0.0 7.7 %copy-start.3 = (f32[128]{0:T(128)S(1)}, f32[128]{0:T(128)}, u32[]{:S(2)}) copy-start(f32[128]{0:T(128)} %param.13) | copy-start | bytes 1540
  4.0 29.3 %collective-permute-start.4 = (bf16[192,3072]{1,0:T(8,128)(2,1)S(1)}, bf16[192,3072]{1,0:T(8,128)(2,1)S(1)}, u32[]{:S(2)}, u32[]{:S(2)}) collective-permute-start(bf16[192,3072]{1,0:T(8,128)(2,1)S(1)} %fusion.6.refs_1_), channel_id=1, source_target_pairs={{0,64},{64,0},{1,65},{65,1},{2,66},{66,2},{3,67},{67,3},{4,68},{68... | collective-permute-start | bytes 3538952 | tf_op jit(solution)/shard_map/ppermute | solution.py:94
  12.7 8.2 %slice-start.4 = ((s8[4718592]{0:T(1024)(128)(4,1)}), s8[4194304]{0:T(1024)(128)(4,1)S(1)}, s32[]{:S(2)}) async-start(s8[4718592]{0:T(1024)(128)(4,1)} %bitcast.25), calls=%async_computation.4 | async-start | bytes 8388608
  12.7 20.6 %slice-start = ((s8[14155776]{0:T(1024)(128)(4,1)}), s8[4194304]{0:T(1024)(128)(4,1)S(1)}, s32[]{:S(2)}) async-start(s8[14155776]{0:T(1024)(128)(4,1)} %bitcast.23), calls=%async_computation | async-start | bytes 8388608
  12.7 20.6 %slice-start.1 = ((s8[14155776]{0:T(1024)(128)(4,1)}), s8[4194304]{0:T(1024)(128)(4,1)S(1)}, s32[]{:S(2)}) async-start(s8[14155776]{0:T(1024)(128)(4,1)} %bitcast.23), calls=%async_computation.1 | async-start | bytes 8388608
  16.3 17.0 %slice-start.2 = ((s8[14155776]{0:T(1024)(128)(4,1)}), s8[4194304]{0:T(1024)(128)(4,1)S(1)}, s32[]{:S(2)}) async-start(s8[14155776]{0:T(1024)(128)(4,1)} %bitcast.23), calls=%async_computation.2 | async-start | bytes 8388608
  16.3 17.0 %slice-start.3 = ((s8[14155776]{0:T(1024)(128)(4,1)}), s8[1572864]{0:T(1024)(128)(4,1)S(1)}, s32[]{:S(2)}) async-start(s8[14155776]{0:T(1024)(128)(4,1)} %bitcast.23), calls=%async_computation.3 | async-start | bytes 3145728
  16.3 23.5 %collective-permute-start = (bf16[4,208,384]{2,1,0:T(8,128)(2,1)S(1)}, bf16[4,208,384]{2,1,0:T(8,128)(2,1)S(1)}, u32[]{:S(2)}, u32[]{:S(2)}) collective-permute-start(bf16[4,208,384]{2,1,0:T(8,128)(2,1)S(1)} %shard_map.101), channel_id=1, source_target_pairs={{0,1},{1,0},{2,3},{3,2},{4,5},{5,4},{6,7},{7,6},{8,9},{9,8},{10,11... | collective-permute-start | bytes 1916936 | tf_op jit(solution)/shard_map/ppermute | solution.py:85
  36.9 70.1 %collective-permute-start.10 = (bf16[384,3072]{1,0:T(8,128)(2,1)S(1)}, bf16[384,3072]{1,0:T(8,128)(2,1)S(1)}, u32[]{:S(2)}, u32[]{:S(2)}) collective-permute-start(bf16[384,3072]{1,0:T(8,128)(2,1)S(1)} %weight_part.1), channel_id=1, source_target_pairs={{0,96},{1,97},{2,98},{3,99},{4,100},{5,101},{6,102},{7,103},{8,104... | collective-permute-start | bytes 7077896 | tf_op jit(solution)/shard_map/ppermute | solution.py:81
  39.9 14.3 %collective-permute-start.5 = (bf16[4,192,384]{2,1,0:T(8,128)(2,1)S(1)}, bf16[4,192,384]{2,1,0:T(8,128)(2,1)S(1)}, u32[]{:S(2)}, u32[]{:S(2)}) collective-permute-start(bf16[4,192,384]{2,1,0:T(8,128)(2,1)S(1)} %shard_map.103), channel_id=1, source_target_pairs={{0,1},{1,0},{2,3},{3,2},{4,5},{5,4},{6,7},{7,6},{8,9},{9,8},{10,11... | collective-permute-start | bytes 1769480 | tf_op jit(solution)/shard_map/ppermute | solution.py:85
  41.9 13.8 %collective-permute-start.1 = (bf16[2,208,384]{2,1,0:T(8,128)(2,1)S(1)}, bf16[2,208,384]{2,1,0:T(8,128)(2,1)S(1)}, u32[]{:S(2)}, u32[]{:S(2)}) collective-permute-start(bf16[2,208,384]{2,1,0:T(8,128)(2,1)S(1)} %pad_maximum_fusion.1), channel_id=1, source_target_pairs={{0,4},{1,5},{2,6},{3,7},{4,0},{5,1},{6,2},{7,3},{8,12},{10,14},{11... | collective-permute-start | bytes 958472 | tf_op jit(solution)/shard_map/ppermute | solution.py:66
  43.2 20.6 %collective-permute-start.2 = (bf16[2,208,384]{2,1,0:T(8,128)(2,1)S(1)}, bf16[2,208,384]{2,1,0:T(8,128)(2,1)S(1)}, u32[]{:S(2)}, u32[]{:S(2)}) collective-permute-start(bf16[2,208,384]{2,1,0:T(8,128)(2,1)S(1)} %pad_maximum_fusion.2), channel_id=1, source_target_pairs={{0,16},{1,17},{2,18},{7,23},{8,24},{9,25},{10,26},{11,27},{13,29},... | collective-permute-start | bytes 958472 | tf_op jit(solution)/shard_map/ppermute | solution.py:66
  48.6 18.9 %collective-permute-start.3 = (bf16[2,208,384]{2,1,0:T(8,128)(2,1)S(1)}, bf16[2,208,384]{2,1,0:T(8,128)(2,1)S(1)}, u32[]{:S(2)}, u32[]{:S(2)}) collective-permute-start(bf16[2,208,384]{2,1,0:T(8,128)(2,1)S(1)} %pad_maximum_fusion.3), channel_id=1, source_target_pairs={{3,23},{4,16},{5,17},{6,18},{9,29},{11,31},{12,24},{13,25},{14,26}... | collective-permute-start | bytes 958472 | tf_op jit(solution)/shard_map/ppermute | solution.py:66
  54.1 22.7 %copy-start.1 = (s32[8,8,128]{2,1,0:T(8,128)S(1)}, s32[8,8,128]{2,1,0:T(8,128)}, u32[]{:S(2)}) copy-start(s32[8,8,128]{2,1,0:T(8,128)} %constant.19.clone.refs_10_) | copy-start | bytes 98308
  54.3 13.3 %collective-permute-start.6 = (bf16[2,192,384]{2,1,0:T(8,128)(2,1)S(1)}, bf16[2,192,384]{2,1,0:T(8,128)(2,1)S(1)}, u32[]{:S(2)}, u32[]{:S(2)}) collective-permute-start(bf16[2,192,384]{2,1,0:T(8,128)(2,1)S(1)} %pad_maximum_fusion.4), channel_id=1, source_target_pairs={{0,4},{1,5},{2,6},{3,7},{4,0},{5,1},{6,2},{7,3},{8,12},{10,14},{11... | collective-permute-start | bytes 884744 | tf_op jit(solution)/shard_map/ppermute | solution.py:66
  55.7 14.4 %collective-permute-start.7 = (bf16[2,192,384]{2,1,0:T(8,128)(2,1)S(1)}, bf16[2,192,384]{2,1,0:T(8,128)(2,1)S(1)}, u32[]{:S(2)}, u32[]{:S(2)}) collective-permute-start(bf16[2,192,384]{2,1,0:T(8,128)(2,1)S(1)} %pad_maximum_fusion.5), channel_id=1, source_target_pairs={{0,16},{1,17},{2,18},{7,23},{8,24},{9,25},{10,26},{11,27},{13,29},... | collective-permute-start | bytes 884744 | tf_op jit(solution)/shard_map/ppermute | solution.py:66
  63.9 12.9 %collective-permute-start.8 = (bf16[2,192,384]{2,1,0:T(8,128)(2,1)S(1)}, bf16[2,192,384]{2,1,0:T(8,128)(2,1)S(1)}, u32[]{:S(2)}, u32[]{:S(2)}) collective-permute-start(bf16[2,192,384]{2,1,0:T(8,128)(2,1)S(1)} %pad_maximum_fusion.6), channel_id=1, source_target_pairs={{3,23},{4,16},{5,17},{6,18},{9,29},{11,31},{12,24},{13,25},{14,26}... | collective-permute-start | bytes 884744 | tf_op jit(solution)/shard_map/ppermute | solution.py:66
  77.4 29.6 %collective-permute-start.9 = (bf16[4,384,256]{2,1,0:T(8,128)(2,1)S(1)}, bf16[4,384,256]{2,1,0:T(8,128)(2,1)S(1)}, u32[]{:S(2)}, u32[]{:S(2)}) collective-permute-start(bf16[4,384,256]{2,1,0:T(8,128)(2,1)S(1)} %get-tuple-element.31), channel_id=1, source_target_pairs={{0,32},{1,33},{2,34},{3,35},{4,36},{5,37},{6,38},{7,39},{8,40},{9,... | collective-permute-start | bytes 2359304 | tf_op jit(solution)/shard_map/ppermute | solution.py:90
  79.3 38.7 %collective-permute-start.11 = (bf16[4,384,256]{2,1,0:T(8,128)(2,1)S(1)}, bf16[4,384,256]{2,1,0:T(8,128)(2,1)S(1)}, u32[]{:S(2)}, u32[]{:S(2)}) collective-permute-start(bf16[4,384,256]{2,1,0:T(8,128)(2,1)S(1)} %get-tuple-element.36), channel_id=1, source_target_pairs={{0,2},{1,7},{2,0},{3,5},{4,6},{5,3},{6,4},{7,1},{8,10},{9,15},{10,... | collective-permute-start | bytes 2359304 | tf_op jit(solution)/shard_map/ppermute | solution.py:90
  81.2 37.1 %collective-permute-start.12 = (bf16[4,384,256]{2,1,0:T(8,128)(2,1)S(1)}, bf16[4,384,256]{2,1,0:T(8,128)(2,1)S(1)}, u32[]{:S(2)}, u32[]{:S(2)}) collective-permute-start(bf16[4,384,256]{2,1,0:T(8,128)(2,1)S(1)} %get-tuple-element.37), channel_id=1, source_target_pairs={{0,8},{1,25},{2,10},{3,27},{4,12},{5,29},{6,14},{7,31},{8,0},{9,17... | collective-permute-start | bytes 2359304 | tf_op jit(solution)/shard_map/ppermute | solution.py:90
  87.5 26.2 %collective-permute-start.13 = (bf16[2,384,256]{2,1,0:T(8,128)(2,1)S(1)}, bf16[2,384,256]{2,1,0:T(8,128)(2,1)S(1)}, u32[]{:S(2)}, u32[]{:S(2)}) collective-permute-start(bf16[2,384,256]{2,1,0:T(8,128)(2,1)S(1)} %get-tuple-element.39), channel_id=1, source_target_pairs={{0,10},{1,31},{2,8},{3,29},{4,14},{5,27},{6,12},{7,25},{8,2},{9,23... | collective-permute-start | bytes 1179656 | tf_op jit(solution)/shard_map/ppermute | solution.py:90
  107.1 15.1 %collective-permute-start.14 = (bf16[2,384,256]{2,1,0:T(8,128)(2,1)S(1)}, bf16[2,384,256]{2,1,0:T(8,128)(2,1)S(1)}, u32[]{:S(2)}, u32[]{:S(2)}) collective-permute-start(bf16[2,384,256]{2,1,0:T(8,128)(2,1)S(1)} %pad_maximum_fusion), channel_id=1, source_target_pairs={{0,2},{1,7},{2,0},{3,5},{4,6},{5,3},{6,4},{7,1},{8,10},{9,15},{10,... | collective-permute-start | bytes 1179656 | tf_op jit(solution)/shard_map/ppermute | solution.py:90
  109.1 13.2 %collective-permute-start.15 = (bf16[2,384,256]{2,1,0:T(8,128)(2,1)S(1)}, bf16[2,384,256]{2,1,0:T(8,128)(2,1)S(1)}, u32[]{:S(2)}, u32[]{:S(2)}) collective-permute-start(bf16[2,384,256]{2,1,0:T(8,128)(2,1)S(1)} %stack.34), channel_id=1, source_target_pairs={{0,8},{1,25},{2,10},{3,27},{4,12},{5,29},{6,14},{7,31},{8,0},{9,17... | collective-permute-start | bytes 1179656 | tf_op jit(solution)/shard_map/ppermute | solution.py:90
  113.7 8.5 %collective-permute-start.16 = (bf16[1,384,256]{2,1,0:T(8,128)(2,1)S(1)}, bf16[1,384,256]{2,1,0:T(8,128)(2,1)S(1)}, u32[]{:S(2)}, u32[]{:S(2)}) collective-permute-start(bf16[1,384,256]{2,1,0:T(8,128)(2,1)S(1)} %get-tuple-element.43), channel_id=1, source_target_pairs={{0,10},{1,31},{2,8},{3,29},{4,14},{5,27},{6,12},{7,25},{8,2},{9,23... | collective-permute-start | bytes 589832 | tf_op jit(solution)/shard_map/ppermute | solution.py:90
  118.0 56.2 %collective-permute-start.22 = (bf16[384,3072]{1,0:T(8,128)(2,1)S(1)}, bf16[384,3072]{1,0:T(8,128)(2,1)S(1)}, u32[]{:S(2)}, u32[]{:S(2)}) collective-permute-start(bf16[384,3072]{1,0:T(8,128)(2,1)S(1)} %collective-permute-done.10.refs_10_), channel_id=1, source_target_pairs={{0,1},{1,0},{2,3},{3,2},{4,5},{5,4},{6,7},{7,6},{8,9},{9,8},{10,11... | collective-permute-start | bytes 7077896 | tf_op jit(solution)/shard_map/ppermute | solution.py:85
  139.1 35.1 %copy-start.2 = (f32[3072]{0:T(1024)S(1)}, f32[3072]{0:T(1024)}, u32[]{:S(2)}) copy-start(f32[3072]{0:T(1024)} %param.17) | copy-start | bytes 36868
  139.1 13.5 %collective-permute-start.17 = (bf16[8,192,128]{2,1,0:T(8,128)(2,1)S(1)}, bf16[8,192,128]{2,1,0:T(8,128)(2,1)S(1)}, u32[]{:S(2)}, u32[]{:S(2)}) collective-permute-start(bf16[8,192,128]{2,1,0:T(8,128)(2,1)S(1)} %get-tuple-element.41), channel_id=1, source_target_pairs={{0,64},{1,65},{2,66},{3,67},{4,68},{5,69},{6,70},{7,71},{8,72},{9,... | collective-permute-start | bytes 1179656 | tf_op jit(solution)/shard_map/ppermute | solution.py:76
  152.6 10.9 %collective-permute-start.18 = (bf16[4,192,128]{2,1,0:T(8,128)(2,1)S(1)}, bf16[4,192,128]{2,1,0:T(8,128)(2,1)S(1)}, u32[]{:S(2)}, u32[]{:S(2)}) collective-permute-start(bf16[4,192,128]{2,1,0:T(8,128)(2,1)S(1)} %pad_maximum_fusion.7), channel_id=1, source_target_pairs={{0,4},{1,5},{2,6},{3,7},{4,0},{5,1},{6,2},{7,3},{8,12},{9,13},{10,... | collective-permute-start | bytes 589832 | tf_op jit(solution)/shard_map/ppermute | solution.py:71
  154.0 10.2 %collective-permute-start.19 = (bf16[4,192,128]{2,1,0:T(8,128)(2,1)S(1)}, bf16[4,192,128]{2,1,0:T(8,128)(2,1)S(1)}, u32[]{:S(2)}, u32[]{:S(2)}) collective-permute-start(bf16[4,192,128]{2,1,0:T(8,128)(2,1)S(1)} %pad_maximum_fusion.8), channel_id=1, source_target_pairs={{0,16},{1,17},{2,18},{3,19},{4,20},{5,21},{6,22},{7,23},{8,24},{9,... | collective-permute-start | bytes 589832 | tf_op jit(solution)/shard_map/ppermute | solution.py:71
  159.6 12.4 %collective-permute-start.20 = (bf16[4,192,128]{2,1,0:T(8,128)(2,1)S(1)}, bf16[4,192,128]{2,1,0:T(8,128)(2,1)S(1)}, u32[]{:S(2)}, u32[]{:S(2)}) collective-permute-start(bf16[4,192,128]{2,1,0:T(8,128)(2,1)S(1)} %pad_maximum_fusion.9), channel_id=1, source_target_pairs={{0,20},{1,21},{2,22},{3,23},{4,16},{5,17},{6,18},{7,19},{8,28},{9,... | collective-permute-start | bytes 589832 | tf_op jit(solution)/shard_map/ppermute | solution.py:71
  172.1 2.1 %collective-permute-start.21 = (bf16[8,192,128]{2,1,0:T(8,128)(2,1)S(1)}, bf16[8,192,128]{2,1,0:T(8,128)(2,1)S(1)}, u32[]{:S(2)}, u32[]{:S(2)}) collective-permute-start(bf16[8,192,128]{2,1,0:T(8,128)(2,1)S(1)} %slice_dynamic-update-slice_fusion), channel_id=1, source_target_pairs={{0,1},{1,0},{2,3},{3,2},{4,5},{5,4},{6,7},{7,6},{8,9},{9,8},{10,11... | collective-permute-start | bytes 1179656 | tf_op jit(solution)/shard_map/ppermute | solution.py:85
  (6 other events, 27.5 us)
where the time goes:
time: 179 us
  starting transfers between devices  70.2 us (39%)
  Pallas kernels  52.2 us (29%)
  waiting for transfers between devices  45.7 us (26%)
  local copies, waits for them, and re-layouts  5.52 us (3%)
  other arithmetic  4.23 us (2%)
    ppermute x7, starting transfers between devices, to_block(): return lax.ppermute(value, 'slab', pairs)  24.4 us
    ppermute x6, starting transfers between devices, to_chip(): return lax.ppermute(value, 'slab', pairs)  21.6 us
    pallas_call x1, Pallas kernels, attend_halo(): pl.pallas_call(halo_kernel, out_shape=[jax.ShapeDtypeStruct((8, TILE // 2...  16.8 us
    pallas_call x1, Pallas kernels, attend_own(): pl.pallas_call(own_kernel, out_shape=[state, state, state], grid_spec=plt...  16 us
    pallas_call x4, Pallas kernels, project(): pl.pallas_call(lambda *refs: project_kernel(other, *refs), out_shape=jax....  14.3 us
    ppermute x1, waiting for transfers between devices, to_group(): return lax.ppermute(value, 'heads', [(0, 1), (1, 0)])  12.1 us
    ppermute x3, starting transfers between devices, from_chip(): return lax.ppermute(value, 'slab', pairs)  10.8 us
    ppermute x1, waiting for transfers between devices, across(): return lax.ppermute(value, ('heads', 'slab'), pairs)  10.6 us
  transfers between devices with their start and end apart: 23, of which 9 were waited for; matrix products, arithmetic and copies ran while one was open for 0% of the time, Pallas kernels for 27%

commit v1 on v0

--- a/solution.py
+++ b/solution.py
@@ -98,14 +98,30 @@
     return pl.BlockSpec(shape, lambda *_: (0,) * len(shape), pipeline_mode=pl.Buffered(1))
 
 
-def modulate(token_rows, mod_shift, mod_scale):
-    token_rows = token_rows.astype(jnp.float32)
-    row_mean = jnp.mean(token_rows, axis=-1, keepdims=True)
-    centered = token_rows - row_mean
+def modulate_kernel(x_ref, shift_ref, scale_ref, out_ref):
+    rows = x_ref[0].astype(jnp.float32)
+    centered = rows - jnp.mean(rows, axis=-1, keepdims=True)
     variance = jnp.mean(centered * centered, axis=-1, keepdims=True)
-    return (centered * lax.rsqrt(variance + 1e-06) * (1.0 + mod_scale) + mod_shift).astype(
-        jnp.bfloat16
-    )
+    out = centered * lax.rsqrt(variance + 1e-06) * (1.0 + scale_ref[...]) + shift_ref[...]
+    out_ref[...] = out.astype(jnp.bfloat16)
+
+
+def modulate(tokens, mod_shift, mod_scale):
+    _, rows, width = tokens.shape
+    step = 48
+    return pl.pallas_call(
+        modulate_kernel,
+        out_shape=jax.ShapeDtypeStruct((rows, width), jnp.bfloat16),
+        grid=(rows // step,),
+        in_specs=[
+            pl.BlockSpec((1, step, width), lambda i: (0, i, 0)),
+            whole((1, width)),
+            whole((1, width)),
+        ],
+        out_specs=pl.BlockSpec((step, width), lambda i: (i, 0)),
+        compiler_params=pltpu.CompilerParams(vmem_limit_bytes=8 << 20),
+        name="modulate",
+    )(tokens, mod_shift.reshape(1, width), mod_scale.reshape(1, width))
 
 
 def project_kernel(other, s_ref, x_ref, w_ref, qg_ref, kg_ref, mask_ref, out_ref):
@@ -351,7 +367,7 @@
     )(live, q, kv)
 
 
-def halo_kernel(s_ref, live_ref, q_ref, m_in, l_in, acc_in, *refs):
+def halo_kernel(first, s_ref, live_ref, q_ref, m_in, l_in, acc_in, *refs):
     pieces, (near_ref, far_ref, kv_ref, score_ref, m_ref, l_ref, acc_ref, list_ref, sems) = refs[:7], refs[7:]
 
     @pl.when(pl.program_id(0) == 0)
@@ -367,7 +383,7 @@
         for copy in copies:
             copy.wait()
 
-    u = pl.program_id(0) ^ u_base(s_ref[0])
+    u = (first + pl.program_id(0)) ^ u_base(s_ref[0])
     m_ref[...] = m_in[0]
 
     def rescale(top):
@@ -384,15 +400,15 @@
     far_ref[0] = mixed[TILE // 2 :]
 
 
-def attend_halo(slab_at, live, q, state, pieces):
-    per_u = pl.BlockSpec((1, TILE, HD), lambda r, s_ref, *_: (r ^ u_base(s_ref[0]), 0, 0))
+def attend_halo(slab_at, live, q, state, pieces, first):
+    per_u = pl.BlockSpec((1, TILE, HD), lambda r, s_ref, *_: ((first + r) ^ u_base(s_ref[0]), 0, 0))
     count = len(HALO_AT)
     return pl.pallas_call(
-        halo_kernel,
-        out_shape=[jax.ShapeDtypeStruct((8, TILE // 2, HD), jnp.bfloat16)] * 2,
+        lambda *refs: halo_kernel(first, *refs),
+        out_shape=[jax.ShapeDtypeStruct((4, TILE // 2, HD), jnp.bfloat16)] * 2,
         grid_spec=pltpu.PrefetchScalarGridSpec(
             num_scalar_prefetch=2,
-            grid=(8,),
+            grid=(4,),
             in_specs=[per_u] * 4 + [pl.BlockSpec(memory_space=pl.ANY)] * len(pieces),
             out_specs=[pl.BlockSpec((1, TILE // 2, HD), lambda r, *_: (r, 0, 0))] * 2,
             scratch_shapes=[
@@ -403,7 +419,6 @@
             + [pltpu.SMEM((count + 1,), jnp.int32), pltpu.SemaphoreType.DMA((len(pieces),))],
         ),
         compiler_params=pltpu.CompilerParams(vmem_limit_bytes=24 << 20),
-        name="attend_halo",
     )(slab_at, live, q, *state, *pieces)
 
 
@@ -476,7 +491,7 @@
     block_mask,
 ):
     slab_at = lax.axis_index("slab").astype(jnp.int32).reshape(1)
-    own = modulate(tokens[0], mod_shift, mod_scale)
+    own = modulate(tokens, mod_shift, mod_scale)
     far = to_group(own)
     mask_rows = jnp.pad(
         jnp.broadcast_to(block_mask.astype(jnp.bfloat16), (MASK_ROWS, 27)), ((0, 0), (0, 3 * HD - 27))
@@ -500,19 +515,24 @@
     q, kv, live, *sends = assemble(slab_at, halves)
     halo = [to_block(piece, moved) for piece, (moved, _) in zip(sends, HALO)] + [None] * 3
     state = attend_own(live, q, kv)
-    *state, over, weight_c = lax.optimization_barrier((*state, halo[2], weight_c))
+    *state, over = lax.optimization_barrier((*state, halo[2]))
     halo[2] = over
     for at, moved, us in ((4, (0, 0, 1), (0, 2)), (5, (0, 1, 0), (0, 1)), (6, (0, 1, 1), (0,))):
         halo[at] = to_block(jnp.stack([over[u] for u in us]), moved)
+    done = {}
+    for first in (4, 0):
+        mixed, crossing = attend_halo(slab_at, live, q, state, halo, first)
+        if not first:
+            mixed, weight_c = lax.optimization_barrier((mixed, weight_c))
+        crossed = across(crossing)
+        for p in (first // 2, first // 2 + 1):
+            r = slice(2 * p - first, 2 * p - first + 2)
+            done[p] = (mixed[r], crossed[r])
     weight_d = to_core(weight_c)
-    mixed, crossing = attend_halo(slab_at, live, q, state, halo)
-    crossed = across(crossing)
-    pieces = [(mixed, crossed)]
-    for p in (1, 2, 3):
-        r = slice(2 * p, 2 * p + 2)
-        moved = from_chip(jnp.concatenate([mixed[r], crossed[r]]), p)
-        pieces.append((moved[:2], moved[2:]))
-    same, cross = zip(*pieces, strict=True)
+    for p in (2, 3, 1):
+        moved = from_chip(jnp.concatenate(done[p]), p)
+        done[p] = (moved[:2], moved[2:])
+    same, cross = zip(*(done[p] for p in range(4)), strict=True)
     core = to_core(jnp.stack([piece[1] for piece in same + cross]))
     gate = branch_gate.reshape(1, -1)
     return output(slab_at, same, cross, core, out_weight, weight_c, weight_d, gate)[None]

time: 179 us -> 178 us (level)
  the two profiles are of different devices: /device:TPU:17 before, /device:TPU:1 now
where the time goes in v1:
time: 178 us; the launch traced here: 177 us
  starting transfers between devices  72.8 us (41%)
  Pallas kernels  55.3 us (31%)
  waiting for transfers between devices  39.4 us (22%)
  local copies, waits for them, and re-layouts  8.24 us (5%)
    ppermute x7, starting transfers between devices, to_block(): return lax.ppermute(value, 'slab', pairs)  26.6 us
    ppermute x6, starting transfers between devices, to_chip(): return lax.ppermute(value, 'slab', pairs)  19.2 us
    pallas_call x2, Pallas kernels, attend_halo(): pl.pallas_call(lambda *refs: halo_kernel(first, *refs), out_shape=[jax.Sh...  18.6 us
    pallas_call x1, Pallas kernels, attend_own(): pl.pallas_call(own_kernel, out_shape=[state, state, state], grid_spec=plt...  16 us
    pallas_call x4, Pallas kernels, project(): pl.pallas_call(lambda *refs: project_kernel(other, *refs), out_shape=jax....  14.3 us
    ppermute x6, waiting for transfers between devices, to_chip(): return lax.ppermute(value, 'slab', pairs)  13.9 us
    ppermute x1, waiting for transfers between devices, to_group(): return lax.ppermute(value, 'heads', [(0, 1), (1, 0)])  12.1 us
    ppermute x3, starting transfers between devices, from_chip(): return lax.ppermute(value, 'slab', pairs)  10.3 us
  transfers between devices with their start and end apart: 24, of which 8 were waited for; matrix products, arithmetic and copies ran while one was open for 0% of the time, Pallas kernels for 26%

profile of v1, /device:TPU:1, one launch (start us, length us, event | category | flops | bytes accessed | tf_op | source)
XLA Modules:
  0.0 176.8 jit_solution(6918684000534166994)
XLA Ops:
  4.0 4.5 %collective-permute-start.4 = (bf16[192,3072]{1,0:T(8,128)(2,1)S(1)}, bf16[192,3072]{1,0:T(8,128)(2,1)S(1)}, u32[]{:S(2)}, u32[]{:S(2)}) collective-permute-start(bf16[192,3072]{1,0:T(8,128)(2,1)S(1)} %modulate.1.refs_1_), channel_id=1, source_target_pairs={{0,64},{64,0},{1,65},{65,1},{2,66},{66,2},{3,67},{67,3},{4,68},{68... | collective-permute-start | bytes 3538952 | tf_op jit(solution)/shard_map/ppermute | solution.py:94
  8.6 5.0 %copy-done = bf16[3072,2304]{1,0:T(8,128)(2,1)S(1)} copy-done((bf16[3072,2304]{1,0:T(8,128)(2,1)S(1)}, bf16[3072,2304]{1,0:T(8,128)(2,1)}, u32[]{:S(2)}) %copy-start) | copy-done | bytes 14155800
  13.6 3.6 %shard_map.101 = bf16[4,208,384]{2,1,0:T(8,128)(2,1)S(1)} custom-call(s32[1]{0:T(128)} %bitcast.refs_0_.s_ref, bf16[192,3072]{1,0:T(8,128)(2,1)S(1)} %modulate.1.refs_1_, bf16[3072,2304]{1,0:T(8,128)(2,1)S(1)} %copy-done, f32[1,128]{1,0:T(1,128)S(1)} %bitcast.16, f32[1,128]{1,0:T(1,128)S(1)} %bitcast.20, bf16[16,384]{1,0:T(8,128)(2,1)S(1)} %pad.7.refs_5_), custom_call_target="tpu_custom_call" | custom-call | tf_op jit(solution)/shard_map/pallas_call | solution.py:161
  18.2 3.5 %shard_map.100.refs_0_ = bf16[4,208,384]{2,1,0:T(8,128)(2,1)S(1)} custom-call(s32[1]{0:T(128)} %bitcast.refs_0_.s_ref, bf16[192,3072]{1,0:T(8,128)(2,1)S(1)} %modulate.1.refs_1_, bf16[3072,2304]{1,0:T(8,128)(2,1)S(1)} %copy-done, f32[1,128]{1,0:T(1,128)S(1)} %bitcast.17, f32[1,128]{1,0:T(1,128)S(1)} %bitcast.21, bf16[16,384]{1,0:T(8,128)(2,1)S(1)} %pad.7.refs_5_), custom_call_target="tpu_custom_call" | custom-call | tf_op jit(solution)/shard_map/pallas_call | solution.py:161
  22.1 12.1 %collective-permute-done.4.refs_1_ = bf16[192,3072]{1,0:T(8,128)(2,1)S(1)} collective-permute-done((bf16[192,3072]{1,0:T(8,128)(2,1)S(1)}, bf16[192,3072]{1,0:T(8,128)(2,1)S(1)}, u32[]{:S(2)}, u32[]{:S(2)}) %collective-permute-start.4) | collective-permute-done | bytes 1179680 | tf_op jit(solution)/shard_map/ppermute | solution.py:94
  34.2 3.6 %shard_map.103 = bf16[4,192,384]{2,1,0:T(8,128)(2,1)S(1)} custom-call(s32[1]{0:T(128)} %bitcast.refs_0_.s_ref, bf16[192,3072]{1,0:T(8,128)(2,1)S(1)} %collective-permute-done.4.refs_1_, bf16[3072,2304]{1,0:T(8,128)(2,1)S(1)} %bitcast.10, f32[1,128]{1,0:T(1,128)S(1)} %bitcast.18, f32[1,128]{1,0:T(1,128)S(1)} %bitcast.22, bf16[16,384]{1,0:T(8,128)(2,1)S(1)} %pad.7.refs_5_), custom_call_target="tpu_custom_call" | custom-call | tf_op jit(solution)/shard_map/pallas_call | solution.py:161
  37.8 1.3 collective-permute-start.5
  39.2 4.7 %collective-permute-start.1 = (bf16[2,208,384]{2,1,0:T(8,128)(2,1)S(1)}, bf16[2,208,384]{2,1,0:T(8,128)(2,1)S(1)}, u32[]{:S(2)}, u32[]{:S(2)}) collective-permute-start(bf16[2,208,384]{2,1,0:T(8,128)(2,1)S(1)} %pad_maximum_fusion.1), channel_id=1, source_target_pairs={{0,4},{1,5},{2,6},{3,7},{4,0},{5,1},{6,2},{7,3},{8,12},{10,14},{11... | collective-permute-start | bytes 958472 | tf_op jit(solution)/shard_map/ppermute | solution.py:66
  43.9 1.9 %collective-permute-start.2 = (bf16[2,208,384]{2,1,0:T(8,128)(2,1)S(1)}, bf16[2,208,384]{2,1,0:T(8,128)(2,1)S(1)}, u32[]{:S(2)}, u32[]{:S(2)}) collective-permute-start(bf16[2,208,384]{2,1,0:T(8,128)(2,1)S(1)} %pad_maximum_fusion.2), channel_id=1, source_target_pairs={{0,16},{1,17},{2,18},{7,23},{8,24},{9,25},{10,26},{11,27},{13,29},... | collective-permute-start | bytes 958472 | tf_op jit(solution)/shard_map/ppermute | solution.py:66
  47.2 3.6 %shard_map.102.refs_5_ = bf16[4,192,384]{2,1,0:T(8,128)(2,1)S(1)} custom-call(s32[1]{0:T(128)} %bitcast.refs_0_.s_ref, bf16[192,3072]{1,0:T(8,128)(2,1)S(1)} %collective-permute-done.4.refs_1_, bf16[3072,2304]{1,0:T(8,128)(2,1)S(1)} %bitcast.10, f32[1,128]{1,0:T(1,128)S(1)} %bitcast.19, f32[1,128]{1,0:T(1,128)S(1)} %bitcast.23, bf16[16,384]{1,0:T(8,128)(2,1)S(1)} %pad.7.refs_5_), custom_call_target="tpu_custom_call" | custom-call | tf_op jit(solution)/shard_map/pallas_call | solution.py:161
  50.9 8.2 %collective-permute-start.6 = (bf16[2,192,384]{2,1,0:T(8,128)(2,1)S(1)}, bf16[2,192,384]{2,1,0:T(8,128)(2,1)S(1)}, u32[]{:S(2)}, u32[]{:S(2)}) collective-permute-start(bf16[2,192,384]{2,1,0:T(8,128)(2,1)S(1)} %pad_maximum_fusion.4), channel_id=1, source_target_pairs={{0,4},{1,5},{2,6},{3,7},{4,0},{5,1},{6,2},{7,3},{8,12},{10,14},{11... | collective-permute-start | bytes 884744 | tf_op jit(solution)/shard_map/ppermute | solution.py:66
  59.1 1.9 %collective-permute-start.7 = (bf16[2,192,384]{2,1,0:T(8,128)(2,1)S(1)}, bf16[2,192,384]{2,1,0:T(8,128)(2,1)S(1)}, u32[]{:S(2)}, u32[]{:S(2)}) collective-permute-start(bf16[2,192,384]{2,1,0:T(8,128)(2,1)S(1)} %pad_maximum_fusion.5), channel_id=1, source_target_pairs={{0,16},{1,17},{2,18},{7,23},{8,24},{9,25},{10,26},{11,27},{13,29},... | collective-permute-start | bytes 884744 | tf_op jit(solution)/shard_map/ppermute | solution.py:66
  62.9 3.8 %collective-permute-done.6.refs_7_ = bf16[2,192,384]{2,1,0:T(8,128)(2,1)S(1)} collective-permute-done((bf16[2,192,384]{2,1,0:T(8,128)(2,1)S(1)}, bf16[2,192,384]{2,1,0:T(8,128)(2,1)S(1)}, u32[]{:S(2)}, u32[]{:S(2)}) %collective-permute-start.6) | collective-permute-done | bytes 294944 | tf_op jit(solution)/shard_map/ppermute | solution.py:66
  66.8 9.5 %collective-permute-done.7.refs_8_ = bf16[2,192,384]{2,1,0:T(8,128)(2,1)S(1)} collective-permute-done((bf16[2,192,384]{2,1,0:T(8,128)(2,1)S(1)}, bf16[2,192,384]{2,1,0:T(8,128)(2,1)S(1)}, u32[]{:S(2)}, u32[]{:S(2)}) %collective-permute-start.7) | collective-permute-done | bytes 294944 | tf_op jit(solution)/shard_map/ppermute | solution.py:66
  76.9 2.9 %collective-permute-start.9 = (bf16[4,384,256]{2,1,0:T(8,128)(2,1)S(1)}, bf16[4,384,256]{2,1,0:T(8,128)(2,1)S(1)}, u32[]{:S(2)}, u32[]{:S(2)}) collective-permute-start(bf16[4,384,256]{2,1,0:T(8,128)(2,1)S(1)} %get-tuple-element.34), channel_id=1, source_target_pairs={{0,32},{1,33},{2,34},{3,35},{4,36},{5,37},{6,38},{7,39},{8,40},{9,... | collective-permute-start | bytes 2359304 | tf_op jit(solution)/shard_map/ppermute | solution.py:90
  79.8 2.3 %collective-permute-start.16 = (bf16[384,3072]{1,0:T(8,128)(2,1)S(1)}, bf16[384,3072]{1,0:T(8,128)(2,1)S(1)}, u32[]{:S(2)}, u32[]{:S(2)}) collective-permute-start(bf16[384,3072]{1,0:T(8,128)(2,1)S(1)} %weight_part.1), channel_id=1, source_target_pairs={{0,96},{1,97},{2,98},{3,99},{4,100},{5,101},{6,102},{7,103},{8,104... | collective-permute-start | bytes 7077896 | tf_op jit(solution)/shard_map/ppermute | solution.py:81
  82.1 4.2 %collective-permute-start.10 = (bf16[4,384,256]{2,1,0:T(8,128)(2,1)S(1)}, bf16[4,384,256]{2,1,0:T(8,128)(2,1)S(1)}, u32[]{:S(2)}, u32[]{:S(2)}) collective-permute-start(bf16[4,384,256]{2,1,0:T(8,128)(2,1)S(1)} %get-tuple-element.38), channel_id=1, source_target_pairs={{0,2},{1,7},{2,0},{3,5},{4,6},{5,3},{6,4},{7,1},{8,10},{9,15},{10,... | collective-permute-start | bytes 2359304 | tf_op jit(solution)/shard_map/ppermute | solution.py:90
  86.2 3.0 %collective-permute-start.11 = (bf16[4,384,256]{2,1,0:T(8,128)(2,1)S(1)}, bf16[4,384,256]{2,1,0:T(8,128)(2,1)S(1)}, u32[]{:S(2)}, u32[]{:S(2)}) collective-permute-start(bf16[4,384,256]{2,1,0:T(8,128)(2,1)S(1)} %get-tuple-element.39), channel_id=1, source_target_pairs={{0,8},{1,25},{2,10},{3,27},{4,12},{5,29},{6,14},{7,31},{8,0},{9,17... | collective-permute-start | bytes 2359304 | tf_op jit(solution)/shard_map/ppermute | solution.py:90
  89.3 4.3 %collective-permute-start.12 = (bf16[2,384,256]{2,1,0:T(8,128)(2,1)S(1)}, bf16[2,384,256]{2,1,0:T(8,128)(2,1)S(1)}, u32[]{:S(2)}, u32[]{:S(2)}) collective-permute-start(bf16[2,384,256]{2,1,0:T(8,128)(2,1)S(1)} %get-tuple-element.41), channel_id=1, source_target_pairs={{0,10},{1,31},{2,8},{3,29},{4,14},{5,27},{6,12},{7,25},{8,2},{9,23... | collective-permute-start | bytes 1179656 | tf_op jit(solution)/shard_map/ppermute | solution.py:90
  93.6 16.0 %attend_own.1 = (f32[8,384,128]{2,1,0:T(8,128)S(1)}, f32[8,384,128]{2,1,0:T(8,128)S(1)}, f32[8,384,128]{2,1,0:T(8,128)S(1)}) custom-call(s32[8,128]{1,0:T(8,128)S(1)} %get-tuple-element.28.live_ref.refs_1_, bf16[8,384,128]{2,1,0:T(8,128)(2,1)S(1)} %get-tuple-element.29.q_ref.refs_2_, bf16[8,384,256]{2,1,0:T(8,128)(2,1)S(1)} %get-tuple-element.30.kv_ref), custom_call_target="tpu_custom_call" | custom-call | tf_op jit(solution)/shard_map/attend_own/pallas_call | solution.py:355
  109.8 2.1 %collective-permute-start.13 = (bf16[2,384,256]{2,1,0:T(8,128)(2,1)S(1)}, bf16[2,384,256]{2,1,0:T(8,128)(2,1)S(1)}, u32[]{:S(2)}, u32[]{:S(2)}) collective-permute-start(bf16[2,384,256]{2,1,0:T(8,128)(2,1)S(1)} %pad_maximum_fusion), channel_id=1, source_target_pairs={{0,2},{1,7},{2,0},{3,5},{4,6},{5,3},{6,4},{7,1},{8,10},{9,15},{10,... | collective-permute-start | bytes 1179656 | tf_op jit(solution)/shard_map/ppermute | solution.py:90
  111.9 5.6 %collective-permute-start.14 = (bf16[2,384,256]{2,1,0:T(8,128)(2,1)S(1)}, bf16[2,384,256]{2,1,0:T(8,128)(2,1)S(1)}, u32[]{:S(2)}, u32[]{:S(2)}) collective-permute-start(bf16[2,384,256]{2,1,0:T(8,128)(2,1)S(1)} %stack.34), channel_id=1, source_target_pairs={{0,8},{1,25},{2,10},{3,27},{4,12},{5,29},{6,14},{7,31},{8,0},{9,17... | collective-permute-start | bytes 1179656 | tf_op jit(solution)/shard_map/ppermute | solution.py:90
  117.5 4.5 %collective-permute-start.15 = (bf16[1,384,256]{2,1,0:T(8,128)(2,1)S(1)}, bf16[1,384,256]{2,1,0:T(8,128)(2,1)S(1)}, u32[]{:S(2)}, u32[]{:S(2)}) collective-permute-start(bf16[1,384,256]{2,1,0:T(8,128)(2,1)S(1)} %get-tuple-element.49), channel_id=1, source_target_pairs={{0,10},{1,31},{2,8},{3,29},{4,14},{5,27},{6,12},{7,25},{8,2},{9,23... | collective-permute-start | bytes 589832 | tf_op jit(solution)/shard_map/ppermute | solution.py:90
  122.0 5.2 %collective-permute-done.15.refs_12_ = bf16[1,384,256]{2,1,0:T(8,128)(2,1)S(1)} collective-permute-done((bf16[1,384,256]{2,1,0:T(8,128)(2,1)S(1)}, bf16[1,384,256]{2,1,0:T(8,128)(2,1)S(1)}, u32[]{:S(2)}, u32[]{:S(2)}) %collective-permute-start.15) | collective-permute-done | bytes 196640 | tf_op jit(solution)/shard_map/ppermute | solution.py:90
  127.2 11.4 %shard_map.105 = (bf16[4,192,128]{2,1,0:T(8,128)(2,1)S(1)}, bf16[4,192,128]{2,1,0:T(8,128)(2,1)S(1)}) custom-call(s32[1]{0:T(128)} %bitcast.refs_0_.s_ref, s32[8,128]{1,0:T(8,128)S(1)} %get-tuple-element.28.live_ref.refs_1_, bf16[8,384,128]{2,1,0:T(8,128)(2,1)S(1)} %get-tuple-element.29.q_ref.refs_2_, f32[8,384,128]{2,1,0:T(8,128)S(1)} %get-tuple-element.35.refs_3_, ...), custom_call_target="tpu_custom_call" | custom-call | tf_op jit(solution)/shard_map/pallas_call | solution.py:406
  138.6 3.0 %collective-permute-start.19 = (bf16[4,192,128]{2,1,0:T(8,128)(2,1)S(1)}, bf16[4,192,128]{2,1,0:T(8,128)(2,1)S(1)}, u32[]{:S(2)}, u32[]{:S(2)}) collective-permute-start(bf16[4,192,128]{2,1,0:T(8,128)(2,1)S(1)} %get-tuple-element.47), channel_id=1, source_target_pairs={{0,64},{1,65},{2,66},{3,67},{4,68},{5,69},{6,70},{7,71},{8,72},{9,... | collective-permute-start | bytes 589832 | tf_op jit(solution)/shard_map/ppermute | solution.py:76
  141.6 7.3 %shard_map.104 = (bf16[4,192,128]{2,1,0:T(8,128)(2,1)S(1)}, bf16[4,192,128]{2,1,0:T(8,128)(2,1)S(1)}) custom-call(s32[1]{0:T(128)} %bitcast.refs_0_.s_ref, s32[8,128]{1,0:T(8,128)S(1)} %get-tuple-element.28.live_ref.refs_1_, bf16[8,384,128]{2,1,0:T(8,128)(2,1)S(1)} %get-tuple-element.29.q_ref.refs_2_, f32[8,384,128]{2,1,0:T(8,128)S(1)} %get-tuple-element.35.refs_3_, ...), custom_call_target="tpu_custom_call" | custom-call | tf_op jit(solution)/shard_map/pallas_call | solution.py:406
  148.9 3.8 %collective-permute-start.17 = (bf16[4,192,128]{2,1,0:T(8,128)(2,1)S(1)}, bf16[4,192,128]{2,1,0:T(8,128)(2,1)S(1)}, u32[]{:S(2)}, u32[]{:S(2)}) collective-permute-start(bf16[4,192,128]{2,1,0:T(8,128)(2,1)S(1)} %get-tuple-element.45), channel_id=1, source_target_pairs={{0,64},{1,65},{2,66},{3,67},{4,68},{5,69},{6,70},{7,71},{8,72},{9,... | collective-permute-start | bytes 589832 | tf_op jit(solution)/shard_map/ppermute | solution.py:76
  152.8 1.9 %collective-permute-start.20 = (bf16[4,192,128]{2,1,0:T(8,128)(2,1)S(1)}, bf16[4,192,128]{2,1,0:T(8,128)(2,1)S(1)}, u32[]{:S(2)}, u32[]{:S(2)}) collective-permute-start(bf16[4,192,128]{2,1,0:T(8,128)(2,1)S(1)} %pad_maximum_fusion.8), channel_id=1, source_target_pairs={{0,16},{1,17},{2,18},{3,19},{4,20},{5,21},{6,22},{7,23},{8,24},{9,... | collective-permute-start | bytes 589832 | tf_op jit(solution)/shard_map/ppermute | solution.py:71
  157.3 7.1 %collective-permute-start.18 = (bf16[4,192,128]{2,1,0:T(8,128)(2,1)S(1)}, bf16[4,192,128]{2,1,0:T(8,128)(2,1)S(1)}, u32[]{:S(2)}, u32[]{:S(2)}) collective-permute-start(bf16[4,192,128]{2,1,0:T(8,128)(2,1)S(1)} %pad_maximum_fusion.7), channel_id=1, source_target_pairs={{0,4},{1,5},{2,6},{3,7},{4,0},{5,1},{6,2},{7,3},{8,12},{9,13},{10,... | collective-permute-start | bytes 589832 | tf_op jit(solution)/shard_map/ppermute | solution.py:71
  164.5 5.9 %collective-permute-done.18 = bf16[4,192,128]{2,1,0:T(8,128)(2,1)S(1)} collective-permute-done((bf16[4,192,128]{2,1,0:T(8,128)(2,1)S(1)}, bf16[4,192,128]{2,1,0:T(8,128)(2,1)S(1)}, u32[]{:S(2)}, u32[]{:S(2)}) %collective-permute-start.18) | collective-permute-done | bytes 196640 | tf_op jit(solution)/shard_map/ppermute | solution.py:71
  172.4 4.4 %output.1 = bf16[192,3072]{1,0:T(8,128)(2,1)} custom-call(s32[1]{0:T(128)} %bitcast.refs_0_.s_ref, bf16[2,192,128]{2,1,0:T(8,128)(2,1)S(1)} %get-tuple-element.76.refs_0_, bf16[2,192,128]{2,1,0:T(8,128)(2,1)S(1)} %get-tuple-element.68.refs_1_, bf16[2,192,128]{2,1,0:T(8,128)(2,1)S(1)} %get-tuple-element.66.refs_2_, ...), custom_call_target="tpu_custom_call" | custom-call | tf_op jit(solution)/shard_map/output/pallas_call | solution.py:462
  (93 shorter events, 14.1 us)
Async XLA Ops:
  0.0 8.5 %copy-start.7 = (f32[128]{0:T(128)S(1)}, f32[128]{0:T(128)}, u32[]{:S(2)}) copy-start(f32[128]{0:T(128)} %param.14) | copy-start | bytes 1540
  0.0 8.5 %copy-start.6 = (f32[128]{0:T(128)S(1)}, f32[128]{0:T(128)}, u32[]{:S(2)}) copy-start(f32[128]{0:T(128)} %param.13) | copy-start | bytes 1540
  4.0 30.2 %collective-permute-start.4 = (bf16[192,3072]{1,0:T(8,128)(2,1)S(1)}, bf16[192,3072]{1,0:T(8,128)(2,1)S(1)}, u32[]{:S(2)}, u32[]{:S(2)}) collective-permute-start(bf16[192,3072]{1,0:T(8,128)(2,1)S(1)} %modulate.1.refs_1_), channel_id=1, source_target_pairs={{0,64},{64,0},{1,65},{65,1},{2,66},{66,2},{3,67},{67,3},{4,68},{68... | collective-permute-start | bytes 3538952 | tf_op jit(solution)/shard_map/ppermute | solution.py:94
  13.6 20.6 %slice-start = ((s8[14155776]{0:T(1024)(128)(4,1)}), s8[4194304]{0:T(1024)(128)(4,1)S(1)}, s32[]{:S(2)}) async-start(s8[14155776]{0:T(1024)(128)(4,1)} %bitcast.9), calls=%async_computation | async-start | bytes 8388608
  13.6 20.6 %slice-start.1 = ((s8[14155776]{0:T(1024)(128)(4,1)}), s8[4194304]{0:T(1024)(128)(4,1)S(1)}, s32[]{:S(2)}) async-start(s8[14155776]{0:T(1024)(128)(4,1)} %bitcast.9), calls=%async_computation.1 | async-start | bytes 8388608
  17.2 17.0 %slice-start.2 = ((s8[14155776]{0:T(1024)(128)(4,1)}), s8[4194304]{0:T(1024)(128)(4,1)S(1)}, s32[]{:S(2)}) async-start(s8[14155776]{0:T(1024)(128)(4,1)} %bitcast.9), calls=%async_computation.2 | async-start | bytes 8388608
  17.2 17.0 %slice-start.3 = ((s8[14155776]{0:T(1024)(128)(4,1)}), s8[1572864]{0:T(1024)(128)(4,1)S(1)}, s32[]{:S(2)}) async-start(s8[14155776]{0:T(1024)(128)(4,1)} %bitcast.9), calls=%async_computation.3 | async-start | bytes 3145728
  17.2 4.9 %collective-permute-start = (bf16[4,208,384]{2,1,0:T(8,128)(2,1)S(1)}, bf16[4,208,384]{2,1,0:T(8,128)(2,1)S(1)}, u32[]{:S(2)}, u32[]{:S(2)}) collective-permute-start(bf16[4,208,384]{2,1,0:T(8,128)(2,1)S(1)} %shard_map.101), channel_id=1, source_target_pairs={{0,1},{1,0},{2,3},{3,2},{4,5},{5,4},{6,7},{7,6},{8,9},{9,8},{10,11... | collective-permute-start | bytes 1916936 | tf_op jit(solution)/shard_map/ppermute | solution.py:85
  37.8 13.0 %collective-permute-start.5 = (bf16[4,192,384]{2,1,0:T(8,128)(2,1)S(1)}, bf16[4,192,384]{2,1,0:T(8,128)(2,1)S(1)}, u32[]{:S(2)}, u32[]{:S(2)}) collective-permute-start(bf16[4,192,384]{2,1,0:T(8,128)(2,1)S(1)} %shard_map.103), channel_id=1, source_target_pairs={{0,1},{1,0},{2,3},{3,2},{4,5},{5,4},{6,7},{7,6},{8,9},{9,8},{10,11... | collective-permute-start | bytes 1769480 | tf_op jit(solution)/shard_map/ppermute | solution.py:85
  39.2 21.9 %collective-permute-start.1 = (bf16[2,208,384]{2,1,0:T(8,128)(2,1)S(1)}, bf16[2,208,384]{2,1,0:T(8,128)(2,1)S(1)}, u32[]{:S(2)}, u32[]{:S(2)}) collective-permute-start(bf16[2,208,384]{2,1,0:T(8,128)(2,1)S(1)} %pad_maximum_fusion.1), channel_id=1, source_target_pairs={{0,4},{1,5},{2,6},{3,7},{4,0},{5,1},{6,2},{7,3},{8,12},{10,14},{11... | collective-permute-start | bytes 958472 | tf_op jit(solution)/shard_map/ppermute | solution.py:66
  43.9 19.0 %collective-permute-start.2 = (bf16[2,208,384]{2,1,0:T(8,128)(2,1)S(1)}, bf16[2,208,384]{2,1,0:T(8,128)(2,1)S(1)}, u32[]{:S(2)}, u32[]{:S(2)}) collective-permute-start(bf16[2,208,384]{2,1,0:T(8,128)(2,1)S(1)} %pad_maximum_fusion.2), channel_id=1, source_target_pairs={{0,16},{1,17},{2,18},{7,23},{8,24},{9,25},{10,26},{11,27},{13,29},... | collective-permute-start | bytes 958472 | tf_op jit(solution)/shard_map/ppermute | solution.py:66
  45.9 17.1 %collective-permute-start.3 = (bf16[2,208,384]{2,1,0:T(8,128)(2,1)S(1)}, bf16[2,208,384]{2,1,0:T(8,128)(2,1)S(1)}, u32[]{:S(2)}, u32[]{:S(2)}) collective-permute-start(bf16[2,208,384]{2,1,0:T(8,128)(2,1)S(1)} %pad_maximum_fusion.3), channel_id=1, source_target_pairs={{3,23},{4,16},{5,17},{6,18},{9,29},{11,31},{12,24},{13,25},{14,26}... | collective-permute-start | bytes 958472 | tf_op jit(solution)/shard_map/ppermute | solution.py:66
  50.8 25.5 %copy-start.2 = (s32[8,8,128]{2,1,0:T(8,128)S(1)}, s32[8,8,128]{2,1,0:T(8,128)}, u32[]{:S(2)}) copy-start(s32[8,8,128]{2,1,0:T(8,128)} %constant.9.clone.refs_10_) | copy-start | bytes 98308
  50.9 15.9 %collective-permute-start.6 = (bf16[2,192,384]{2,1,0:T(8,128)(2,1)S(1)}, bf16[2,192,384]{2,1,0:T(8,128)(2,1)S(1)}, u32[]{:S(2)}, u32[]{:S(2)}) collective-permute-start(bf16[2,192,384]{2,1,0:T(8,128)(2,1)S(1)} %pad_maximum_fusion.4), channel_id=1, source_target_pairs={{0,4},{1,5},{2,6},{3,7},{4,0},{5,1},{6,2},{7,3},{8,12},{10,14},{11... | collective-permute-start | bytes 884744 | tf_op jit(solution)/shard_map/ppermute | solution.py:66
  59.1 17.1 %collective-permute-start.7 = (bf16[2,192,384]{2,1,0:T(8,128)(2,1)S(1)}, bf16[2,192,384]{2,1,0:T(8,128)(2,1)S(1)}, u32[]{:S(2)}, u32[]{:S(2)}) collective-permute-start(bf16[2,192,384]{2,1,0:T(8,128)(2,1)S(1)} %pad_maximum_fusion.5), channel_id=1, source_target_pairs={{0,16},{1,17},{2,18},{7,23},{8,24},{9,25},{10,26},{11,27},{13,29},... | collective-permute-start | bytes 884744 | tf_op jit(solution)/shard_map/ppermute | solution.py:66
  61.1 15.2 %collective-permute-start.8 = (bf16[2,192,384]{2,1,0:T(8,128)(2,1)S(1)}, bf16[2,192,384]{2,1,0:T(8,128)(2,1)S(1)}, u32[]{:S(2)}, u32[]{:S(2)}) collective-permute-start(bf16[2,192,384]{2,1,0:T(8,128)(2,1)S(1)} %pad_maximum_fusion.6), channel_id=1, source_target_pairs={{3,23},{4,16},{5,17},{6,18},{9,29},{11,31},{12,24},{13,25},{14,26}... | collective-permute-start | bytes 884744 | tf_op jit(solution)/shard_map/ppermute | solution.py:66
  76.9 32.8 %collective-permute-start.9 = (bf16[4,384,256]{2,1,0:T(8,128)(2,1)S(1)}, bf16[4,384,256]{2,1,0:T(8,128)(2,1)S(1)}, u32[]{:S(2)}, u32[]{:S(2)}) collective-permute-start(bf16[4,384,256]{2,1,0:T(8,128)(2,1)S(1)} %get-tuple-element.34), channel_id=1, source_target_pairs={{0,32},{1,33},{2,34},{3,35},{4,36},{5,37},{6,38},{7,39},{8,40},{9,... | collective-permute-start | bytes 2359304 | tf_op jit(solution)/shard_map/ppermute | solution.py:90
  79.8 77.4 %collective-permute-start.16 = (bf16[384,3072]{1,0:T(8,128)(2,1)S(1)}, bf16[384,3072]{1,0:T(8,128)(2,1)S(1)}, u32[]{:S(2)}, u32[]{:S(2)}) collective-permute-start(bf16[384,3072]{1,0:T(8,128)(2,1)S(1)} %weight_part.1), channel_id=1, source_target_pairs={{0,96},{1,97},{2,98},{3,99},{4,100},{5,101},{6,102},{7,103},{8,104... | collective-permute-start | bytes 7077896 | tf_op jit(solution)/shard_map/ppermute | solution.py:81
  82.1 35.4 %collective-permute-start.10 = (bf16[4,384,256]{2,1,0:T(8,128)(2,1)S(1)}, bf16[4,384,256]{2,1,0:T(8,128)(2,1)S(1)}, u32[]{:S(2)}, u32[]{:S(2)}) collective-permute-start(bf16[4,384,256]{2,1,0:T(8,128)(2,1)S(1)} %get-tuple-element.38), channel_id=1, source_target_pairs={{0,2},{1,7},{2,0},{3,5},{4,6},{5,3},{6,4},{7,1},{8,10},{9,15},{10,... | collective-permute-start | bytes 2359304 | tf_op jit(solution)/shard_map/ppermute | solution.py:90
  86.2 35.8 %collective-permute-start.11 = (bf16[4,384,256]{2,1,0:T(8,128)(2,1)S(1)}, bf16[4,384,256]{2,1,0:T(8,128)(2,1)S(1)}, u32[]{:S(2)}, u32[]{:S(2)}) collective-permute-start(bf16[4,384,256]{2,1,0:T(8,128)(2,1)S(1)} %get-tuple-element.39), channel_id=1, source_target_pairs={{0,8},{1,25},{2,10},{3,27},{4,12},{5,29},{6,14},{7,31},{8,0},{9,17... | collective-permute-start | bytes 2359304 | tf_op jit(solution)/shard_map/ppermute | solution.py:90
  89.3 22.6 %collective-permute-start.12 = (bf16[2,384,256]{2,1,0:T(8,128)(2,1)S(1)}, bf16[2,384,256]{2,1,0:T(8,128)(2,1)S(1)}, u32[]{:S(2)}, u32[]{:S(2)}) collective-permute-start(bf16[2,384,256]{2,1,0:T(8,128)(2,1)S(1)} %get-tuple-element.41), channel_id=1, source_target_pairs={{0,10},{1,31},{2,8},{3,29},{4,14},{5,27},{6,12},{7,25},{8,2},{9,23... | collective-permute-start | bytes 1179656 | tf_op jit(solution)/shard_map/ppermute | solution.py:90
  109.8 17.5 %collective-permute-start.13 = (bf16[2,384,256]{2,1,0:T(8,128)(2,1)S(1)}, bf16[2,384,256]{2,1,0:T(8,128)(2,1)S(1)}, u32[]{:S(2)}, u32[]{:S(2)}) collective-permute-start(bf16[2,384,256]{2,1,0:T(8,128)(2,1)S(1)} %pad_maximum_fusion), channel_id=1, source_target_pairs={{0,2},{1,7},{2,0},{3,5},{4,6},{5,3},{6,4},{7,1},{8,10},{9,15},{10,... | collective-permute-start | bytes 1179656 | tf_op jit(solution)/shard_map/ppermute | solution.py:90
  111.9 15.4 %collective-permute-start.14 = (bf16[2,384,256]{2,1,0:T(8,128)(2,1)S(1)}, bf16[2,384,256]{2,1,0:T(8,128)(2,1)S(1)}, u32[]{:S(2)}, u32[]{:S(2)}) collective-permute-start(bf16[2,384,256]{2,1,0:T(8,128)(2,1)S(1)} %stack.34), channel_id=1, source_target_pairs={{0,8},{1,25},{2,10},{3,27},{4,12},{5,29},{6,14},{7,31},{8,0},{9,17... | collective-permute-start | bytes 1179656 | tf_op jit(solution)/shard_map/ppermute | solution.py:90
  117.5 9.7 %collective-permute-start.15 = (bf16[1,384,256]{2,1,0:T(8,128)(2,1)S(1)}, bf16[1,384,256]{2,1,0:T(8,128)(2,1)S(1)}, u32[]{:S(2)}, u32[]{:S(2)}) collective-permute-start(bf16[1,384,256]{2,1,0:T(8,128)(2,1)S(1)} %get-tuple-element.49), channel_id=1, source_target_pairs={{0,10},{1,31},{2,8},{3,29},{4,14},{5,27},{6,12},{7,25},{8,2},{9,23... | collective-permute-start | bytes 589832 | tf_op jit(solution)/shard_map/ppermute | solution.py:90
  138.6 14.1 %collective-permute-start.19 = (bf16[4,192,128]{2,1,0:T(8,128)(2,1)S(1)}, bf16[4,192,128]{2,1,0:T(8,128)(2,1)S(1)}, u32[]{:S(2)}, u32[]{:S(2)}) collective-permute-start(bf16[4,192,128]{2,1,0:T(8,128)(2,1)S(1)} %get-tuple-element.47), channel_id=1, source_target_pairs={{0,64},{1,65},{2,66},{3,67},{4,68},{5,69},{6,70},{7,71},{8,72},{9,... | collective-permute-start | bytes 589832 | tf_op jit(solution)/shard_map/ppermute | solution.py:76
  148.9 8.2 %collective-permute-start.17 = (bf16[4,192,128]{2,1,0:T(8,128)(2,1)S(1)}, bf16[4,192,128]{2,1,0:T(8,128)(2,1)S(1)}, u32[]{:S(2)}, u32[]{:S(2)}) collective-permute-start(bf16[4,192,128]{2,1,0:T(8,128)(2,1)S(1)} %get-tuple-element.45), channel_id=1, source_target_pairs={{0,64},{1,65},{2,66},{3,67},{4,68},{5,69},{6,70},{7,71},{8,72},{9,... | collective-permute-start | bytes 589832 | tf_op jit(solution)/shard_map/ppermute | solution.py:76
  152.8 11.7 %collective-permute-start.20 = (bf16[4,192,128]{2,1,0:T(8,128)(2,1)S(1)}, bf16[4,192,128]{2,1,0:T(8,128)(2,1)S(1)}, u32[]{:S(2)}, u32[]{:S(2)}) collective-permute-start(bf16[4,192,128]{2,1,0:T(8,128)(2,1)S(1)} %pad_maximum_fusion.8), channel_id=1, source_target_pairs={{0,16},{1,17},{2,18},{3,19},{4,20},{5,21},{6,22},{7,23},{8,24},{9,... | collective-permute-start | bytes 589832 | tf_op jit(solution)/shard_map/ppermute | solution.py:71
  154.7 17.7 %copy-start.5 = (f32[3072]{0:T(1024)S(1)}, f32[3072]{0:T(1024)}, u32[]{:S(2)}) copy-start(f32[3072]{0:T(1024)} %param.17) | copy-start | bytes 36868
  154.8 15.6 %collective-permute-start.21 = (bf16[4,192,128]{2,1,0:T(8,128)(2,1)S(1)}, bf16[4,192,128]{2,1,0:T(8,128)(2,1)S(1)}, u32[]{:S(2)}, u32[]{:S(2)}) collective-permute-start(bf16[4,192,128]{2,1,0:T(8,128)(2,1)S(1)} %pad_maximum_fusion.9), channel_id=1, source_target_pairs={{0,20},{1,21},{2,22},{3,23},{4,16},{5,17},{6,18},{7,19},{8,28},{9,... | collective-permute-start | bytes 589832 | tf_op jit(solution)/shard_map/ppermute | solution.py:71
  157.2 15.2 %collective-permute-start.23 = (bf16[384,3072]{1,0:T(8,128)(2,1)S(1)}, bf16[384,3072]{1,0:T(8,128)(2,1)S(1)}, u32[]{:S(2)}, u32[]{:S(2)}) collective-permute-start(bf16[384,3072]{1,0:T(8,128)(2,1)S(1)} %collective-permute-done.16.refs_10_), channel_id=1, source_target_pairs={{0,1},{1,0},{2,3},{3,2},{4,5},{5,4},{6,7},{7,6},{8,9},{9,8},{10,11... | collective-permute-start | bytes 7077896 | tf_op jit(solution)/shard_map/ppermute | solution.py:85
  157.3 13.0 %collective-permute-start.18 = (bf16[4,192,128]{2,1,0:T(8,128)(2,1)S(1)}, bf16[4,192,128]{2,1,0:T(8,128)(2,1)S(1)}, u32[]{:S(2)}, u32[]{:S(2)}) collective-permute-start(bf16[4,192,128]{2,1,0:T(8,128)(2,1)S(1)} %pad_maximum_fusion.7), channel_id=1, source_target_pairs={{0,4},{1,5},{2,6},{3,7},{4,0},{5,1},{6,2},{7,3},{8,12},{9,13},{10,... | collective-permute-start | bytes 589832 | tf_op jit(solution)/shard_map/ppermute | solution.py:71
  170.5 1.9 %collective-permute-start.22 = (bf16[8,192,128]{2,1,0:T(8,128)(2,1)S(1)}, bf16[8,192,128]{2,1,0:T(8,128)(2,1)S(1)}, u32[]{:S(2)}, u32[]{:S(2)}) collective-permute-start(bf16[8,192,128]{2,1,0:T(8,128)(2,1)S(1)} %slice_dynamic-update-slice_fusion), channel_id=1, source_target_pairs={{0,1},{1,0},{2,3},{3,2},{4,5},{5,4},{6,7},{7,6},{8,9},{9,8},{10,11... | collective-permute-start | bytes 1179656 | tf_op jit(solution)/shard_map/ppermute | solution.py:85
  (7 other events, 29.1 us)

commit v2 on v1

--- a/solution.py
+++ b/solution.py
@@ -400,15 +400,15 @@
     far_ref[0] = mixed[TILE // 2 :]
 
 
-def attend_halo(slab_at, live, q, state, pieces, first):
+def attend_halo(slab_at, live, q, state, pieces, first, tiles):
     per_u = pl.BlockSpec((1, TILE, HD), lambda r, s_ref, *_: ((first + r) ^ u_base(s_ref[0]), 0, 0))
     count = len(HALO_AT)
     return pl.pallas_call(
         lambda *refs: halo_kernel(first, *refs),
-        out_shape=[jax.ShapeDtypeStruct((4, TILE // 2, HD), jnp.bfloat16)] * 2,
+        out_shape=[jax.ShapeDtypeStruct((tiles, TILE // 2, HD), jnp.bfloat16)] * 2,
         grid_spec=pltpu.PrefetchScalarGridSpec(
             num_scalar_prefetch=2,
-            grid=(4,),
+            grid=(tiles,),
             in_specs=[per_u] * 4 + [pl.BlockSpec(memory_space=pl.ANY)] * len(pieces),
             out_specs=[pl.BlockSpec((1, TILE // 2, HD), lambda r, *_: (r, 0, 0))] * 2,
             scratch_shapes=[
@@ -513,23 +513,26 @@
         halves.append((keep, core, *near))
     weight_c = weight_across(part)
     q, kv, live, *sends = assemble(slab_at, halves)
-    halo = [to_block(piece, moved) for piece, (moved, _) in zip(sends, HALO)] + [None] * 3
+    halo = []
+    for piece, (moved, _) in zip(sends, HALO):
+        halo.append(to_block(piece, moved))
+    halo += [None] * 3
     state = attend_own(live, q, kv)
     *state, over = lax.optimization_barrier((*state, halo[2]))
     halo[2] = over
     for at, moved, us in ((4, (0, 0, 1), (0, 2)), (5, (0, 1, 0), (0, 1)), (6, (0, 1, 1), (0,))):
         halo[at] = to_block(jnp.stack([over[u] for u in us]), moved)
     done = {}
-    for first in (4, 0):
-        mixed, crossing = attend_halo(slab_at, live, q, state, halo, first)
+    for first, tiles in ((2, 6), (0, 2)):
+        mixed, crossing = attend_halo(slab_at, live, q, state, halo, first, tiles)
         if not first:
             mixed, weight_c = lax.optimization_barrier((mixed, weight_c))
         crossed = across(crossing)
-        for p in (first // 2, first // 2 + 1):
+        for p in range(first // 2, (first + tiles) // 2):
             r = slice(2 * p - first, 2 * p - first + 2)
             done[p] = (mixed[r], crossed[r])
     weight_d = to_core(weight_c)
-    for p in (2, 3, 1):
+    for p in (3, 2, 1):
         moved = from_chip(jnp.concatenate(done[p]), p)
         done[p] = (moved[:2], moved[2:])
     same, cross = zip(*(done[p] for p in range(4)), strict=True)

time: 178 us -> 174 us (0.978)
  the two profiles are of different devices: /device:TPU:1 before, /device:TPU:49 now
where the time goes in v2:
time: 174 us
  starting transfers between devices  74.6 us (43%)
  Pallas kernels  53.8 us (31%)
  waiting for transfers between devices  36 us (21%)
  local copies, waits for them, and re-layouts  8.22 us (5%)
    ppermute x7, starting transfers between devices, to_block(): return lax.ppermute(value, 'slab', pairs)  27.2 us
    ppermute x6, starting transfers between devices, to_chip(): return lax.ppermute(value, 'slab', pairs)  20 us
    pallas_call x2, Pallas kernels, attend_halo(): pl.pallas_call(lambda *refs: halo_kernel(first, *refs), out_shape=[jax.Sh...  17.7 us
    pallas_call x1, Pallas kernels, attend_own(): pl.pallas_call(own_kernel, out_shape=[state, state, state], grid_spec=plt...  15.5 us
    pallas_call x4, Pallas kernels, project(): pl.pallas_call(lambda *refs: project_kernel(other, *refs), out_shape=jax....  14.2 us
    ppermute x1, waiting for transfers between devices, to_group(): return lax.ppermute(value, 'heads', [(0, 1), (1, 0)])  12.1 us
    ppermute x3, starting transfers between devices, from_chip(): return lax.ppermute(value, 'slab', pairs)  11.5 us
    ppermute x6, waiting for transfers between devices, to_chip(): return lax.ppermute(value, 'slab', pairs)  10.7 us
  transfers between devices with their start and end apart: 24, of which 7 were waited for; matrix products, arithmetic and copies ran while one was open for 0% of the time, Pallas kernels for 26%

profile of v2, /device:TPU:49, one launch (start us, length us, event | category | flops | bytes accessed | tf_op | source)
XLA Modules:
  0.0 173.6 jit_solution(5686011226990405865)
XLA Ops:
  4.0 2.8 %collective-permute-start.4 = (bf16[192,3072]{1,0:T(8,128)(2,1)S(1)}, bf16[192,3072]{1,0:T(8,128)(2,1)S(1)}, u32[]{:S(2)}, u32[]{:S(2)}) collective-permute-start(bf16[192,3072]{1,0:T(8,128)(2,1)S(1)} %modulate.1.refs_1_), channel_id=1, source_target_pairs={{0,64},{64,0},{1,65},{65,1},{2,66},{66,2},{3,67},{67,3},{4,68},{68... | collective-permute-start | bytes 3538952 | tf_op jit(solution)/shard_map/ppermute | solution.py:94
  6.9 5.0 %copy-done = bf16[3072,2304]{1,0:T(8,128)(2,1)S(1)} copy-done((bf16[3072,2304]{1,0:T(8,128)(2,1)S(1)}, bf16[3072,2304]{1,0:T(8,128)(2,1)}, u32[]{:S(2)}) %copy-start) | copy-done | bytes 14155800
  11.9 3.6 %shard_map.101 = bf16[4,208,384]{2,1,0:T(8,128)(2,1)S(1)} custom-call(s32[1]{0:T(128)} %bitcast.refs_0_.s_ref, bf16[192,3072]{1,0:T(8,128)(2,1)S(1)} %modulate.1.refs_1_, bf16[3072,2304]{1,0:T(8,128)(2,1)S(1)} %copy-done, f32[1,128]{1,0:T(1,128)S(1)} %bitcast.16, f32[1,128]{1,0:T(1,128)S(1)} %bitcast.20, bf16[16,384]{1,0:T(8,128)(2,1)S(1)} %pad.7.refs_5_), custom_call_target="tpu_custom_call" | custom-call | tf_op jit(solution)/shard_map/pallas_call | solution.py:161
  16.5 3.5 %shard_map.100.refs_0_ = bf16[4,208,384]{2,1,0:T(8,128)(2,1)S(1)} custom-call(s32[1]{0:T(128)} %bitcast.refs_0_.s_ref, bf16[192,3072]{1,0:T(8,128)(2,1)S(1)} %modulate.1.refs_1_, bf16[3072,2304]{1,0:T(8,128)(2,1)S(1)} %copy-done, f32[1,128]{1,0:T(1,128)S(1)} %bitcast.17, f32[1,128]{1,0:T(1,128)S(1)} %bitcast.21, bf16[16,384]{1,0:T(8,128)(2,1)S(1)} %pad.7.refs_5_), custom_call_target="tpu_custom_call" | custom-call | tf_op jit(solution)/shard_map/pallas_call | solution.py:161
  20.4 12.1 %collective-permute-done.4.refs_1_ = bf16[192,3072]{1,0:T(8,128)(2,1)S(1)} collective-permute-done((bf16[192,3072]{1,0:T(8,128)(2,1)S(1)}, bf16[192,3072]{1,0:T(8,128)(2,1)S(1)}, u32[]{:S(2)}, u32[]{:S(2)}) %collective-permute-start.4) | collective-permute-done | bytes 1179680 | tf_op jit(solution)/shard_map/ppermute | solution.py:94
  32.5 3.6 %shard_map.103 = bf16[4,192,384]{2,1,0:T(8,128)(2,1)S(1)} custom-call(s32[1]{0:T(128)} %bitcast.refs_0_.s_ref, bf16[192,3072]{1,0:T(8,128)(2,1)S(1)} %collective-permute-done.4.refs_1_, bf16[3072,2304]{1,0:T(8,128)(2,1)S(1)} %bitcast.10, f32[1,128]{1,0:T(1,128)S(1)} %bitcast.18, f32[1,128]{1,0:T(1,128)S(1)} %bitcast.22, bf16[16,384]{1,0:T(8,128)(2,1)S(1)} %pad.7.refs_5_), custom_call_target="tpu_custom_call" | custom-call | tf_op jit(solution)/shard_map/pallas_call | solution.py:161
  39.1 5.3 %collective-permute-start.2 = (bf16[2,208,384]{2,1,0:T(8,128)(2,1)S(1)}, bf16[2,208,384]{2,1,0:T(8,128)(2,1)S(1)}, u32[]{:S(2)}, u32[]{:S(2)}) collective-permute-start(bf16[2,208,384]{2,1,0:T(8,128)(2,1)S(1)} %pad_maximum_fusion.2), channel_id=1, source_target_pairs={{0,16},{1,17},{2,18},{7,23},{8,24},{9,25},{10,26},{11,27},{13,29},... | collective-permute-start | bytes 958472 | tf_op jit(solution)/shard_map/ppermute | solution.py:66
  44.5 1.9 %collective-permute-start.3 = (bf16[2,208,384]{2,1,0:T(8,128)(2,1)S(1)}, bf16[2,208,384]{2,1,0:T(8,128)(2,1)S(1)}, u32[]{:S(2)}, u32[]{:S(2)}) collective-permute-start(bf16[2,208,384]{2,1,0:T(8,128)(2,1)S(1)} %pad_maximum_fusion.3), channel_id=1, source_target_pairs={{3,23},{4,16},{5,17},{6,18},{9,29},{11,31},{12,24},{13,25},{14,26}... | collective-permute-start | bytes 958472 | tf_op jit(solution)/shard_map/ppermute | solution.py:66
  46.4 1.7 collective-permute-start.16
  48.1 3.5 %shard_map.102.refs_5_ = bf16[4,192,384]{2,1,0:T(8,128)(2,1)S(1)} custom-call(s32[1]{0:T(128)} %bitcast.refs_0_.s_ref, bf16[192,3072]{1,0:T(8,128)(2,1)S(1)} %collective-permute-done.4.refs_1_, bf16[3072,2304]{1,0:T(8,128)(2,1)S(1)} %bitcast.10, f32[1,128]{1,0:T(1,128)S(1)} %bitcast.19, f32[1,128]{1,0:T(1,128)S(1)} %bitcast.23, bf16[16,384]{1,0:T(8,128)(2,1)S(1)} %pad.7.refs_5_), custom_call_target="tpu_custom_call" | custom-call | tf_op jit(solution)/shard_map/pallas_call | solution.py:161
  53.2 8.2 %collective-permute-start.7 = (bf16[2,192,384]{2,1,0:T(8,128)(2,1)S(1)}, bf16[2,192,384]{2,1,0:T(8,128)(2,1)S(1)}, u32[]{:S(2)}, u32[]{:S(2)}) collective-permute-start(bf16[2,192,384]{2,1,0:T(8,128)(2,1)S(1)} %pad_maximum_fusion.5), channel_id=1, source_target_pairs={{0,16},{1,17},{2,18},{7,23},{8,24},{9,25},{10,26},{11,27},{13,29},... | collective-permute-start | bytes 884744 | tf_op jit(solution)/shard_map/ppermute | solution.py:66
  61.4 2.0 %collective-permute-start.8 = (bf16[2,192,384]{2,1,0:T(8,128)(2,1)S(1)}, bf16[2,192,384]{2,1,0:T(8,128)(2,1)S(1)}, u32[]{:S(2)}, u32[]{:S(2)}) collective-permute-start(bf16[2,192,384]{2,1,0:T(8,128)(2,1)S(1)} %pad_maximum_fusion.6), channel_id=1, source_target_pairs={{3,23},{4,16},{5,17},{6,18},{9,29},{11,31},{12,24},{13,25},{14,26}... | collective-permute-start | bytes 884744 | tf_op jit(solution)/shard_map/ppermute | solution.py:66
  63.4 3.9 %collective-permute-done.7.refs_8_ = bf16[2,192,384]{2,1,0:T(8,128)(2,1)S(1)} collective-permute-done((bf16[2,192,384]{2,1,0:T(8,128)(2,1)S(1)}, bf16[2,192,384]{2,1,0:T(8,128)(2,1)S(1)}, u32[]{:S(2)}, u32[]{:S(2)}) %collective-permute-start.7) | collective-permute-done | bytes 294944 | tf_op jit(solution)/shard_map/ppermute | solution.py:66
  67.3 6.7 %collective-permute-done.8.refs_9_ = bf16[2,192,384]{2,1,0:T(8,128)(2,1)S(1)} collective-permute-done((bf16[2,192,384]{2,1,0:T(8,128)(2,1)S(1)}, bf16[2,192,384]{2,1,0:T(8,128)(2,1)S(1)}, u32[]{:S(2)}, u32[]{:S(2)}) %collective-permute-start.8) | collective-permute-done | bytes 294944 | tf_op jit(solution)/shard_map/ppermute | solution.py:66
  74.6 3.8 %collective-permute-start.9 = (bf16[4,384,256]{2,1,0:T(8,128)(2,1)S(1)}, bf16[4,384,256]{2,1,0:T(8,128)(2,1)S(1)}, u32[]{:S(2)}, u32[]{:S(2)}) collective-permute-start(bf16[4,384,256]{2,1,0:T(8,128)(2,1)S(1)} %get-tuple-element.34), channel_id=1, source_target_pairs={{0,32},{1,33},{2,34},{3,35},{4,36},{5,37},{6,38},{7,39},{8,40},{9,... | collective-permute-start | bytes 2359304 | tf_op jit(solution)/shard_map/ppermute | solution.py:90
  78.5 2.8 %collective-permute-start.10 = (bf16[4,384,256]{2,1,0:T(8,128)(2,1)S(1)}, bf16[4,384,256]{2,1,0:T(8,128)(2,1)S(1)}, u32[]{:S(2)}, u32[]{:S(2)}) collective-permute-start(bf16[4,384,256]{2,1,0:T(8,128)(2,1)S(1)} %get-tuple-element.38), channel_id=1, source_target_pairs={{0,2},{1,7},{2,0},{3,5},{4,6},{5,3},{6,4},{7,1},{8,10},{9,15},{10,... | collective-permute-start | bytes 2359304 | tf_op jit(solution)/shard_map/ppermute | solution.py:90
  81.2 5.2 %collective-permute-start.11 = (bf16[4,384,256]{2,1,0:T(8,128)(2,1)S(1)}, bf16[4,384,256]{2,1,0:T(8,128)(2,1)S(1)}, u32[]{:S(2)}, u32[]{:S(2)}) collective-permute-start(bf16[4,384,256]{2,1,0:T(8,128)(2,1)S(1)} %get-tuple-element.39), channel_id=1, source_target_pairs={{0,8},{1,25},{2,10},{3,27},{4,12},{5,29},{6,14},{7,31},{8,0},{9,17... | collective-permute-start | bytes 2359304 | tf_op jit(solution)/shard_map/ppermute | solution.py:90
  86.4 4.3 %collective-permute-start.12 = (bf16[2,384,256]{2,1,0:T(8,128)(2,1)S(1)}, bf16[2,384,256]{2,1,0:T(8,128)(2,1)S(1)}, u32[]{:S(2)}, u32[]{:S(2)}) collective-permute-start(bf16[2,384,256]{2,1,0:T(8,128)(2,1)S(1)} %get-tuple-element.41), channel_id=1, source_target_pairs={{0,10},{1,31},{2,8},{3,29},{4,14},{5,27},{6,12},{7,25},{8,2},{9,23... | collective-permute-start | bytes 1179656 | tf_op jit(solution)/shard_map/ppermute | solution.py:90
  90.7 15.5 %attend_own.1 = (f32[8,384,128]{2,1,0:T(8,128)S(1)}, f32[8,384,128]{2,1,0:T(8,128)S(1)}, f32[8,384,128]{2,1,0:T(8,128)S(1)}) custom-call(s32[8,128]{1,0:T(8,128)S(1)} %get-tuple-element.28.live_ref.refs_1_, bf16[8,384,128]{2,1,0:T(8,128)(2,1)S(1)} %get-tuple-element.29.q_ref.refs_2_, bf16[8,384,256]{2,1,0:T(8,128)(2,1)S(1)} %get-tuple-element.30.kv_ref), custom_call_target="tpu_custom_call" | custom-call | tf_op jit(solution)/shard_map/attend_own/pallas_call | solution.py:355
  106.3 3.9 %collective-permute-start.13 = (bf16[2,384,256]{2,1,0:T(8,128)(2,1)S(1)}, bf16[2,384,256]{2,1,0:T(8,128)(2,1)S(1)}, u32[]{:S(2)}, u32[]{:S(2)}) collective-permute-start(bf16[2,384,256]{2,1,0:T(8,128)(2,1)S(1)} %pad_maximum_fusion), channel_id=1, source_target_pairs={{0,2},{1,7},{2,0},{3,5},{4,6},{5,3},{6,4},{7,1},{8,10},{9,15},{10,... | collective-permute-start | bytes 1179656 | tf_op jit(solution)/shard_map/ppermute | solution.py:90
  110.3 2.7 %collective-permute-start.14 = (bf16[2,384,256]{2,1,0:T(8,128)(2,1)S(1)}, bf16[2,384,256]{2,1,0:T(8,128)(2,1)S(1)}, u32[]{:S(2)}, u32[]{:S(2)}) collective-permute-start(bf16[2,384,256]{2,1,0:T(8,128)(2,1)S(1)} %stack.34), channel_id=1, source_target_pairs={{0,8},{1,25},{2,10},{3,27},{4,12},{5,29},{6,14},{7,31},{8,0},{9,17... | collective-permute-start | bytes 1179656 | tf_op jit(solution)/shard_map/ppermute | solution.py:90
  113.0 4.5 %collective-permute-start.15 = (bf16[1,384,256]{2,1,0:T(8,128)(2,1)S(1)}, bf16[1,384,256]{2,1,0:T(8,128)(2,1)S(1)}, u32[]{:S(2)}, u32[]{:S(2)}) collective-permute-start(bf16[1,384,256]{2,1,0:T(8,128)(2,1)S(1)} %get-tuple-element.49), channel_id=1, source_target_pairs={{0,10},{1,31},{2,8},{3,29},{4,14},{5,27},{6,12},{7,25},{8,2},{9,23... | collective-permute-start | bytes 589832 | tf_op jit(solution)/shard_map/ppermute | solution.py:90
  117.5 4.0 %collective-permute-done.15.refs_12_ = bf16[1,384,256]{2,1,0:T(8,128)(2,1)S(1)} collective-permute-done((bf16[1,384,256]{2,1,0:T(8,128)(2,1)S(1)}, bf16[1,384,256]{2,1,0:T(8,128)(2,1)S(1)}, u32[]{:S(2)}, u32[]{:S(2)}) %collective-permute-start.15) | collective-permute-done | bytes 196640 | tf_op jit(solution)/shard_map/ppermute | solution.py:90
  121.5 14.5 %shard_map.105 = (bf16[6,192,128]{2,1,0:T(8,128)(2,1)S(1)}, bf16[6,192,128]{2,1,0:T(8,128)(2,1)S(1)}) custom-call(s32[1]{0:T(128)} %bitcast.refs_0_.s_ref, s32[8,128]{1,0:T(8,128)S(1)} %get-tuple-element.28.live_ref.refs_1_, bf16[8,384,128]{2,1,0:T(8,128)(2,1)S(1)} %get-tuple-element.29.q_ref.refs_2_, f32[8,384,128]{2,1,0:T(8,128)S(1)} %get-tuple-element.35.refs_3_, ...), custom_call_target="tpu_custom_call" | custom-call | tf_op jit(solution)/shard_map/pallas_call | solution.py:406
  136.0 1.9 %collective-permute-start.17 = (bf16[6,192,128]{2,1,0:T(8,128)(2,1)S(1)}, bf16[6,192,128]{2,1,0:T(8,128)(2,1)S(1)}, u32[]{:S(2)}, u32[]{:S(2)}) collective-permute-start(bf16[6,192,128]{2,1,0:T(8,128)(2,1)S(1)} %get-tuple-element.46), channel_id=1, source_target_pairs={{0,64},{1,65},{2,66},{3,67},{4,68},{5,69},{6,70},{7,71},{8,72},{9,... | collective-permute-start | bytes 884744 | tf_op jit(solution)/shard_map/ppermute | solution.py:76
  138.0 3.2 %shard_map.104 = (bf16[2,192,128]{2,1,0:T(8,128)(2,1)S(1)}, bf16[2,192,128]{2,1,0:T(8,128)(2,1)S(1)}) custom-call(s32[1]{0:T(128)} %bitcast.refs_0_.s_ref, s32[8,128]{1,0:T(8,128)S(1)} %get-tuple-element.28.live_ref.refs_1_, bf16[8,384,128]{2,1,0:T(8,128)(2,1)S(1)} %get-tuple-element.29.q_ref.refs_2_, f32[8,384,128]{2,1,0:T(8,128)S(1)} %get-tuple-element.35.refs_3_, ...), custom_call_target="tpu_custom_call" | custom-call | tf_op jit(solution)/shard_map/pallas_call | solution.py:406
  141.2 4.9 %collective-permute-start.21 = (bf16[2,192,128]{2,1,0:T(8,128)(2,1)S(1)}, bf16[2,192,128]{2,1,0:T(8,128)(2,1)S(1)}, u32[]{:S(2)}, u32[]{:S(2)}) collective-permute-start(bf16[2,192,128]{2,1,0:T(8,128)(2,1)S(1)} %get-tuple-element.47), channel_id=1, source_target_pairs={{0,64},{1,65},{2,66},{3,67},{4,68},{5,69},{6,70},{7,71},{8,72},{9,... | collective-permute-start | bytes 294920 | tf_op jit(solution)/shard_map/ppermute | solution.py:76
  148.3 6.3 %collective-permute-start.19 = (bf16[4,192,128]{2,1,0:T(8,128)(2,1)S(1)}, bf16[4,192,128]{2,1,0:T(8,128)(2,1)S(1)}, u32[]{:S(2)}, u32[]{:S(2)}) collective-permute-start(bf16[4,192,128]{2,1,0:T(8,128)(2,1)S(1)} %pad_maximum_fusion.8), channel_id=1, source_target_pairs={{0,16},{1,17},{2,18},{3,19},{4,20},{5,21},{6,22},{7,23},{8,24},{9,... | collective-permute-start | bytes 589832 | tf_op jit(solution)/shard_map/ppermute | solution.py:71
  154.6 4.0 %collective-permute-start.20 = (bf16[4,192,128]{2,1,0:T(8,128)(2,1)S(1)}, bf16[4,192,128]{2,1,0:T(8,128)(2,1)S(1)}, u32[]{:S(2)}, u32[]{:S(2)}) collective-permute-start(bf16[4,192,128]{2,1,0:T(8,128)(2,1)S(1)} %pad_maximum_fusion.9), channel_id=1, source_target_pairs={{0,20},{1,21},{2,22},{3,23},{4,16},{5,17},{6,18},{7,19},{8,28},{9,... | collective-permute-start | bytes 589832 | tf_op jit(solution)/shard_map/ppermute | solution.py:71
  158.8 7.1 %collective-permute-done.20 = bf16[4,192,128]{2,1,0:T(8,128)(2,1)S(1)} collective-permute-done((bf16[4,192,128]{2,1,0:T(8,128)(2,1)S(1)}, bf16[4,192,128]{2,1,0:T(8,128)(2,1)S(1)}, u32[]{:S(2)}, u32[]{:S(2)}) %collective-permute-start.20) | collective-permute-done | bytes 196640 | tf_op jit(solution)/shard_map/ppermute | solution.py:71
  166.0 1.9 %collective-permute-start.22 = (bf16[8,192,128]{2,1,0:T(8,128)(2,1)S(1)}, bf16[8,192,128]{2,1,0:T(8,128)(2,1)S(1)}, u32[]{:S(2)}, u32[]{:S(2)}) collective-permute-start(bf16[8,192,128]{2,1,0:T(8,128)(2,1)S(1)} %slice_dynamic-update-slice_fusion), channel_id=1, source_target_pairs={{0,1},{1,0},{2,3},{3,2},{4,5},{5,4},{6,7},{7,6},{8,9},{9,8},{10,11... | collective-permute-start | bytes 1179656 | tf_op jit(solution)/shard_map/ppermute | solution.py:85
  169.3 4.4 %output.1 = bf16[192,3072]{1,0:T(8,128)(2,1)} custom-call(s32[1]{0:T(128)} %bitcast.refs_0_.s_ref, bf16[2,192,128]{2,1,0:T(8,128)(2,1)S(1)} %get-tuple-element.44.refs_0_, bf16[2,192,128]{2,1,0:T(8,128)(2,1)S(1)} %get-tuple-element.74.refs_1_, bf16[2,192,128]{2,1,0:T(8,128)(2,1)S(1)} %get-tuple-element.72.refs_2_, ...), custom_call_target="tpu_custom_call" | custom-call | tf_op jit(solution)/shard_map/output/pallas_call | solution.py:462
  (91 shorter events, 14.3 us)
Async XLA Ops:
  0.0 6.8 %copy-start.6 = (f32[128]{0:T(128)S(1)}, f32[128]{0:T(128)}, u32[]{:S(2)}) copy-start(f32[128]{0:T(128)} %param.13) | copy-start | bytes 1540
  4.0 28.4 %collective-permute-start.4 = (bf16[192,3072]{1,0:T(8,128)(2,1)S(1)}, bf16[192,3072]{1,0:T(8,128)(2,1)S(1)}, u32[]{:S(2)}, u32[]{:S(2)}) collective-permute-start(bf16[192,3072]{1,0:T(8,128)(2,1)S(1)} %modulate.1.refs_1_), channel_id=1, source_target_pairs={{0,64},{64,0},{1,65},{65,1},{2,66},{66,2},{3,67},{67,3},{4,68},{68... | collective-permute-start | bytes 3538952 | tf_op jit(solution)/shard_map/ppermute | solution.py:94
  11.9 8.2 %slice-start.4 = ((s8[4718592]{0:T(1024)(128)(4,1)}), s8[4194304]{0:T(1024)(128)(4,1)S(1)}, s32[]{:S(2)}) async-start(s8[4718592]{0:T(1024)(128)(4,1)} %bitcast.11), calls=%async_computation.4 | async-start | bytes 8388608
  11.9 20.6 %slice-start = ((s8[14155776]{0:T(1024)(128)(4,1)}), s8[4194304]{0:T(1024)(128)(4,1)S(1)}, s32[]{:S(2)}) async-start(s8[14155776]{0:T(1024)(128)(4,1)} %bitcast.9), calls=%async_computation | async-start | bytes 8388608
  11.9 20.6 %slice-start.1 = ((s8[14155776]{0:T(1024)(128)(4,1)}), s8[4194304]{0:T(1024)(128)(4,1)S(1)}, s32[]{:S(2)}) async-start(s8[14155776]{0:T(1024)(128)(4,1)} %bitcast.9), calls=%async_computation.1 | async-start | bytes 8388608
  15.5 17.0 %slice-start.2 = ((s8[14155776]{0:T(1024)(128)(4,1)}), s8[4194304]{0:T(1024)(128)(4,1)S(1)}, s32[]{:S(2)}) async-start(s8[14155776]{0:T(1024)(128)(4,1)} %bitcast.9), calls=%async_computation.2 | async-start | bytes 8388608
  15.5 17.0 %slice-start.3 = ((s8[14155776]{0:T(1024)(128)(4,1)}), s8[1572864]{0:T(1024)(128)(4,1)S(1)}, s32[]{:S(2)}) async-start(s8[14155776]{0:T(1024)(128)(4,1)} %bitcast.9), calls=%async_computation.3 | async-start | bytes 3145728
  15.5 4.9 %collective-permute-start = (bf16[4,208,384]{2,1,0:T(8,128)(2,1)S(1)}, bf16[4,208,384]{2,1,0:T(8,128)(2,1)S(1)}, u32[]{:S(2)}, u32[]{:S(2)}) collective-permute-start(bf16[4,208,384]{2,1,0:T(8,128)(2,1)S(1)} %shard_map.101), channel_id=1, source_target_pairs={{0,1},{1,0},{2,3},{3,2},{4,5},{5,4},{6,7},{7,6},{8,9},{9,8},{10,11... | collective-permute-start | bytes 1916936 | tf_op jit(solution)/shard_map/ppermute | solution.py:85
  36.1 15.6 %collective-permute-start.5 = (bf16[4,192,384]{2,1,0:T(8,128)(2,1)S(1)}, bf16[4,192,384]{2,1,0:T(8,128)(2,1)S(1)}, u32[]{:S(2)}, u32[]{:S(2)}) collective-permute-start(bf16[4,192,384]{2,1,0:T(8,128)(2,1)S(1)} %shard_map.103), channel_id=1, source_target_pairs={{0,1},{1,0},{2,3},{3,2},{4,5},{5,4},{6,7},{7,6},{8,9},{9,8},{10,11... | collective-permute-start | bytes 1769480 | tf_op jit(solution)/shard_map/ppermute | solution.py:85
  37.7 15.5 %collective-permute-start.1 = (bf16[2,208,384]{2,1,0:T(8,128)(2,1)S(1)}, bf16[2,208,384]{2,1,0:T(8,128)(2,1)S(1)}, u32[]{:S(2)}, u32[]{:S(2)}) collective-permute-start(bf16[2,208,384]{2,1,0:T(8,128)(2,1)S(1)} %pad_maximum_fusion.1), channel_id=1, source_target_pairs={{0,4},{1,5},{2,6},{3,7},{4,0},{5,1},{6,2},{7,3},{8,12},{10,14},{11... | collective-permute-start | bytes 958472 | tf_op jit(solution)/shard_map/ppermute | solution.py:66
  39.1 22.3 %collective-permute-start.2 = (bf16[2,208,384]{2,1,0:T(8,128)(2,1)S(1)}, bf16[2,208,384]{2,1,0:T(8,128)(2,1)S(1)}, u32[]{:S(2)}, u32[]{:S(2)}) collective-permute-start(bf16[2,208,384]{2,1,0:T(8,128)(2,1)S(1)} %pad_maximum_fusion.2), channel_id=1, source_target_pairs={{0,16},{1,17},{2,18},{7,23},{8,24},{9,25},{10,26},{11,27},{13,29},... | collective-permute-start | bytes 958472 | tf_op jit(solution)/shard_map/ppermute | solution.py:66
  44.5 18.9 %collective-permute-start.3 = (bf16[2,208,384]{2,1,0:T(8,128)(2,1)S(1)}, bf16[2,208,384]{2,1,0:T(8,128)(2,1)S(1)}, u32[]{:S(2)}, u32[]{:S(2)}) collective-permute-start(bf16[2,208,384]{2,1,0:T(8,128)(2,1)S(1)} %pad_maximum_fusion.3), channel_id=1, source_target_pairs={{3,23},{4,16},{5,17},{6,18},{9,29},{11,31},{12,24},{13,25},{14,26}... | collective-permute-start | bytes 958472 | tf_op jit(solution)/shard_map/ppermute | solution.py:66
  46.4 99.7 %collective-permute-start.16 = (bf16[384,3072]{1,0:T(8,128)(2,1)S(1)}, bf16[384,3072]{1,0:T(8,128)(2,1)S(1)}, u32[]{:S(2)}, u32[]{:S(2)}) collective-permute-start(bf16[384,3072]{1,0:T(8,128)(2,1)S(1)} %weight_part.1), channel_id=1, source_target_pairs={{0,96},{1,97},{2,98},{3,99},{4,100},{5,101},{6,102},{7,103},{8,104... | collective-permute-start | bytes 7077896 | tf_op jit(solution)/shard_map/ppermute | solution.py:81
  51.6 22.4 %copy-start.2 = (s32[8,8,128]{2,1,0:T(8,128)S(1)}, s32[8,8,128]{2,1,0:T(8,128)}, u32[]{:S(2)}) copy-start(s32[8,8,128]{2,1,0:T(8,128)} %constant.9.clone.refs_10_) | copy-start | bytes 98308
  51.8 11.6 %collective-permute-start.6 = (bf16[2,192,384]{2,1,0:T(8,128)(2,1)S(1)}, bf16[2,192,384]{2,1,0:T(8,128)(2,1)S(1)}, u32[]{:S(2)}, u32[]{:S(2)}) collective-permute-start(bf16[2,192,384]{2,1,0:T(8,128)(2,1)S(1)} %pad_maximum_fusion.4), channel_id=1, source_target_pairs={{0,4},{1,5},{2,6},{3,7},{4,0},{5,1},{6,2},{7,3},{8,12},{10,14},{11... | collective-permute-start | bytes 884744 | tf_op jit(solution)/shard_map/ppermute | solution.py:66
  53.2 14.1 %collective-permute-start.7 = (bf16[2,192,384]{2,1,0:T(8,128)(2,1)S(1)}, bf16[2,192,384]{2,1,0:T(8,128)(2,1)S(1)}, u32[]{:S(2)}, u32[]{:S(2)}) collective-permute-start(bf16[2,192,384]{2,1,0:T(8,128)(2,1)S(1)} %pad_maximum_fusion.5), channel_id=1, source_target_pairs={{0,16},{1,17},{2,18},{7,23},{8,24},{9,25},{10,26},{11,27},{13,29},... | collective-permute-start | bytes 884744 | tf_op jit(solution)/shard_map/ppermute | solution.py:66
  61.4 12.7 %collective-permute-start.8 = (bf16[2,192,384]{2,1,0:T(8,128)(2,1)S(1)}, bf16[2,192,384]{2,1,0:T(8,128)(2,1)S(1)}, u32[]{:S(2)}, u32[]{:S(2)}) collective-permute-start(bf16[2,192,384]{2,1,0:T(8,128)(2,1)S(1)} %pad_maximum_fusion.6), channel_id=1, source_target_pairs={{3,23},{4,16},{5,17},{6,18},{9,29},{11,31},{12,24},{13,25},{14,26}... | collective-permute-start | bytes 884744 | tf_op jit(solution)/shard_map/ppermute | solution.py:66
  74.6 31.6 %collective-permute-start.9 = (bf16[4,384,256]{2,1,0:T(8,128)(2,1)S(1)}, bf16[4,384,256]{2,1,0:T(8,128)(2,1)S(1)}, u32[]{:S(2)}, u32[]{:S(2)}) collective-permute-start(bf16[4,384,256]{2,1,0:T(8,128)(2,1)S(1)} %get-tuple-element.34), channel_id=1, source_target_pairs={{0,32},{1,33},{2,34},{3,35},{4,36},{5,37},{6,38},{7,39},{8,40},{9,... | collective-permute-start | bytes 2359304 | tf_op jit(solution)/shard_map/ppermute | solution.py:90
  78.5 34.5 %collective-permute-start.10 = (bf16[4,384,256]{2,1,0:T(8,128)(2,1)S(1)}, bf16[4,384,256]{2,1,0:T(8,128)(2,1)S(1)}, u32[]{:S(2)}, u32[]{:S(2)}) collective-permute-start(bf16[4,384,256]{2,1,0:T(8,128)(2,1)S(1)} %get-tuple-element.38), channel_id=1, source_target_pairs={{0,2},{1,7},{2,0},{3,5},{4,6},{5,3},{6,4},{7,1},{8,10},{9,15},{10,... | collective-permute-start | bytes 2359304 | tf_op jit(solution)/shard_map/ppermute | solution.py:90
  81.2 36.3 %collective-permute-start.11 = (bf16[4,384,256]{2,1,0:T(8,128)(2,1)S(1)}, bf16[4,384,256]{2,1,0:T(8,128)(2,1)S(1)}, u32[]{:S(2)}, u32[]{:S(2)}) collective-permute-start(bf16[4,384,256]{2,1,0:T(8,128)(2,1)S(1)} %get-tuple-element.39), channel_id=1, source_target_pairs={{0,8},{1,25},{2,10},{3,27},{4,12},{5,29},{6,14},{7,31},{8,0},{9,17... | collective-permute-start | bytes 2359304 | tf_op jit(solution)/shard_map/ppermute | solution.py:90
  86.4 23.9 %collective-permute-start.12 = (bf16[2,384,256]{2,1,0:T(8,128)(2,1)S(1)}, bf16[2,384,256]{2,1,0:T(8,128)(2,1)S(1)}, u32[]{:S(2)}, u32[]{:S(2)}) collective-permute-start(bf16[2,384,256]{2,1,0:T(8,128)(2,1)S(1)} %get-tuple-element.41), channel_id=1, source_target_pairs={{0,10},{1,31},{2,8},{3,29},{4,14},{5,27},{6,12},{7,25},{8,2},{9,23... | collective-permute-start | bytes 1179656 | tf_op jit(solution)/shard_map/ppermute | solution.py:90
  106.3 15.2 %collective-permute-start.13 = (bf16[2,384,256]{2,1,0:T(8,128)(2,1)S(1)}, bf16[2,384,256]{2,1,0:T(8,128)(2,1)S(1)}, u32[]{:S(2)}, u32[]{:S(2)}) collective-permute-start(bf16[2,384,256]{2,1,0:T(8,128)(2,1)S(1)} %pad_maximum_fusion), channel_id=1, source_target_pairs={{0,2},{1,7},{2,0},{3,5},{4,6},{5,3},{6,4},{7,1},{8,10},{9,15},{10,... | collective-permute-start | bytes 1179656 | tf_op jit(solution)/shard_map/ppermute | solution.py:90
  110.3 11.2 %collective-permute-start.14 = (bf16[2,384,256]{2,1,0:T(8,128)(2,1)S(1)}, bf16[2,384,256]{2,1,0:T(8,128)(2,1)S(1)}, u32[]{:S(2)}, u32[]{:S(2)}) collective-permute-start(bf16[2,384,256]{2,1,0:T(8,128)(2,1)S(1)} %stack.34), channel_id=1, source_target_pairs={{0,8},{1,25},{2,10},{3,27},{4,12},{5,29},{6,14},{7,31},{8,0},{9,17... | collective-permute-start | bytes 1179656 | tf_op jit(solution)/shard_map/ppermute | solution.py:90
  113.0 8.5 %collective-permute-start.15 = (bf16[1,384,256]{2,1,0:T(8,128)(2,1)S(1)}, bf16[1,384,256]{2,1,0:T(8,128)(2,1)S(1)}, u32[]{:S(2)}, u32[]{:S(2)}) collective-permute-start(bf16[1,384,256]{2,1,0:T(8,128)(2,1)S(1)} %get-tuple-element.49), channel_id=1, source_target_pairs={{0,10},{1,31},{2,8},{3,29},{4,14},{5,27},{6,12},{7,25},{8,2},{9,23... | collective-permute-start | bytes 589832 | tf_op jit(solution)/shard_map/ppermute | solution.py:90
  136.0 10.9 %collective-permute-start.17 = (bf16[6,192,128]{2,1,0:T(8,128)(2,1)S(1)}, bf16[6,192,128]{2,1,0:T(8,128)(2,1)S(1)}, u32[]{:S(2)}, u32[]{:S(2)}) collective-permute-start(bf16[6,192,128]{2,1,0:T(8,128)(2,1)S(1)} %get-tuple-element.46), channel_id=1, source_target_pairs={{0,64},{1,65},{2,66},{3,67},{4,68},{5,69},{6,70},{7,71},{8,72},{9,... | collective-permute-start | bytes 884744 | tf_op jit(solution)/shard_map/ppermute | solution.py:76
  141.2 24.8 %collective-permute-start.21 = (bf16[2,192,128]{2,1,0:T(8,128)(2,1)S(1)}, bf16[2,192,128]{2,1,0:T(8,128)(2,1)S(1)}, u32[]{:S(2)}, u32[]{:S(2)}) collective-permute-start(bf16[2,192,128]{2,1,0:T(8,128)(2,1)S(1)} %get-tuple-element.47), channel_id=1, source_target_pairs={{0,64},{1,65},{2,66},{3,67},{4,68},{5,69},{6,70},{7,71},{8,72},{9,... | collective-permute-start | bytes 294920 | tf_op jit(solution)/shard_map/ppermute | solution.py:76
  146.9 22.3 %copy-start.5 = (f32[3072]{0:T(1024)S(1)}, f32[3072]{0:T(1024)}, u32[]{:S(2)}) copy-start(f32[3072]{0:T(1024)} %param.17) | copy-start | bytes 36868
  147.0 11.7 %collective-permute-start.18 = (bf16[4,192,128]{2,1,0:T(8,128)(2,1)S(1)}, bf16[4,192,128]{2,1,0:T(8,128)(2,1)S(1)}, u32[]{:S(2)}, u32[]{:S(2)}) collective-permute-start(bf16[4,192,128]{2,1,0:T(8,128)(2,1)S(1)} %pad_maximum_fusion.7), channel_id=1, source_target_pairs={{0,4},{1,5},{2,6},{3,7},{4,0},{5,1},{6,2},{7,3},{8,12},{9,13},{10,... | collective-permute-start | bytes 589832 | tf_op jit(solution)/shard_map/ppermute | solution.py:71
  148.3 10.4 %collective-permute-start.19 = (bf16[4,192,128]{2,1,0:T(8,128)(2,1)S(1)}, bf16[4,192,128]{2,1,0:T(8,128)(2,1)S(1)}, u32[]{:S(2)}, u32[]{:S(2)}) collective-permute-start(bf16[4,192,128]{2,1,0:T(8,128)(2,1)S(1)} %pad_maximum_fusion.8), channel_id=1, source_target_pairs={{0,16},{1,17},{2,18},{3,19},{4,20},{5,21},{6,22},{7,23},{8,24},{9,... | collective-permute-start | bytes 589832 | tf_op jit(solution)/shard_map/ppermute | solution.py:71
  154.6 11.3 %collective-permute-start.20 = (bf16[4,192,128]{2,1,0:T(8,128)(2,1)S(1)}, bf16[4,192,128]{2,1,0:T(8,128)(2,1)S(1)}, u32[]{:S(2)}, u32[]{:S(2)}) collective-permute-start(bf16[4,192,128]{2,1,0:T(8,128)(2,1)S(1)} %pad_maximum_fusion.9), channel_id=1, source_target_pairs={{0,20},{1,21},{2,22},{3,23},{4,16},{5,17},{6,18},{7,19},{8,28},{9,... | collective-permute-start | bytes 589832 | tf_op jit(solution)/shard_map/ppermute | solution.py:71
  158.6 10.7 %collective-permute-start.23 = (bf16[384,3072]{1,0:T(8,128)(2,1)S(1)}, bf16[384,3072]{1,0:T(8,128)(2,1)S(1)}, u32[]{:S(2)}, u32[]{:S(2)}) collective-permute-start(bf16[384,3072]{1,0:T(8,128)(2,1)S(1)} %collective-permute-done.16.refs_10_), channel_id=1, source_target_pairs={{0,1},{1,0},{2,3},{3,2},{4,5},{5,4},{6,7},{7,6},{8,9},{9,8},{10,11... | collective-permute-start | bytes 7077896 | tf_op jit(solution)/shard_map/ppermute | solution.py:85
  166.0 3.3 %collective-permute-start.22 = (bf16[8,192,128]{2,1,0:T(8,128)(2,1)S(1)}, bf16[8,192,128]{2,1,0:T(8,128)(2,1)S(1)}, u32[]{:S(2)}, u32[]{:S(2)}) collective-permute-start(bf16[8,192,128]{2,1,0:T(8,128)(2,1)S(1)} %slice_dynamic-update-slice_fusion), channel_id=1, source_target_pairs={{0,1},{1,0},{2,3},{3,2},{4,5},{5,4},{6,7},{7,6},{8,9},{9,8},{10,11... | collective-permute-start | bytes 1179656 | tf_op jit(solution)/shard_map/ppermute | solution.py:85
  (7 other events, 26.0 us)

commit v3 on v2

--- a/solution.py
+++ b/solution.py
@@ -16,9 +16,9 @@
     ((0, 0, 1), (0, 2, 4, 6)),
     ((0, 1, 0), (0, 1, 4, 5)),
     ((1, 0, 0), (0, 1, 2, 3)),
-    ((0, 1, 1), (0, 4)),
     ((1, 0, 1), (0, 2)),
     ((1, 1, 0), (0, 1)),
+    ((0, 1, 1), (0, 4)),
     ((1, 1, 1), (0,)),
 )
 OWN_AT = [((u >> 2) & 1, (u >> 1) & 1, u & 1) for u in range(8)]
@@ -253,7 +253,7 @@
         ((8, TILE, HD), jnp.bfloat16),
         ((8, TILE, 2 * HD), jnp.bfloat16),
         ((8, HD), jnp.int32),
-    ] + [((len(us), TILE, 2 * HD), jnp.bfloat16) for _, us in HALO[:4]]
+    ] + [((len(us), TILE, 2 * HD), jnp.bfloat16) for _, us in HALO[:3]]
     in_specs = []
     for keep, *_ in halves:
         rows = keep.shape[1]
@@ -336,8 +336,9 @@
     each(weigh)
 
 
-def own_kernel(live_ref, q_ref, kv_ref, m_ref, l_ref, acc_ref, s_ref, list_ref):
-    u = pl.program_id(0)
+def own_kernel(first, live_ref, q_ref, kv_ref, *refs):
+    u = first + pl.program_id(0)
+    m_ref, l_ref, acc_ref, s_ref, list_ref = refs[-5:]
     m, l, acc = m_ref.at[0], l_ref.at[0], acc_ref.at[0]
     m[...] = jnp.full_like(m[...], NEG)
 
@@ -349,26 +350,27 @@
     attend(u, 0, 8, live_ref, q_ref[0], kv_ref, s_ref, list_ref, m, l, acc, rescale)
 
 
-def attend_own(live, q, kv):
-    per_u = pl.BlockSpec((1, TILE, HD), lambda u, *_: (u, 0, 0))
+def attend_own(live, q, kv, first, tiles, prior):
+    per_u = pl.BlockSpec((1, TILE, HD), lambda u, *_: (first + u, 0, 0))
     state = jax.ShapeDtypeStruct((8, TILE, HD), jnp.float32)
     return pl.pallas_call(
-        own_kernel,
+        lambda *refs: own_kernel(first, *refs),
         out_shape=[state, state, state],
         grid_spec=pltpu.PrefetchScalarGridSpec(
             num_scalar_prefetch=1,
-            grid=(8,),
-            in_specs=[per_u, whole((8, TILE, 2 * HD))],
+            grid=(tiles,),
+            in_specs=[per_u, whole((8, TILE, 2 * HD))]
+            + [pl.BlockSpec(memory_space=pl.ANY)] * len(prior),
             out_specs=[per_u] * 3,
             scratch_shapes=[pltpu.VMEM((8, TILE, TILE), jnp.float32), pltpu.SMEM((9,), jnp.int32)],
         ),
+        input_output_aliases={3 + i: i for i in range(len(prior))},
         compiler_params=pltpu.CompilerParams(vmem_limit_bytes=14 << 20),
-        name="attend_own",
-    )(live, q, kv)
+    )(live, q, kv, *prior)
 
 
 def halo_kernel(first, s_ref, live_ref, q_ref, m_in, l_in, acc_in, *refs):
-    pieces, (near_ref, far_ref, kv_ref, score_ref, m_ref, l_ref, acc_ref, list_ref, sems) = refs[:7], refs[7:]
+    pieces, (near_ref, far_ref, kv_ref, score_ref, m_ref, l_ref, acc_ref, list_ref, sems) = refs[:6], refs[6:]
 
     @pl.when(pl.program_id(0) == 0)
     def _():
@@ -457,7 +459,7 @@
 def output(slab_at, same, cross, core, weight, weight_c, weight_d, gate):
     inner, width = weight.shape
     half = TILE // 2
-    cols = 1024
+    cols = 512
     by_col = lambda rows: pl.BlockSpec((rows, cols), lambda n, s_ref: (0, n))
     return pl.pallas_call(
         output_kernel,
@@ -516,12 +518,14 @@
     halo = []
     for piece, (moved, _) in zip(sends, HALO):
         halo.append(to_block(piece, moved))
-    halo += [None] * 3
-    state = attend_own(live, q, kv)
-    *state, over = lax.optimization_barrier((*state, halo[2]))
-    halo[2] = over
-    for at, moved, us in ((4, (0, 0, 1), (0, 2)), (5, (0, 1, 0), (0, 1)), (6, (0, 1, 1), (0,))):
-        halo[at] = to_block(jnp.stack([over[u] for u in us]), moved)
+    state = attend_own(live, q, kv, 0, 4, ())
+    *state, side, over = lax.optimization_barrier((*state, halo[0], halo[2]))
+    halo = [side, halo[1], over]
+    for moved, tiles in (
+        ((0, 0, 1), (over[0], over[2])), ((0, 1, 0), (over[0], over[1], side[0], side[2])), ((0, 1, 1), (over[0],))
+    ):
+        halo.append(to_block(jnp.stack(tiles), moved))
+    state = attend_own(live, q, kv, 4, 4, state)
     done = {}
     for first, tiles in ((2, 6), (0, 2)):
         mixed, crossing = attend_halo(slab_at, live, q, state, halo, first, tiles)

time: 174 us -> 180 us (1.034)
  the two profiles are of different devices: /device:TPU:49 before, /device:TPU:17 now
where the time goes in v3:
time: 180 us; the launch traced here: 179 us
  starting transfers between devices  71.8 us (40%)
  Pallas kernels  55.7 us (31%)
  waiting for transfers between devices  42.6 us (24%)
  local copies, waits for them, and re-layouts  8.25 us (5%)
    ppermute x6, starting transfers between devices, to_block(): return lax.ppermute(value, 'slab', pairs)  22.7 us
    ppermute x6, starting transfers between devices, to_chip(): return lax.ppermute(value, 'slab', pairs)  19.9 us
    pallas_call x2, Pallas kernels, attend_halo(): pl.pallas_call(lambda *refs: halo_kernel(first, *refs), out_shape=[jax.Sh...  17.9 us
    pallas_call x2, Pallas kernels, attend_own(): pl.pallas_call(lambda *refs: own_kernel(first, *refs), out_shape=[state,...  16.6 us
    pallas_call x4, Pallas kernels, project(): pl.pallas_call(lambda *refs: project_kernel(other, *refs), out_shape=jax....  14.2 us
    ppermute x1, waiting for transfers between devices, to_group(): return lax.ppermute(value, 'heads', [(0, 1), (1, 0)])  12.1 us
    ppermute x6, waiting for transfers between devices, to_chip(): return lax.ppermute(value, 'slab', pairs)  10.7 us
    ppermute x3, starting transfers between devices, from_chip(): return lax.ppermute(value, 'slab', pairs)  9.99 us
  transfers between devices with their start and end apart: 23, of which 8 were waited for; matrix products, arithmetic and copies ran while one was open for 0% of the time, Pallas kernels for 26%

profile of v3, /device:TPU:17, one launch (start us, length us, event | category | flops | bytes accessed | tf_op | source)
XLA Modules:
  0.0 179.4 jit_solution(12850852329666049688)
XLA Ops:
  4.0 3.7 %collective-permute-start.4 = (bf16[192,3072]{1,0:T(8,128)(2,1)S(1)}, bf16[192,3072]{1,0:T(8,128)(2,1)S(1)}, u32[]{:S(2)}, u32[]{:S(2)}) collective-permute-start(bf16[192,3072]{1,0:T(8,128)(2,1)S(1)} %modulate.1.refs_1_), channel_id=1, source_target_pairs={{0,64},{64,0},{1,65},{65,1},{2,66},{66,2},{3,67},{67,3},{4,68},{68... | collective-permute-start | bytes 3538952 | tf_op jit(solution)/shard_map/ppermute | solution.py:94
  7.8 5.0 %copy-done = bf16[3072,2304]{1,0:T(8,128)(2,1)S(1)} copy-done((bf16[3072,2304]{1,0:T(8,128)(2,1)S(1)}, bf16[3072,2304]{1,0:T(8,128)(2,1)}, u32[]{:S(2)}) %copy-start) | copy-done | bytes 14155800
  12.8 3.6 %shard_map.101 = bf16[4,208,384]{2,1,0:T(8,128)(2,1)S(1)} custom-call(s32[1]{0:T(128)} %bitcast.refs_0_.s_ref, bf16[192,3072]{1,0:T(8,128)(2,1)S(1)} %modulate.1.refs_1_, bf16[3072,2304]{1,0:T(8,128)(2,1)S(1)} %copy-done, f32[1,128]{1,0:T(1,128)S(1)} %bitcast.16, f32[1,128]{1,0:T(1,128)S(1)} %bitcast.20, bf16[16,384]{1,0:T(8,128)(2,1)S(1)} %pad.7.refs_5_), custom_call_target="tpu_custom_call" | custom-call | tf_op jit(solution)/shard_map/pallas_call | solution.py:161
  17.4 3.5 %shard_map.100.refs_0_ = bf16[4,208,384]{2,1,0:T(8,128)(2,1)S(1)} custom-call(s32[1]{0:T(128)} %bitcast.refs_0_.s_ref, bf16[192,3072]{1,0:T(8,128)(2,1)S(1)} %modulate.1.refs_1_, bf16[3072,2304]{1,0:T(8,128)(2,1)S(1)} %copy-done, f32[1,128]{1,0:T(1,128)S(1)} %bitcast.17, f32[1,128]{1,0:T(1,128)S(1)} %bitcast.21, bf16[16,384]{1,0:T(8,128)(2,1)S(1)} %pad.7.refs_5_), custom_call_target="tpu_custom_call" | custom-call | tf_op jit(solution)/shard_map/pallas_call | solution.py:161
  21.3 12.1 %collective-permute-done.4.refs_1_ = bf16[192,3072]{1,0:T(8,128)(2,1)S(1)} collective-permute-done((bf16[192,3072]{1,0:T(8,128)(2,1)S(1)}, bf16[192,3072]{1,0:T(8,128)(2,1)S(1)}, u32[]{:S(2)}, u32[]{:S(2)}) %collective-permute-start.4) | collective-permute-done | bytes 1179680 | tf_op jit(solution)/shard_map/ppermute | solution.py:94
  33.4 3.6 %shard_map.103 = bf16[4,192,384]{2,1,0:T(8,128)(2,1)S(1)} custom-call(s32[1]{0:T(128)} %bitcast.refs_0_.s_ref, bf16[192,3072]{1,0:T(8,128)(2,1)S(1)} %collective-permute-done.4.refs_1_, bf16[3072,2304]{1,0:T(8,128)(2,1)S(1)} %bitcast.10, f32[1,128]{1,0:T(1,128)S(1)} %bitcast.18, f32[1,128]{1,0:T(1,128)S(1)} %bitcast.22, bf16[16,384]{1,0:T(8,128)(2,1)S(1)} %pad.7.refs_5_), custom_call_target="tpu_custom_call" | custom-call | tf_op jit(solution)/shard_map/pallas_call | solution.py:161
  39.7 5.3 %collective-permute-start.2 = (bf16[2,208,384]{2,1,0:T(8,128)(2,1)S(1)}, bf16[2,208,384]{2,1,0:T(8,128)(2,1)S(1)}, u32[]{:S(2)}, u32[]{:S(2)}) collective-permute-start(bf16[2,208,384]{2,1,0:T(8,128)(2,1)S(1)} %pad_maximum_fusion.3), channel_id=1, source_target_pairs={{0,16},{1,17},{2,18},{7,23},{8,24},{9,25},{10,26},{11,27},{13,29},... | collective-permute-start | bytes 958472 | tf_op jit(solution)/shard_map/ppermute | solution.py:66
  45.1 1.9 %collective-permute-start.3 = (bf16[2,208,384]{2,1,0:T(8,128)(2,1)S(1)}, bf16[2,208,384]{2,1,0:T(8,128)(2,1)S(1)}, u32[]{:S(2)}, u32[]{:S(2)}) collective-permute-start(bf16[2,208,384]{2,1,0:T(8,128)(2,1)S(1)} %pad_maximum_fusion.4), channel_id=1, source_target_pairs={{3,23},{4,16},{5,17},{6,18},{9,29},{11,31},{12,24},{13,25},{14,26}... | collective-permute-start | bytes 958472 | tf_op jit(solution)/shard_map/ppermute | solution.py:66
  47.0 3.2 %collective-permute-start.15 = (bf16[384,3072]{1,0:T(8,128)(2,1)S(1)}, bf16[384,3072]{1,0:T(8,128)(2,1)S(1)}, u32[]{:S(2)}, u32[]{:S(2)}) collective-permute-start(bf16[384,3072]{1,0:T(8,128)(2,1)S(1)} %weight_part.1), channel_id=1, source_target_pairs={{0,96},{1,97},{2,98},{3,99},{4,100},{5,101},{6,102},{7,103},{8,104... | collective-permute-start | bytes 7077896 | tf_op jit(solution)/shard_map/ppermute | solution.py:81
  50.2 3.5 %shard_map.102.refs_5_ = bf16[4,192,384]{2,1,0:T(8,128)(2,1)S(1)} custom-call(s32[1]{0:T(128)} %bitcast.refs_0_.s_ref, bf16[192,3072]{1,0:T(8,128)(2,1)S(1)} %collective-permute-done.4.refs_1_, bf16[3072,2304]{1,0:T(8,128)(2,1)S(1)} %bitcast.10, f32[1,128]{1,0:T(1,128)S(1)} %bitcast.19, f32[1,128]{1,0:T(1,128)S(1)} %bitcast.23, bf16[16,384]{1,0:T(8,128)(2,1)S(1)} %pad.7.refs_5_), custom_call_target="tpu_custom_call" | custom-call | tf_op jit(solution)/shard_map/pallas_call | solution.py:161
  55.3 8.2 %collective-permute-start.7 = (bf16[2,192,384]{2,1,0:T(8,128)(2,1)S(1)}, bf16[2,192,384]{2,1,0:T(8,128)(2,1)S(1)}, u32[]{:S(2)}, u32[]{:S(2)}) collective-permute-start(bf16[2,192,384]{2,1,0:T(8,128)(2,1)S(1)} %pad_maximum_fusion.6), channel_id=1, source_target_pairs={{0,16},{1,17},{2,18},{7,23},{8,24},{9,25},{10,26},{11,27},{13,29},... | collective-permute-start | bytes 884744 | tf_op jit(solution)/shard_map/ppermute | solution.py:66
  63.5 1.9 %collective-permute-start.8 = (bf16[2,192,384]{2,1,0:T(8,128)(2,1)S(1)}, bf16[2,192,384]{2,1,0:T(8,128)(2,1)S(1)}, u32[]{:S(2)}, u32[]{:S(2)}) collective-permute-start(bf16[2,192,384]{2,1,0:T(8,128)(2,1)S(1)} %pad_maximum_fusion.7), channel_id=1, source_target_pairs={{3,23},{4,16},{5,17},{6,18},{9,29},{11,31},{12,24},{13,25},{14,26}... | collective-permute-start | bytes 884744 | tf_op jit(solution)/shard_map/ppermute | solution.py:66
  65.5 4.0 %collective-permute-done.7.refs_8_ = bf16[2,192,384]{2,1,0:T(8,128)(2,1)S(1)} collective-permute-done((bf16[2,192,384]{2,1,0:T(8,128)(2,1)S(1)}, bf16[2,192,384]{2,1,0:T(8,128)(2,1)S(1)}, u32[]{:S(2)}, u32[]{:S(2)}) %collective-permute-start.7) | collective-permute-done | bytes 294944 | tf_op jit(solution)/shard_map/ppermute | solution.py:66
  69.4 6.7 %collective-permute-done.8.refs_9_ = bf16[2,192,384]{2,1,0:T(8,128)(2,1)S(1)} collective-permute-done((bf16[2,192,384]{2,1,0:T(8,128)(2,1)S(1)}, bf16[2,192,384]{2,1,0:T(8,128)(2,1)S(1)}, u32[]{:S(2)}, u32[]{:S(2)}) %collective-permute-start.8) | collective-permute-done | bytes 294944 | tf_op jit(solution)/shard_map/ppermute | solution.py:66
  76.7 2.7 %collective-permute-start.9 = (bf16[4,384,256]{2,1,0:T(8,128)(2,1)S(1)}, bf16[4,384,256]{2,1,0:T(8,128)(2,1)S(1)}, u32[]{:S(2)}, u32[]{:S(2)}) collective-permute-start(bf16[4,384,256]{2,1,0:T(8,128)(2,1)S(1)} %get-tuple-element.37), channel_id=1, source_target_pairs={{0,2},{1,7},{2,0},{3,5},{4,6},{5,3},{6,4},{7,1},{8,10},{9,15},{10,... | collective-permute-start | bytes 2359304 | tf_op jit(solution)/shard_map/ppermute | solution.py:90
  79.5 1.9 %collective-permute-start.10 = (bf16[4,384,256]{2,1,0:T(8,128)(2,1)S(1)}, bf16[4,384,256]{2,1,0:T(8,128)(2,1)S(1)}, u32[]{:S(2)}, u32[]{:S(2)}) collective-permute-start(bf16[4,384,256]{2,1,0:T(8,128)(2,1)S(1)} %get-tuple-element.38), channel_id=1, source_target_pairs={{0,32},{1,33},{2,34},{3,35},{4,36},{5,37},{6,38},{7,39},{8,40},{9,... | collective-permute-start | bytes 2359304 | tf_op jit(solution)/shard_map/ppermute | solution.py:90
  81.4 5.2 %collective-permute-start.11 = (bf16[4,384,256]{2,1,0:T(8,128)(2,1)S(1)}, bf16[4,384,256]{2,1,0:T(8,128)(2,1)S(1)}, u32[]{:S(2)}, u32[]{:S(2)}) collective-permute-start(bf16[4,384,256]{2,1,0:T(8,128)(2,1)S(1)} %get-tuple-element.46), channel_id=1, source_target_pairs={{0,8},{1,25},{2,10},{3,27},{4,12},{5,29},{6,14},{7,31},{8,0},{9,17... | collective-permute-start | bytes 2359304 | tf_op jit(solution)/shard_map/ppermute | solution.py:90
  86.6 8.0 %shard_map.104 = (f32[8,384,128]{2,1,0:T(8,128)S(1)}, f32[8,384,128]{2,1,0:T(8,128)S(1)}, f32[8,384,128]{2,1,0:T(8,128)S(1)}) custom-call(s32[8,128]{1,0:T(8,128)S(1)} %get-tuple-element.31.refs_0_.refs_1_, bf16[8,384,128]{2,1,0:T(8,128)(2,1)S(1)} %get-tuple-element.32.refs_1_.refs_2_, bf16[8,384,256]{2,1,0:T(8,128)(2,1)S(1)} %get-tuple-element.33.refs_2_), custom_call_target="tpu_custom_call" | custom-call | tf_op jit(solution)/shard_map/pallas_call | solution.py:356
  94.6 4.2 %collective-permute-done.10.refs_8_ = bf16[4,384,256]{2,1,0:T(8,128)(2,1)S(1)} collective-permute-done((bf16[4,384,256]{2,1,0:T(8,128)(2,1)S(1)}, bf16[4,384,256]{2,1,0:T(8,128)(2,1)S(1)}, u32[]{:S(2)}, u32[]{:S(2)}) %collective-permute-start.10) | collective-permute-done | bytes 786464 | tf_op jit(solution)/shard_map/ppermute | solution.py:90
  98.9 6.5 %collective-permute-start.13 = (bf16[4,384,256]{2,1,0:T(8,128)(2,1)S(1)}, bf16[4,384,256]{2,1,0:T(8,128)(2,1)S(1)}, u32[]{:S(2)}, u32[]{:S(2)}) collective-permute-start(bf16[4,384,256]{2,1,0:T(8,128)(2,1)S(1)} %pad_maximum_fusion), channel_id=1, source_target_pairs={{0,8},{1,25},{2,10},{3,27},{4,12},{5,29},{6,14},{7,31},{8,0},{9,17... | collective-permute-start | bytes 2359304 | tf_op jit(solution)/shard_map/ppermute | solution.py:90
  105.5 2.8 %collective-permute-start.12 = (bf16[2,384,256]{2,1,0:T(8,128)(2,1)S(1)}, bf16[2,384,256]{2,1,0:T(8,128)(2,1)S(1)}, u32[]{:S(2)}, u32[]{:S(2)}) collective-permute-start(bf16[2,384,256]{2,1,0:T(8,128)(2,1)S(1)} %pad_maximum_fusion.1), channel_id=1, source_target_pairs={{0,2},{1,7},{2,0},{3,5},{4,6},{5,3},{6,4},{7,1},{8,10},{9,15},{10,... | collective-permute-start | bytes 1179656 | tf_op jit(solution)/shard_map/ppermute | solution.py:90
  108.3 3.6 %collective-permute-start.14 = (bf16[1,384,256]{2,1,0:T(8,128)(2,1)S(1)}, bf16[1,384,256]{2,1,0:T(8,128)(2,1)S(1)}, u32[]{:S(2)}, u32[]{:S(2)}) collective-permute-start(bf16[1,384,256]{2,1,0:T(8,128)(2,1)S(1)} %get-tuple-element.57), channel_id=1, source_target_pairs={{0,10},{1,31},{2,8},{3,29},{4,14},{5,27},{6,12},{7,25},{8,2},{9,23... | collective-permute-start | bytes 589832 | tf_op jit(solution)/shard_map/ppermute | solution.py:90
  111.9 8.7 %shard_map.105 = (f32[8,384,128]{2,1,0:T(8,128)S(1)}, f32[8,384,128]{2,1,0:T(8,128)S(1)}, f32[8,384,128]{2,1,0:T(8,128)S(1)}) custom-call(s32[8,128]{1,0:T(8,128)S(1)} %get-tuple-element.31.refs_0_.refs_1_, bf16[8,384,128]{2,1,0:T(8,128)(2,1)S(1)} %get-tuple-element.32.refs_1_.refs_2_, ...), custom_call_target="tpu_custom_call", output_to_operand_aliasing={{0}: (3, {}), {1}: (4, {}), {2}: (5, {})} | custom-call | tf_op jit(solution)/shard_map/pallas_call | solution.py:356
  120.6 5.0 %shard_map.106 = (bf16[2,192,128]{2,1,0:T(8,128)(2,1)S(1)}, bf16[2,192,128]{2,1,0:T(8,128)(2,1)S(1)}) custom-call(s32[1]{0:T(128)} %bitcast.refs_0_.s_ref, s32[8,128]{1,0:T(8,128)S(1)} %get-tuple-element.31.refs_0_.refs_1_, bf16[8,384,128]{2,1,0:T(8,128)(2,1)S(1)} %get-tuple-element.32.refs_1_.refs_2_, f32[8,384,128]{2,1,0:T(8,128)S(1)} %get-tuple-element.42.refs_3_, ...), custom_call_target="tpu_custom_call" | custom-call | tf_op jit(solution)/shard_map/pallas_call | solution.py:408
  125.6 3.0 %collective-permute-start.20 = (bf16[2,192,128]{2,1,0:T(8,128)(2,1)S(1)}, bf16[2,192,128]{2,1,0:T(8,128)(2,1)S(1)}, u32[]{:S(2)}, u32[]{:S(2)}) collective-permute-start(bf16[2,192,128]{2,1,0:T(8,128)(2,1)S(1)} %get-tuple-element.53), channel_id=1, source_target_pairs={{0,64},{1,65},{2,66},{3,67},{4,68},{5,69},{6,70},{7,71},{8,72},{9,... | collective-permute-start | bytes 294920 | tf_op jit(solution)/shard_map/ppermute | solution.py:76
  128.6 12.9 %shard_map.107 = (bf16[6,192,128]{2,1,0:T(8,128)(2,1)S(1)}, bf16[6,192,128]{2,1,0:T(8,128)(2,1)S(1)}) custom-call(s32[1]{0:T(128)} %bitcast.refs_0_.s_ref, s32[8,128]{1,0:T(8,128)S(1)} %get-tuple-element.31.refs_0_.refs_1_, bf16[8,384,128]{2,1,0:T(8,128)(2,1)S(1)} %get-tuple-element.32.refs_1_.refs_2_, f32[8,384,128]{2,1,0:T(8,128)S(1)} %get-tuple-element.42.refs_3_, ...), custom_call_target="tpu_custom_call" | custom-call | tf_op jit(solution)/shard_map/pallas_call | solution.py:408
  141.5 3.8 %collective-permute-start.16 = (bf16[6,192,128]{2,1,0:T(8,128)(2,1)S(1)}, bf16[6,192,128]{2,1,0:T(8,128)(2,1)S(1)}, u32[]{:S(2)}, u32[]{:S(2)}) collective-permute-start(bf16[6,192,128]{2,1,0:T(8,128)(2,1)S(1)} %get-tuple-element.52), channel_id=1, source_target_pairs={{0,64},{1,65},{2,66},{3,67},{4,68},{5,69},{6,70},{7,71},{8,72},{9,... | collective-permute-start | bytes 884744 | tf_op jit(solution)/shard_map/ppermute | solution.py:76
  146.9 6.8 %collective-permute-done.16 = bf16[6,192,128]{2,1,0:T(8,128)(2,1)S(1)} collective-permute-done((bf16[6,192,128]{2,1,0:T(8,128)(2,1)S(1)}, bf16[6,192,128]{2,1,0:T(8,128)(2,1)S(1)}, u32[]{:S(2)}, u32[]{:S(2)}) %collective-permute-start.16) | collective-permute-done | bytes 294944 | tf_op jit(solution)/shard_map/ppermute | solution.py:76
  155.1 4.7 %collective-permute-start.18 = (bf16[4,192,128]{2,1,0:T(8,128)(2,1)S(1)}, bf16[4,192,128]{2,1,0:T(8,128)(2,1)S(1)}, u32[]{:S(2)}, u32[]{:S(2)}) collective-permute-start(bf16[4,192,128]{2,1,0:T(8,128)(2,1)S(1)} %pad_maximum_fusion.9), channel_id=1, source_target_pairs={{0,16},{1,17},{2,18},{3,19},{4,20},{5,21},{6,22},{7,23},{8,24},{9,... | collective-permute-start | bytes 589832 | tf_op jit(solution)/shard_map/ppermute | solution.py:71
  159.8 4.0 %collective-permute-start.19 = (bf16[4,192,128]{2,1,0:T(8,128)(2,1)S(1)}, bf16[4,192,128]{2,1,0:T(8,128)(2,1)S(1)}, u32[]{:S(2)}, u32[]{:S(2)}) collective-permute-start(bf16[4,192,128]{2,1,0:T(8,128)(2,1)S(1)} %pad_maximum_fusion.10), channel_id=1, source_target_pairs={{0,20},{1,21},{2,22},{3,23},{4,16},{5,17},{6,18},{7,19},{8,28},{9,... | collective-permute-start | bytes 589832 | tf_op jit(solution)/shard_map/ppermute | solution.py:71
  164.3 7.2 %collective-permute-done.19 = bf16[4,192,128]{2,1,0:T(8,128)(2,1)S(1)} collective-permute-done((bf16[4,192,128]{2,1,0:T(8,128)(2,1)S(1)}, bf16[4,192,128]{2,1,0:T(8,128)(2,1)S(1)}, u32[]{:S(2)}, u32[]{:S(2)}) %collective-permute-start.19) | collective-permute-done | bytes 196640 | tf_op jit(solution)/shard_map/ppermute | solution.py:71
  174.5 5.0 %output.1 = bf16[192,3072]{1,0:T(8,128)(2,1)} custom-call(s32[1]{0:T(128)} %bitcast.refs_0_.s_ref, bf16[2,192,128]{2,1,0:T(8,128)(2,1)S(1)} %get-tuple-element.50.refs_0_, bf16[2,192,128]{2,1,0:T(8,128)(2,1)S(1)} %get-tuple-element.82.refs_1_, bf16[2,192,128]{2,1,0:T(8,128)(2,1)S(1)} %get-tuple-element.80.refs_2_, ...), custom_call_target="tpu_custom_call" | custom-call | tf_op jit(solution)/shard_map/output/pallas_call | solution.py:464
  (92 shorter events, 16.8 us)
Async XLA Ops:
  0.0 7.7 %copy-start.7 = (f32[128]{0:T(128)S(1)}, f32[128]{0:T(128)}, u32[]{:S(2)}) copy-start(f32[128]{0:T(128)} %param.14) | copy-start | bytes 1540
  0.0 7.7 %copy-start.6 = (f32[128]{0:T(128)S(1)}, f32[128]{0:T(128)}, u32[]{:S(2)}) copy-start(f32[128]{0:T(128)} %param.13) | copy-start | bytes 1540
  4.0 29.3 %collective-permute-start.4 = (bf16[192,3072]{1,0:T(8,128)(2,1)S(1)}, bf16[192,3072]{1,0:T(8,128)(2,1)S(1)}, u32[]{:S(2)}, u32[]{:S(2)}) collective-permute-start(bf16[192,3072]{1,0:T(8,128)(2,1)S(1)} %modulate.1.refs_1_), channel_id=1, source_target_pairs={{0,64},{64,0},{1,65},{65,1},{2,66},{66,2},{3,67},{67,3},{4,68},{68... | collective-permute-start | bytes 3538952 | tf_op jit(solution)/shard_map/ppermute | solution.py:94
  12.8 8.2 %slice-start.4 = ((s8[4718592]{0:T(1024)(128)(4,1)}), s8[4194304]{0:T(1024)(128)(4,1)S(1)}, s32[]{:S(2)}) async-start(s8[4718592]{0:T(1024)(128)(4,1)} %bitcast.11), calls=%async_computation.4 | async-start | bytes 8388608
  12.8 20.6 %slice-start = ((s8[14155776]{0:T(1024)(128)(4,1)}), s8[4194304]{0:T(1024)(128)(4,1)S(1)}, s32[]{:S(2)}) async-start(s8[14155776]{0:T(1024)(128)(4,1)} %bitcast.9), calls=%async_computation | async-start | bytes 8388608
  12.8 20.6 %slice-start.1 = ((s8[14155776]{0:T(1024)(128)(4,1)}), s8[4194304]{0:T(1024)(128)(4,1)S(1)}, s32[]{:S(2)}) async-start(s8[14155776]{0:T(1024)(128)(4,1)} %bitcast.9), calls=%async_computation.1 | async-start | bytes 8388608
  16.4 17.0 %slice-start.2 = ((s8[14155776]{0:T(1024)(128)(4,1)}), s8[4194304]{0:T(1024)(128)(4,1)S(1)}, s32[]{:S(2)}) async-start(s8[14155776]{0:T(1024)(128)(4,1)} %bitcast.9), calls=%async_computation.2 | async-start | bytes 8388608
  16.4 17.0 %slice-start.3 = ((s8[14155776]{0:T(1024)(128)(4,1)}), s8[1572864]{0:T(1024)(128)(4,1)S(1)}, s32[]{:S(2)}) async-start(s8[14155776]{0:T(1024)(128)(4,1)} %bitcast.9), calls=%async_computation.3 | async-start | bytes 3145728
  16.4 4.8 %collective-permute-start = (bf16[4,208,384]{2,1,0:T(8,128)(2,1)S(1)}, bf16[4,208,384]{2,1,0:T(8,128)(2,1)S(1)}, u32[]{:S(2)}, u32[]{:S(2)}) collective-permute-start(bf16[4,208,384]{2,1,0:T(8,128)(2,1)S(1)} %shard_map.101), channel_id=1, source_target_pairs={{0,1},{1,0},{2,3},{3,2},{4,5},{5,4},{6,7},{7,6},{8,9},{9,8},{10,11... | collective-permute-start | bytes 1916936 | tf_op jit(solution)/shard_map/ppermute | solution.py:85
  37.0 16.9 %collective-permute-start.5 = (bf16[4,192,384]{2,1,0:T(8,128)(2,1)S(1)}, bf16[4,192,384]{2,1,0:T(8,128)(2,1)S(1)}, u32[]{:S(2)}, u32[]{:S(2)}) collective-permute-start(bf16[4,192,384]{2,1,0:T(8,128)(2,1)S(1)} %shard_map.103), channel_id=1, source_target_pairs={{0,1},{1,0},{2,3},{3,2},{4,5},{5,4},{6,7},{7,6},{8,9},{9,8},{10,11... | collective-permute-start | bytes 1769480 | tf_op jit(solution)/shard_map/ppermute | solution.py:85
  38.4 17.0 %collective-permute-start.1 = (bf16[2,208,384]{2,1,0:T(8,128)(2,1)S(1)}, bf16[2,208,384]{2,1,0:T(8,128)(2,1)S(1)}, u32[]{:S(2)}, u32[]{:S(2)}) collective-permute-start(bf16[2,208,384]{2,1,0:T(8,128)(2,1)S(1)} %pad_maximum_fusion.2), channel_id=1, source_target_pairs={{0,4},{1,5},{2,6},{3,7},{4,0},{5,1},{6,2},{7,3},{8,12},{10,14},{11... | collective-permute-start | bytes 958472 | tf_op jit(solution)/shard_map/ppermute | solution.py:66
  39.7 23.8 %collective-permute-start.2 = (bf16[2,208,384]{2,1,0:T(8,128)(2,1)S(1)}, bf16[2,208,384]{2,1,0:T(8,128)(2,1)S(1)}, u32[]{:S(2)}, u32[]{:S(2)}) collective-permute-start(bf16[2,208,384]{2,1,0:T(8,128)(2,1)S(1)} %pad_maximum_fusion.3), channel_id=1, source_target_pairs={{0,16},{1,17},{2,18},{7,23},{8,24},{9,25},{10,26},{11,27},{13,29},... | collective-permute-start | bytes 958472 | tf_op jit(solution)/shard_map/ppermute | solution.py:66
  45.1 20.3 %collective-permute-start.3 = (bf16[2,208,384]{2,1,0:T(8,128)(2,1)S(1)}, bf16[2,208,384]{2,1,0:T(8,128)(2,1)S(1)}, u32[]{:S(2)}, u32[]{:S(2)}) collective-permute-start(bf16[2,208,384]{2,1,0:T(8,128)(2,1)S(1)} %pad_maximum_fusion.4), channel_id=1, source_target_pairs={{3,23},{4,16},{5,17},{6,18},{9,29},{11,31},{12,24},{13,25},{14,26}... | collective-permute-start | bytes 958472 | tf_op jit(solution)/shard_map/ppermute | solution.py:66
  47.0 78.6 %collective-permute-start.15 = (bf16[384,3072]{1,0:T(8,128)(2,1)S(1)}, bf16[384,3072]{1,0:T(8,128)(2,1)S(1)}, u32[]{:S(2)}, u32[]{:S(2)}) collective-permute-start(bf16[384,3072]{1,0:T(8,128)(2,1)S(1)} %weight_part.1), channel_id=1, source_target_pairs={{0,96},{1,97},{2,98},{3,99},{4,100},{5,101},{6,102},{7,103},{8,104... | collective-permute-start | bytes 7077896 | tf_op jit(solution)/shard_map/ppermute | solution.py:81
  53.8 22.4 %copy-start.2 = (s32[8,8,128]{2,1,0:T(8,128)S(1)}, s32[8,8,128]{2,1,0:T(8,128)}, u32[]{:S(2)}) copy-start(s32[8,8,128]{2,1,0:T(8,128)} %constant.9.clone.refs_10_) | copy-start | bytes 98308
  54.0 11.5 %collective-permute-start.6 = (bf16[2,192,384]{2,1,0:T(8,128)(2,1)S(1)}, bf16[2,192,384]{2,1,0:T(8,128)(2,1)S(1)}, u32[]{:S(2)}, u32[]{:S(2)}) collective-permute-start(bf16[2,192,384]{2,1,0:T(8,128)(2,1)S(1)} %pad_maximum_fusion.5), channel_id=1, source_target_pairs={{0,4},{1,5},{2,6},{3,7},{4,0},{5,1},{6,2},{7,3},{8,12},{10,14},{11... | collective-permute-start | bytes 884744 | tf_op jit(solution)/shard_map/ppermute | solution.py:66
  55.3 14.1 %collective-permute-start.7 = (bf16[2,192,384]{2,1,0:T(8,128)(2,1)S(1)}, bf16[2,192,384]{2,1,0:T(8,128)(2,1)S(1)}, u32[]{:S(2)}, u32[]{:S(2)}) collective-permute-start(bf16[2,192,384]{2,1,0:T(8,128)(2,1)S(1)} %pad_maximum_fusion.6), channel_id=1, source_target_pairs={{0,16},{1,17},{2,18},{7,23},{8,24},{9,25},{10,26},{11,27},{13,29},... | collective-permute-start | bytes 884744 | tf_op jit(solution)/shard_map/ppermute | solution.py:66
  63.5 12.7 %collective-permute-start.8 = (bf16[2,192,384]{2,1,0:T(8,128)(2,1)S(1)}, bf16[2,192,384]{2,1,0:T(8,128)(2,1)S(1)}, u32[]{:S(2)}, u32[]{:S(2)}) collective-permute-start(bf16[2,192,384]{2,1,0:T(8,128)(2,1)S(1)} %pad_maximum_fusion.7), channel_id=1, source_target_pairs={{3,23},{4,16},{5,17},{6,18},{9,29},{11,31},{12,24},{13,25},{14,26}... | collective-permute-start | bytes 884744 | tf_op jit(solution)/shard_map/ppermute | solution.py:66
  76.7 17.8 %collective-permute-start.9 = (bf16[4,384,256]{2,1,0:T(8,128)(2,1)S(1)}, bf16[4,384,256]{2,1,0:T(8,128)(2,1)S(1)}, u32[]{:S(2)}, u32[]{:S(2)}) collective-permute-start(bf16[4,384,256]{2,1,0:T(8,128)(2,1)S(1)} %get-tuple-element.37), channel_id=1, source_target_pairs={{0,2},{1,7},{2,0},{3,5},{4,6},{5,3},{6,4},{7,1},{8,10},{9,15},{10,... | collective-permute-start | bytes 2359304 | tf_op jit(solution)/shard_map/ppermute | solution.py:90
  79.5 19.2 %collective-permute-start.10 = (bf16[4,384,256]{2,1,0:T(8,128)(2,1)S(1)}, bf16[4,384,256]{2,1,0:T(8,128)(2,1)S(1)}, u32[]{:S(2)}, u32[]{:S(2)}) collective-permute-start(bf16[4,384,256]{2,1,0:T(8,128)(2,1)S(1)} %get-tuple-element.38), channel_id=1, source_target_pairs={{0,32},{1,33},{2,34},{3,35},{4,36},{5,37},{6,38},{7,39},{8,40},{9,... | collective-permute-start | bytes 2359304 | tf_op jit(solution)/shard_map/ppermute | solution.py:90
  81.4 39.2 %collective-permute-start.11 = (bf16[4,384,256]{2,1,0:T(8,128)(2,1)S(1)}, bf16[4,384,256]{2,1,0:T(8,128)(2,1)S(1)}, u32[]{:S(2)}, u32[]{:S(2)}) collective-permute-start(bf16[4,384,256]{2,1,0:T(8,128)(2,1)S(1)} %get-tuple-element.46), channel_id=1, source_target_pairs={{0,8},{1,25},{2,10},{3,27},{4,12},{5,29},{6,14},{7,31},{8,0},{9,17... | collective-permute-start | bytes 2359304 | tf_op jit(solution)/shard_map/ppermute | solution.py:90
  98.9 21.7 %collective-permute-start.13 = (bf16[4,384,256]{2,1,0:T(8,128)(2,1)S(1)}, bf16[4,384,256]{2,1,0:T(8,128)(2,1)S(1)}, u32[]{:S(2)}, u32[]{:S(2)}) collective-permute-start(bf16[4,384,256]{2,1,0:T(8,128)(2,1)S(1)} %pad_maximum_fusion), channel_id=1, source_target_pairs={{0,8},{1,25},{2,10},{3,27},{4,12},{5,29},{6,14},{7,31},{8,0},{9,17... | collective-permute-start | bytes 2359304 | tf_op jit(solution)/shard_map/ppermute | solution.py:90
  105.5 15.1 %collective-permute-start.12 = (bf16[2,384,256]{2,1,0:T(8,128)(2,1)S(1)}, bf16[2,384,256]{2,1,0:T(8,128)(2,1)S(1)}, u32[]{:S(2)}, u32[]{:S(2)}) collective-permute-start(bf16[2,384,256]{2,1,0:T(8,128)(2,1)S(1)} %pad_maximum_fusion.1), channel_id=1, source_target_pairs={{0,2},{1,7},{2,0},{3,5},{4,6},{5,3},{6,4},{7,1},{8,10},{9,15},{10,... | collective-permute-start | bytes 1179656 | tf_op jit(solution)/shard_map/ppermute | solution.py:90
  108.3 12.3 %collective-permute-start.14 = (bf16[1,384,256]{2,1,0:T(8,128)(2,1)S(1)}, bf16[1,384,256]{2,1,0:T(8,128)(2,1)S(1)}, u32[]{:S(2)}, u32[]{:S(2)}) collective-permute-start(bf16[1,384,256]{2,1,0:T(8,128)(2,1)S(1)} %get-tuple-element.57), channel_id=1, source_target_pairs={{0,10},{1,31},{2,8},{3,29},{4,14},{5,27},{6,12},{7,25},{8,2},{9,23... | collective-permute-start | bytes 589832 | tf_op jit(solution)/shard_map/ppermute | solution.py:90
  125.6 45.8 %collective-permute-start.20 = (bf16[2,192,128]{2,1,0:T(8,128)(2,1)S(1)}, bf16[2,192,128]{2,1,0:T(8,128)(2,1)S(1)}, u32[]{:S(2)}, u32[]{:S(2)}) collective-permute-start(bf16[2,192,128]{2,1,0:T(8,128)(2,1)S(1)} %get-tuple-element.53), channel_id=1, source_target_pairs={{0,64},{1,65},{2,66},{3,67},{4,68},{5,69},{6,70},{7,71},{8,72},{9,... | collective-permute-start | bytes 294920 | tf_op jit(solution)/shard_map/ppermute | solution.py:76
  141.5 12.1 %collective-permute-start.16 = (bf16[6,192,128]{2,1,0:T(8,128)(2,1)S(1)}, bf16[6,192,128]{2,1,0:T(8,128)(2,1)S(1)}, u32[]{:S(2)}, u32[]{:S(2)}) collective-permute-start(bf16[6,192,128]{2,1,0:T(8,128)(2,1)S(1)} %get-tuple-element.52), channel_id=1, source_target_pairs={{0,64},{1,65},{2,66},{3,67},{4,68},{5,69},{6,70},{7,71},{8,72},{9,... | collective-permute-start | bytes 884744 | tf_op jit(solution)/shard_map/ppermute | solution.py:76
  145.3 29.2 %collective-permute-start.22 = (bf16[384,3072]{1,0:T(8,128)(2,1)S(1)}, bf16[384,3072]{1,0:T(8,128)(2,1)S(1)}, u32[]{:S(2)}, u32[]{:S(2)}) collective-permute-start(bf16[384,3072]{1,0:T(8,128)(2,1)S(1)} %collective-permute-done.15.refs_10_), channel_id=1, source_target_pairs={{0,1},{1,0},{2,3},{3,2},{4,5},{5,4},{6,7},{7,6},{8,9},{9,8},{10,11... | collective-permute-start | bytes 7077896 | tf_op jit(solution)/shard_map/ppermute | solution.py:85
  153.7 20.8 %copy-start.5 = (f32[3072]{0:T(1024)S(1)}, f32[3072]{0:T(1024)}, u32[]{:S(2)}) copy-start(f32[3072]{0:T(1024)} %param.17) | copy-start | bytes 36868
  153.7 10.1 %collective-permute-start.17 = (bf16[4,192,128]{2,1,0:T(8,128)(2,1)S(1)}, bf16[4,192,128]{2,1,0:T(8,128)(2,1)S(1)}, u32[]{:S(2)}, u32[]{:S(2)}) collective-permute-start(bf16[4,192,128]{2,1,0:T(8,128)(2,1)S(1)} %pad_maximum_fusion.8), channel_id=1, source_target_pairs={{0,4},{1,5},{2,6},{3,7},{4,0},{5,1},{6,2},{7,3},{8,12},{9,13},{10,... | collective-permute-start | bytes 589832 | tf_op jit(solution)/shard_map/ppermute | solution.py:71
  155.1 9.2 %collective-permute-start.18 = (bf16[4,192,128]{2,1,0:T(8,128)(2,1)S(1)}, bf16[4,192,128]{2,1,0:T(8,128)(2,1)S(1)}, u32[]{:S(2)}, u32[]{:S(2)}) collective-permute-start(bf16[4,192,128]{2,1,0:T(8,128)(2,1)S(1)} %pad_maximum_fusion.9), channel_id=1, source_target_pairs={{0,16},{1,17},{2,18},{3,19},{4,20},{5,21},{6,22},{7,23},{8,24},{9,... | collective-permute-start | bytes 589832 | tf_op jit(solution)/shard_map/ppermute | solution.py:71
  159.8 11.6 %collective-permute-start.19 = (bf16[4,192,128]{2,1,0:T(8,128)(2,1)S(1)}, bf16[4,192,128]{2,1,0:T(8,128)(2,1)S(1)}, u32[]{:S(2)}, u32[]{:S(2)}) collective-permute-start(bf16[4,192,128]{2,1,0:T(8,128)(2,1)S(1)} %pad_maximum_fusion.10), channel_id=1, source_target_pairs={{0,20},{1,21},{2,22},{3,23},{4,16},{5,17},{6,18},{7,19},{8,28},{9,... | collective-permute-start | bytes 589832 | tf_op jit(solution)/shard_map/ppermute | solution.py:71
  171.5 3.0 %collective-permute-start.21 = (bf16[8,192,128]{2,1,0:T(8,128)(2,1)S(1)}, bf16[8,192,128]{2,1,0:T(8,128)(2,1)S(1)}, u32[]{:S(2)}, u32[]{:S(2)}) collective-permute-start(bf16[8,192,128]{2,1,0:T(8,128)(2,1)S(1)} %slice_dynamic-update-slice_fusion), channel_id=1, source_target_pairs={{0,1},{1,0},{2,3},{3,2},{4,5},{5,4},{6,7},{7,6},{8,9},{9,8},{10,11... | collective-permute-start | bytes 1179656 | tf_op jit(solution)/shard_map/ppermute | solution.py:85
  (6 other events, 20.1 us)

commit v4 on v3

--- a/solution.py
+++ b/solution.py
@@ -127,53 +127,49 @@
 def project_kernel(other, s_ref, x_ref, w_ref, qg_ref, kg_ref, mask_ref, out_ref):
     s = s_ref[0]
     rows = x_ref.shape[0]
-    slot = slot_of(s, (s & 1) ^ other, pl.program_id(0))
-
-    @pl.when(slot < 3)
-    def _():
-        acc = jnp.dot(x_ref[...], w_ref[...], preferred_element_type=jnp.float32).astype(jnp.bfloat16)
-
-        def normed(part, gain):
-            part = part.astype(jnp.float32)
-            return part * lax.rsqrt(jnp.mean(part * part, axis=-1, keepdims=True) + 1e-06) * gain
-
-        q = normed(acc[:, :HD], qg_ref[...]) * HD ** (-0.5)
-        out_ref[0, :rows, :HD] = q.astype(jnp.bfloat16)
-        out_ref[0, :rows, HD : 2 * HD] = normed(acc[:, HD : 2 * HD], kg_ref[...]).astype(jnp.bfloat16)
-        out_ref[0, :rows, 2 * HD :] = acc[:, 2 * HD :]
-        if out_ref.shape[1] > rows:
-            out_ref[0, rows:, :] = mask_ref[...]
-
-    @pl.when(slot >= 3)
-    def _():
-        out_ref[0] = jnp.zeros_like(out_ref[0])
+    core = (s & 1) ^ other
+
+    def normed(part, gain):
+        part = part.astype(jnp.float32)
+        return part * lax.rsqrt(jnp.mean(part * part, axis=-1, keepdims=True) + 1e-06) * gain
+
+    def one_slot(i, _):
+        slot = slot_of(s, core, i)
+
+        @pl.when(slot < 3)
+        def _():
+            at = pl.multiple_of((core * 3 + slot) * (3 * HD), 3 * HD)
+            acc = jnp.dot(
+                x_ref[...], w_ref[:, pl.ds(at, 3 * HD)], preferred_element_type=jnp.float32
+            ).astype(jnp.bfloat16)
+            q = normed(acc[:, :HD], qg_ref[...]) * HD ** (-0.5)
+            out_ref[i, :rows, :HD] = q.astype(jnp.bfloat16)
+            out_ref[i, :rows, HD : 2 * HD] = normed(acc[:, HD : 2 * HD], kg_ref[...]).astype(
+                jnp.bfloat16
+            )
+            out_ref[i, :rows, 2 * HD :] = acc[:, 2 * HD :]
+            if out_ref.shape[1] > rows:
+                out_ref[i, rows:, :] = mask_ref[...]
+
+        @pl.when(slot >= 3)
+        def _():
+            out_ref[i] = jnp.zeros_like(out_ref[i])
+
+        return 0
+
+    lax.fori_loop(0, 4, one_slot, 0)
 
 
 def project(slab_at, x, weight, query_gain, key_gain, mask_rows, other, with_mask):
-    rows, width = x.shape
+    rows, _ = x.shape
     out_rows = rows + (MASK_ROWS if with_mask else 0)
-
-    def weight_at(i, s_ref):
-        s = s_ref[0]
-        core = (s & 1) ^ other
-        return (0, core * 3 + jnp.minimum(slot_of(s, core, i), 2))
-
+    vmem = pl.BlockSpec(memory_space=pltpu.VMEM)
     return pl.pallas_call(
         lambda *refs: project_kernel(other, *refs),
         out_shape=jax.ShapeDtypeStruct((4, out_rows, 3 * HD), jnp.bfloat16),
-        grid_spec=pltpu.PrefetchScalarGridSpec(
-            num_scalar_prefetch=1,
-            grid=(4,),
-            in_specs=[
-                whole((rows, width)),
-                pl.BlockSpec((width, 3 * HD), weight_at),
-                whole((1, HD)),
-                whole((1, HD)),
-                whole((MASK_ROWS, 3 * HD)),
-            ],
-            out_specs=pl.BlockSpec((1, out_rows, 3 * HD), lambda i, s_ref: (i, 0, 0)),
-        ),
-        compiler_params=pltpu.CompilerParams(vmem_limit_bytes=7 << 20),
+        in_specs=[pl.BlockSpec(memory_space=pltpu.SMEM)] + [vmem] * 5,
+        out_specs=vmem,
+        compiler_params=pltpu.CompilerParams(vmem_limit_bytes=20 << 20),
     )(slab_at, x, weight, query_gain, key_gain, mask_rows)
 
 
@@ -459,7 +455,7 @@
 def output(slab_at, same, cross, core, weight, weight_c, weight_d, gate):
     inner, width = weight.shape
     half = TILE // 2
-    cols = 512
+    cols = 1024
     by_col = lambda rows: pl.BlockSpec((rows, cols), lambda n, s_ref: (0, n))
     return pl.pallas_call(
         output_kernel,
@@ -476,7 +472,7 @@
                 pltpu.VMEM((half, inner // 2), jnp.bfloat16),
             ],
         ),
-        compiler_params=pltpu.CompilerParams(vmem_limit_bytes=14 << 20),
+        compiler_params=pltpu.CompilerParams(vmem_limit_bytes=10 << 20),
         name="output",
     )(slab_at, *same, *cross, core, weight, weight_c, weight_d, gate)
 
@@ -518,14 +514,16 @@
     halo = []
     for piece, (moved, _) in zip(sends, HALO):
         halo.append(to_block(piece, moved))
-    state = attend_own(live, q, kv, 0, 4, ())
+    state = attend_own(live, q, kv, 0, 6, ())
     *state, side, over = lax.optimization_barrier((*state, halo[0], halo[2]))
     halo = [side, halo[1], over]
     for moved, tiles in (
-        ((0, 0, 1), (over[0], over[2])), ((0, 1, 0), (over[0], over[1], side[0], side[2])), ((0, 1, 1), (over[0],))
+        ((0, 0, 1), (over[0], over[2])),
+        ((0, 1, 0), (over[0], over[1], side[0], side[2])),
+        ((0, 1, 1), (over[0],)),
     ):
         halo.append(to_block(jnp.stack(tiles), moved))
-    state = attend_own(live, q, kv, 4, 4, state)
+    state = attend_own(live, q, kv, 6, 2, state)
     done = {}
     for first, tiles in ((2, 6), (0, 2)):
         mixed, crossing = attend_halo(slab_at, live, q, state, halo, first, tiles)

time: 180 us -> 174 us (0.967)
  waiting for transfers between devices: 42.6 us -> 38.4 us
  Pallas kernels: 55.7 us -> 51.8 us
    pallas_call x4, Pallas kernels: 14.2 us -> 11 us  [project(): pl.pallas_call(lambda *refs: project_kernel(other, *refs), out_shape=jax....]
    ppermute x4, starting transfers between devices: 5.52 us -> 8.25 us  [to_core(): return lax.ppermute(value, 'slab', [(s, s ^ 1) for s in range(64)])]
    ppermute x6, waiting for transfers between devices: 4.17 us -> 1.45 us  [to_block(): return lax.ppermute(value, 'slab', pairs)]
  transfers between devices with their start and end apart: 23 -> 23, of which waited for: 8 -> 7; matrix products, arithmetic and copies ran while one was open for 0% -> 1% of each run, Pallas kernels for 26% -> 25%
where the time goes in v4:
time: 174 us; the launch traced here: 173 us
  starting transfers between devices  73.6 us (42%)
  Pallas kernels  51.8 us (30%)
  waiting for transfers between devices  38.4 us (22%)
  local copies, waits for them, and re-layouts  8.25 us (5%)
    ppermute x6, starting transfers between devices, to_block(): return lax.ppermute(value, 'slab', pairs)  21.9 us
    ppermute x6, starting transfers between devices, to_chip(): return lax.ppermute(value, 'slab', pairs)  19.9 us
    pallas_call x2, Pallas kernels, attend_halo(): pl.pallas_call(lambda *refs: halo_kernel(first, *refs), out_shape=[jax.Sh...  17.9 us
    pallas_call x2, Pallas kernels, attend_own(): pl.pallas_call(lambda *refs: own_kernel(first, *refs), out_shape=[state,...  16.6 us
    ppermute x1, waiting for transfers between devices, to_group(): return lax.ppermute(value, 'heads', [(0, 1), (1, 0)])  13.7 us
    pallas_call x4, Pallas kernels, project(): pl.pallas_call(lambda *refs: project_kernel(other, *refs), out_shape=jax....  11 us
    ppermute x6, waiting for transfers between devices, to_chip(): return lax.ppermute(value, 'slab', pairs)  10.7 us
    ppermute x3, starting transfers between devices, from_chip(): return lax.ppermute(value, 'slab', pairs)  9.83 us
  transfers between devices with their start and end apart: 23, of which 7 were waited for; matrix products, arithmetic and copies ran while one was open for 1% of the time, Pallas kernels for 25%

profile of v4, /device:TPU:17, one launch (start us, length us, event | category | flops | bytes accessed | tf_op | source)
XLA Modules:
  0.0 173.2 jit_solution(15959456640912512884)
XLA Ops:
  4.0 3.7 %collective-permute-start.4 = (bf16[192,3072]{1,0:T(8,128)(2,1)S(1)}, bf16[192,3072]{1,0:T(8,128)(2,1)S(1)}, u32[]{:S(2)}, u32[]{:S(2)}) collective-permute-start(bf16[192,3072]{1,0:T(8,128)(2,1)S(1)} %modulate.1.refs_1_), channel_id=1, source_target_pairs={{0,64},{64,0},{1,65},{65,1},{2,66},{66,2},{3,67},{67,3},{4,68},{68... | collective-permute-start | bytes 3538952 | tf_op jit(solution)/shard_map/ppermute | solution.py:94
  7.8 5.0 %copy-done = bf16[3072,2304]{1,0:T(8,128)(2,1)S(1)} copy-done((bf16[3072,2304]{1,0:T(8,128)(2,1)S(1)}, bf16[3072,2304]{1,0:T(8,128)(2,1)}, u32[]{:S(2)}) %copy-start) | copy-done | bytes 14155800
  12.8 2.7 %shard_map.101 = bf16[4,208,384]{2,1,0:T(8,128)(2,1)S(1)} custom-call(s32[1]{0:T(128)} %bitcast.refs_0_.s_ref, bf16[192,3072]{1,0:T(8,128)(2,1)S(1)} %modulate.1.refs_1_, bf16[3072,2304]{1,0:T(8,128)(2,1)S(1)} %copy-done, f32[1,128]{1,0:T(1,128)S(1)} %bitcast.16, f32[1,128]{1,0:T(1,128)S(1)} %bitcast.20, bf16[16,384]{1,0:T(8,128)(2,1)S(1)} %pad.7.refs_5_), custom_call_target="tpu_custom_call" | custom-call | tf_op jit(solution)/shard_map/pallas_call | solution.py:167
  16.6 2.7 %shard_map.100.refs_0_ = bf16[4,208,384]{2,1,0:T(8,128)(2,1)S(1)} custom-call(s32[1]{0:T(128)} %bitcast.refs_0_.s_ref, bf16[192,3072]{1,0:T(8,128)(2,1)S(1)} %modulate.1.refs_1_, bf16[3072,2304]{1,0:T(8,128)(2,1)S(1)} %copy-done, f32[1,128]{1,0:T(1,128)S(1)} %bitcast.17, f32[1,128]{1,0:T(1,128)S(1)} %bitcast.21, bf16[16,384]{1,0:T(8,128)(2,1)S(1)} %pad.7.refs_5_), custom_call_target="tpu_custom_call" | custom-call | tf_op jit(solution)/shard_map/pallas_call | solution.py:167
  19.7 13.7 %collective-permute-done.4.refs_1_ = bf16[192,3072]{1,0:T(8,128)(2,1)S(1)} collective-permute-done((bf16[192,3072]{1,0:T(8,128)(2,1)S(1)}, bf16[192,3072]{1,0:T(8,128)(2,1)S(1)}, u32[]{:S(2)}, u32[]{:S(2)}) %collective-permute-start.4) | collective-permute-done | bytes 1179680 | tf_op jit(solution)/shard_map/ppermute | solution.py:94
  33.4 2.8 %shard_map.103 = bf16[4,192,384]{2,1,0:T(8,128)(2,1)S(1)} custom-call(s32[1]{0:T(128)} %bitcast.refs_0_.s_ref, bf16[192,3072]{1,0:T(8,128)(2,1)S(1)} %collective-permute-done.4.refs_1_, bf16[3072,2304]{1,0:T(8,128)(2,1)S(1)} %bitcast.10, f32[1,128]{1,0:T(1,128)S(1)} %bitcast.18, f32[1,128]{1,0:T(1,128)S(1)} %bitcast.22, bf16[16,384]{1,0:T(8,128)(2,1)S(1)} %pad.7.refs_5_), custom_call_target="tpu_custom_call" | custom-call | tf_op jit(solution)/shard_map/pallas_call | solution.py:167
  38.9 5.3 %collective-permute-start.2 = (bf16[2,208,384]{2,1,0:T(8,128)(2,1)S(1)}, bf16[2,208,384]{2,1,0:T(8,128)(2,1)S(1)}, u32[]{:S(2)}, u32[]{:S(2)}) collective-permute-start(bf16[2,208,384]{2,1,0:T(8,128)(2,1)S(1)} %pad_maximum_fusion.3), channel_id=1, source_target_pairs={{0,16},{1,17},{2,18},{7,23},{8,24},{9,25},{10,26},{11,27},{13,29},... | collective-permute-start | bytes 958472 | tf_op jit(solution)/shard_map/ppermute | solution.py:66
  44.3 1.9 %collective-permute-start.3 = (bf16[2,208,384]{2,1,0:T(8,128)(2,1)S(1)}, bf16[2,208,384]{2,1,0:T(8,128)(2,1)S(1)}, u32[]{:S(2)}, u32[]{:S(2)}) collective-permute-start(bf16[2,208,384]{2,1,0:T(8,128)(2,1)S(1)} %pad_maximum_fusion.4), channel_id=1, source_target_pairs={{3,23},{4,16},{5,17},{6,18},{9,29},{11,31},{12,24},{13,25},{14,26}... | collective-permute-start | bytes 958472 | tf_op jit(solution)/shard_map/ppermute | solution.py:66
  46.2 3.2 %collective-permute-start.15 = (bf16[384,3072]{1,0:T(8,128)(2,1)S(1)}, bf16[384,3072]{1,0:T(8,128)(2,1)S(1)}, u32[]{:S(2)}, u32[]{:S(2)}) collective-permute-start(bf16[384,3072]{1,0:T(8,128)(2,1)S(1)} %weight_part.1), channel_id=1, source_target_pairs={{0,96},{1,97},{2,98},{3,99},{4,100},{5,101},{6,102},{7,103},{8,104... | collective-permute-start | bytes 7077896 | tf_op jit(solution)/shard_map/ppermute | solution.py:81
  49.4 2.7 %shard_map.102.refs_5_ = bf16[4,192,384]{2,1,0:T(8,128)(2,1)S(1)} custom-call(s32[1]{0:T(128)} %bitcast.refs_0_.s_ref, bf16[192,3072]{1,0:T(8,128)(2,1)S(1)} %collective-permute-done.4.refs_1_, bf16[3072,2304]{1,0:T(8,128)(2,1)S(1)} %bitcast.10, f32[1,128]{1,0:T(1,128)S(1)} %bitcast.19, f32[1,128]{1,0:T(1,128)S(1)} %bitcast.23, bf16[16,384]{1,0:T(8,128)(2,1)S(1)} %pad.7.refs_5_), custom_call_target="tpu_custom_call" | custom-call | tf_op jit(solution)/shard_map/pallas_call | solution.py:167
  53.7 8.2 %collective-permute-start.7 = (bf16[2,192,384]{2,1,0:T(8,128)(2,1)S(1)}, bf16[2,192,384]{2,1,0:T(8,128)(2,1)S(1)}, u32[]{:S(2)}, u32[]{:S(2)}) collective-permute-start(bf16[2,192,384]{2,1,0:T(8,128)(2,1)S(1)} %pad_maximum_fusion.6), channel_id=1, source_target_pairs={{0,16},{1,17},{2,18},{7,23},{8,24},{9,25},{10,26},{11,27},{13,29},... | collective-permute-start | bytes 884744 | tf_op jit(solution)/shard_map/ppermute | solution.py:66
  61.9 1.9 %collective-permute-start.8 = (bf16[2,192,384]{2,1,0:T(8,128)(2,1)S(1)}, bf16[2,192,384]{2,1,0:T(8,128)(2,1)S(1)}, u32[]{:S(2)}, u32[]{:S(2)}) collective-permute-start(bf16[2,192,384]{2,1,0:T(8,128)(2,1)S(1)} %pad_maximum_fusion.7), channel_id=1, source_target_pairs={{3,23},{4,16},{5,17},{6,18},{9,29},{11,31},{12,24},{13,25},{14,26}... | collective-permute-start | bytes 884744 | tf_op jit(solution)/shard_map/ppermute | solution.py:66
  63.9 4.0 %collective-permute-done.7.refs_8_ = bf16[2,192,384]{2,1,0:T(8,128)(2,1)S(1)} collective-permute-done((bf16[2,192,384]{2,1,0:T(8,128)(2,1)S(1)}, bf16[2,192,384]{2,1,0:T(8,128)(2,1)S(1)}, u32[]{:S(2)}, u32[]{:S(2)}) %collective-permute-start.7) | collective-permute-done | bytes 294944 | tf_op jit(solution)/shard_map/ppermute | solution.py:66
  67.8 6.7 %collective-permute-done.8.refs_9_ = bf16[2,192,384]{2,1,0:T(8,128)(2,1)S(1)} collective-permute-done((bf16[2,192,384]{2,1,0:T(8,128)(2,1)S(1)}, bf16[2,192,384]{2,1,0:T(8,128)(2,1)S(1)}, u32[]{:S(2)}, u32[]{:S(2)}) %collective-permute-start.8) | collective-permute-done | bytes 294944 | tf_op jit(solution)/shard_map/ppermute | solution.py:66
  75.1 2.7 %collective-permute-start.9 = (bf16[4,384,256]{2,1,0:T(8,128)(2,1)S(1)}, bf16[4,384,256]{2,1,0:T(8,128)(2,1)S(1)}, u32[]{:S(2)}, u32[]{:S(2)}) collective-permute-start(bf16[4,384,256]{2,1,0:T(8,128)(2,1)S(1)} %get-tuple-element.37), channel_id=1, source_target_pairs={{0,2},{1,7},{2,0},{3,5},{4,6},{5,3},{6,4},{7,1},{8,10},{9,15},{10,... | collective-permute-start | bytes 2359304 | tf_op jit(solution)/shard_map/ppermute | solution.py:90
  79.8 5.1 %collective-permute-start.11 = (bf16[4,384,256]{2,1,0:T(8,128)(2,1)S(1)}, bf16[4,384,256]{2,1,0:T(8,128)(2,1)S(1)}, u32[]{:S(2)}, u32[]{:S(2)}) collective-permute-start(bf16[4,384,256]{2,1,0:T(8,128)(2,1)S(1)} %get-tuple-element.46), channel_id=1, source_target_pairs={{0,8},{1,25},{2,10},{3,27},{4,12},{5,29},{6,14},{7,31},{8,0},{9,17... | collective-permute-start | bytes 2359304 | tf_op jit(solution)/shard_map/ppermute | solution.py:90
  84.9 12.9 %shard_map.104 = (f32[8,384,128]{2,1,0:T(8,128)S(1)}, f32[8,384,128]{2,1,0:T(8,128)S(1)}, f32[8,384,128]{2,1,0:T(8,128)S(1)}) custom-call(s32[8,128]{1,0:T(8,128)S(1)} %get-tuple-element.31.refs_0_.refs_1_, bf16[8,384,128]{2,1,0:T(8,128)(2,1)S(1)} %get-tuple-element.32.refs_1_.refs_2_, bf16[8,384,256]{2,1,0:T(8,128)(2,1)S(1)} %get-tuple-element.33.refs_2_), custom_call_target="tpu_custom_call" | custom-call | tf_op jit(solution)/shard_map/pallas_call | solution.py:352
  98.0 5.7 %collective-permute-start.13 = (bf16[4,384,256]{2,1,0:T(8,128)(2,1)S(1)}, bf16[4,384,256]{2,1,0:T(8,128)(2,1)S(1)}, u32[]{:S(2)}, u32[]{:S(2)}) collective-permute-start(bf16[4,384,256]{2,1,0:T(8,128)(2,1)S(1)} %pad_maximum_fusion), channel_id=1, source_target_pairs={{0,8},{1,25},{2,10},{3,27},{4,12},{5,29},{6,14},{7,31},{8,0},{9,17... | collective-permute-start | bytes 2359304 | tf_op jit(solution)/shard_map/ppermute | solution.py:90
  103.9 2.8 %collective-permute-start.12 = (bf16[2,384,256]{2,1,0:T(8,128)(2,1)S(1)}, bf16[2,384,256]{2,1,0:T(8,128)(2,1)S(1)}, u32[]{:S(2)}, u32[]{:S(2)}) collective-permute-start(bf16[2,384,256]{2,1,0:T(8,128)(2,1)S(1)} %pad_maximum_fusion.1), channel_id=1, source_target_pairs={{0,2},{1,7},{2,0},{3,5},{4,6},{5,3},{6,4},{7,1},{8,10},{9,15},{10,... | collective-permute-start | bytes 1179656 | tf_op jit(solution)/shard_map/ppermute | solution.py:90
  106.7 3.6 %collective-permute-start.14 = (bf16[1,384,256]{2,1,0:T(8,128)(2,1)S(1)}, bf16[1,384,256]{2,1,0:T(8,128)(2,1)S(1)}, u32[]{:S(2)}, u32[]{:S(2)}) collective-permute-start(bf16[1,384,256]{2,1,0:T(8,128)(2,1)S(1)} %get-tuple-element.57), channel_id=1, source_target_pairs={{0,10},{1,31},{2,8},{3,29},{4,14},{5,27},{6,12},{7,25},{8,2},{9,23... | collective-permute-start | bytes 589832 | tf_op jit(solution)/shard_map/ppermute | solution.py:90
  110.3 3.7 %shard_map.105 = (f32[8,384,128]{2,1,0:T(8,128)S(1)}, f32[8,384,128]{2,1,0:T(8,128)S(1)}, f32[8,384,128]{2,1,0:T(8,128)S(1)}) custom-call(s32[8,128]{1,0:T(8,128)S(1)} %get-tuple-element.31.refs_0_.refs_1_, bf16[8,384,128]{2,1,0:T(8,128)(2,1)S(1)} %get-tuple-element.32.refs_1_.refs_2_, ...), custom_call_target="tpu_custom_call", output_to_operand_aliasing={{0}: (3, {}), {1}: (4, {}), {2}: (5, {})} | custom-call | tf_op jit(solution)/shard_map/pallas_call | solution.py:352
  115.4 5.0 %shard_map.106 = (bf16[2,192,128]{2,1,0:T(8,128)(2,1)S(1)}, bf16[2,192,128]{2,1,0:T(8,128)(2,1)S(1)}) custom-call(s32[1]{0:T(128)} %bitcast.refs_0_.s_ref, s32[8,128]{1,0:T(8,128)S(1)} %get-tuple-element.31.refs_0_.refs_1_, bf16[8,384,128]{2,1,0:T(8,128)(2,1)S(1)} %get-tuple-element.32.refs_1_.refs_2_, f32[8,384,128]{2,1,0:T(8,128)S(1)} %get-tuple-element.42.refs_3_, ...), custom_call_target="tpu_custom_call" | custom-call | tf_op jit(solution)/shard_map/pallas_call | solution.py:404
  120.4 3.5 %collective-permute-start.20 = (bf16[2,192,128]{2,1,0:T(8,128)(2,1)S(1)}, bf16[2,192,128]{2,1,0:T(8,128)(2,1)S(1)}, u32[]{:S(2)}, u32[]{:S(2)}) collective-permute-start(bf16[2,192,128]{2,1,0:T(8,128)(2,1)S(1)} %get-tuple-element.53), channel_id=1, source_target_pairs={{0,64},{1,65},{2,66},{3,67},{4,68},{5,69},{6,70},{7,71},{8,72},{9,... | collective-permute-start | bytes 294920 | tf_op jit(solution)/shard_map/ppermute | solution.py:76
  123.9 12.9 %shard_map.107 = (bf16[6,192,128]{2,1,0:T(8,128)(2,1)S(1)}, bf16[6,192,128]{2,1,0:T(8,128)(2,1)S(1)}) custom-call(s32[1]{0:T(128)} %bitcast.refs_0_.s_ref, s32[8,128]{1,0:T(8,128)S(1)} %get-tuple-element.31.refs_0_.refs_1_, bf16[8,384,128]{2,1,0:T(8,128)(2,1)S(1)} %get-tuple-element.32.refs_1_.refs_2_, f32[8,384,128]{2,1,0:T(8,128)S(1)} %get-tuple-element.42.refs_3_, ...), custom_call_target="tpu_custom_call" | custom-call | tf_op jit(solution)/shard_map/pallas_call | solution.py:404
  136.8 3.3 %collective-permute-start.16 = (bf16[6,192,128]{2,1,0:T(8,128)(2,1)S(1)}, bf16[6,192,128]{2,1,0:T(8,128)(2,1)S(1)}, u32[]{:S(2)}, u32[]{:S(2)}) collective-permute-start(bf16[6,192,128]{2,1,0:T(8,128)(2,1)S(1)} %get-tuple-element.52), channel_id=1, source_target_pairs={{0,64},{1,65},{2,66},{3,67},{4,68},{5,69},{6,70},{7,71},{8,72},{9,... | collective-permute-start | bytes 884744 | tf_op jit(solution)/shard_map/ppermute | solution.py:76
  140.1 2.9 %collective-permute-start.22 = (bf16[384,3072]{1,0:T(8,128)(2,1)S(1)}, bf16[384,3072]{1,0:T(8,128)(2,1)S(1)}, u32[]{:S(2)}, u32[]{:S(2)}) collective-permute-start(bf16[384,3072]{1,0:T(8,128)(2,1)S(1)} %collective-permute-done.15.refs_10_), channel_id=1, source_target_pairs={{0,1},{1,0},{2,3},{3,2},{4,5},{5,4},{6,7},{7,6},{8,9},{9,8},{10,11... | collective-permute-start | bytes 7077896 | tf_op jit(solution)/shard_map/ppermute | solution.py:85
  143.1 5.0 %collective-permute-done.16 = bf16[6,192,128]{2,1,0:T(8,128)(2,1)S(1)} collective-permute-done((bf16[6,192,128]{2,1,0:T(8,128)(2,1)S(1)}, bf16[6,192,128]{2,1,0:T(8,128)(2,1)S(1)}, u32[]{:S(2)}, u32[]{:S(2)}) %collective-permute-start.16) | collective-permute-done | bytes 294944 | tf_op jit(solution)/shard_map/ppermute | solution.py:76
  149.5 4.6 %collective-permute-start.18 = (bf16[4,192,128]{2,1,0:T(8,128)(2,1)S(1)}, bf16[4,192,128]{2,1,0:T(8,128)(2,1)S(1)}, u32[]{:S(2)}, u32[]{:S(2)}) collective-permute-start(bf16[4,192,128]{2,1,0:T(8,128)(2,1)S(1)} %pad_maximum_fusion.9), channel_id=1, source_target_pairs={{0,16},{1,17},{2,18},{3,19},{4,20},{5,21},{6,22},{7,23},{8,24},{9,... | collective-permute-start | bytes 589832 | tf_op jit(solution)/shard_map/ppermute | solution.py:71
  154.0 4.0 %collective-permute-start.19 = (bf16[4,192,128]{2,1,0:T(8,128)(2,1)S(1)}, bf16[4,192,128]{2,1,0:T(8,128)(2,1)S(1)}, u32[]{:S(2)}, u32[]{:S(2)}) collective-permute-start(bf16[4,192,128]{2,1,0:T(8,128)(2,1)S(1)} %pad_maximum_fusion.10), channel_id=1, source_target_pairs={{0,20},{1,21},{2,22},{3,23},{4,16},{5,17},{6,18},{7,19},{8,28},{9,... | collective-permute-start | bytes 589832 | tf_op jit(solution)/shard_map/ppermute | solution.py:71
  158.1 6.3 %collective-permute-done.19 = bf16[4,192,128]{2,1,0:T(8,128)(2,1)S(1)} collective-permute-done((bf16[4,192,128]{2,1,0:T(8,128)(2,1)S(1)}, bf16[4,192,128]{2,1,0:T(8,128)(2,1)S(1)}, u32[]{:S(2)}, u32[]{:S(2)}) %collective-permute-start.19) | collective-permute-done | bytes 196640 | tf_op jit(solution)/shard_map/ppermute | solution.py:71
  164.5 3.0 %collective-permute-start.21 = (bf16[8,192,128]{2,1,0:T(8,128)(2,1)S(1)}, bf16[8,192,128]{2,1,0:T(8,128)(2,1)S(1)}, u32[]{:S(2)}, u32[]{:S(2)}) collective-permute-start(bf16[8,192,128]{2,1,0:T(8,128)(2,1)S(1)} %slice_dynamic-update-slice_fusion), channel_id=1, source_target_pairs={{0,1},{1,0},{2,3},{3,2},{4,5},{5,4},{6,7},{7,6},{8,9},{9,8},{10,11... | collective-permute-start | bytes 1179656 | tf_op jit(solution)/shard_map/ppermute | solution.py:85
  168.8 4.4 %output.1 = bf16[192,3072]{1,0:T(8,128)(2,1)} custom-call(s32[1]{0:T(128)} %bitcast.refs_0_.s_ref, bf16[2,192,128]{2,1,0:T(8,128)(2,1)S(1)} %get-tuple-element.50.refs_0_, bf16[2,192,128]{2,1,0:T(8,128)(2,1)S(1)} %get-tuple-element.82.refs_1_, bf16[2,192,128]{2,1,0:T(8,128)(2,1)S(1)} %get-tuple-element.80.refs_2_, ...), custom_call_target="tpu_custom_call" | custom-call | tf_op jit(solution)/shard_map/output/pallas_call | solution.py:460
  (92 shorter events, 16.6 us)
Async XLA Ops:
  0.0 7.7 %copy-start.8 = (s32[1,27]{1,0:T(1,128)S(1)}, s32[1,27]{1,0:T(1,128)}, u32[]{:S(2)}) copy-start(s32[1,27]{1,0:T(1,128)} %param.18) | copy-start | bytes 328
  0.0 7.7 %copy-start.7 = (f32[128]{0:T(128)S(1)}, f32[128]{0:T(128)}, u32[]{:S(2)}) copy-start(f32[128]{0:T(128)} %param.14) | copy-start | bytes 1540
  0.0 7.7 %copy-start.6 = (f32[128]{0:T(128)S(1)}, f32[128]{0:T(128)}, u32[]{:S(2)}) copy-start(f32[128]{0:T(128)} %param.13) | copy-start | bytes 1540
  4.0 29.3 %collective-permute-start.4 = (bf16[192,3072]{1,0:T(8,128)(2,1)S(1)}, bf16[192,3072]{1,0:T(8,128)(2,1)S(1)}, u32[]{:S(2)}, u32[]{:S(2)}) collective-permute-start(bf16[192,3072]{1,0:T(8,128)(2,1)S(1)} %modulate.1.refs_1_), channel_id=1, source_target_pairs={{0,64},{64,0},{1,65},{65,1},{2,66},{66,2},{3,67},{67,3},{4,68},{68... | collective-permute-start | bytes 3538952 | tf_op jit(solution)/shard_map/ppermute | solution.py:94
  12.8 20.6 %slice-start = ((s8[14155776]{0:T(1024)(128)(4,1)}), s8[4194304]{0:T(1024)(128)(4,1)S(1)}, s32[]{:S(2)}) async-start(s8[14155776]{0:T(1024)(128)(4,1)} %bitcast.9), calls=%async_computation | async-start | bytes 8388608
  12.8 20.6 %slice-start.1 = ((s8[14155776]{0:T(1024)(128)(4,1)}), s8[4194304]{0:T(1024)(128)(4,1)S(1)}, s32[]{:S(2)}) async-start(s8[14155776]{0:T(1024)(128)(4,1)} %bitcast.9), calls=%async_computation.1 | async-start | bytes 8388608
  15.5 17.9 %slice-start.2 = ((s8[14155776]{0:T(1024)(128)(4,1)}), s8[4194304]{0:T(1024)(128)(4,1)S(1)}, s32[]{:S(2)}) async-start(s8[14155776]{0:T(1024)(128)(4,1)} %bitcast.9), calls=%async_computation.2 | async-start | bytes 8388608
  15.5 17.8 %slice-start.3 = ((s8[14155776]{0:T(1024)(128)(4,1)}), s8[1572864]{0:T(1024)(128)(4,1)S(1)}, s32[]{:S(2)}) async-start(s8[14155776]{0:T(1024)(128)(4,1)} %bitcast.9), calls=%async_computation.3 | async-start | bytes 3145728
  15.5 4.0 %collective-permute-start = (bf16[4,208,384]{2,1,0:T(8,128)(2,1)S(1)}, bf16[4,208,384]{2,1,0:T(8,128)(2,1)S(1)}, u32[]{:S(2)}, u32[]{:S(2)}) collective-permute-start(bf16[4,208,384]{2,1,0:T(8,128)(2,1)S(1)} %shard_map.101), channel_id=1, source_target_pairs={{0,1},{1,0},{2,3},{3,2},{4,5},{5,4},{6,7},{7,6},{8,9},{9,8},{10,11... | collective-permute-start | bytes 1916936 | tf_op jit(solution)/shard_map/ppermute | solution.py:85
  36.2 16.0 %collective-permute-start.5 = (bf16[4,192,384]{2,1,0:T(8,128)(2,1)S(1)}, bf16[4,192,384]{2,1,0:T(8,128)(2,1)S(1)}, u32[]{:S(2)}, u32[]{:S(2)}) collective-permute-start(bf16[4,192,384]{2,1,0:T(8,128)(2,1)S(1)} %shard_map.103), channel_id=1, source_target_pairs={{0,1},{1,0},{2,3},{3,2},{4,5},{5,4},{6,7},{7,6},{8,9},{9,8},{10,11... | collective-permute-start | bytes 1769480 | tf_op jit(solution)/shard_map/ppermute | solution.py:85
  37.5 16.2 %collective-permute-start.1 = (bf16[2,208,384]{2,1,0:T(8,128)(2,1)S(1)}, bf16[2,208,384]{2,1,0:T(8,128)(2,1)S(1)}, u32[]{:S(2)}, u32[]{:S(2)}) collective-permute-start(bf16[2,208,384]{2,1,0:T(8,128)(2,1)S(1)} %pad_maximum_fusion.2), channel_id=1, source_target_pairs={{0,4},{1,5},{2,6},{3,7},{4,0},{5,1},{6,2},{7,3},{8,12},{10,14},{11... | collective-permute-start | bytes 958472 | tf_op jit(solution)/shard_map/ppermute | solution.py:66
  38.9 23.0 %collective-permute-start.2 = (bf16[2,208,384]{2,1,0:T(8,128)(2,1)S(1)}, bf16[2,208,384]{2,1,0:T(8,128)(2,1)S(1)}, u32[]{:S(2)}, u32[]{:S(2)}) collective-permute-start(bf16[2,208,384]{2,1,0:T(8,128)(2,1)S(1)} %pad_maximum_fusion.3), channel_id=1, source_target_pairs={{0,16},{1,17},{2,18},{7,23},{8,24},{9,25},{10,26},{11,27},{13,29},... | collective-permute-start | bytes 958472 | tf_op jit(solution)/shard_map/ppermute | solution.py:66
  44.3 19.6 %collective-permute-start.3 = (bf16[2,208,384]{2,1,0:T(8,128)(2,1)S(1)}, bf16[2,208,384]{2,1,0:T(8,128)(2,1)S(1)}, u32[]{:S(2)}, u32[]{:S(2)}) collective-permute-start(bf16[2,208,384]{2,1,0:T(8,128)(2,1)S(1)} %pad_maximum_fusion.4), channel_id=1, source_target_pairs={{3,23},{4,16},{5,17},{6,18},{9,29},{11,31},{12,24},{13,25},{14,26}... | collective-permute-start | bytes 958472 | tf_op jit(solution)/shard_map/ppermute | solution.py:66
  46.2 74.2 %collective-permute-start.15 = (bf16[384,3072]{1,0:T(8,128)(2,1)S(1)}, bf16[384,3072]{1,0:T(8,128)(2,1)S(1)}, u32[]{:S(2)}, u32[]{:S(2)}) collective-permute-start(bf16[384,3072]{1,0:T(8,128)(2,1)S(1)} %weight_part.1), channel_id=1, source_target_pairs={{0,96},{1,97},{2,98},{3,99},{4,100},{5,101},{6,102},{7,103},{8,104... | collective-permute-start | bytes 7077896 | tf_op jit(solution)/shard_map/ppermute | solution.py:81
  52.1 22.4 %copy-start.2 = (s32[8,8,128]{2,1,0:T(8,128)S(1)}, s32[8,8,128]{2,1,0:T(8,128)}, u32[]{:S(2)}) copy-start(s32[8,8,128]{2,1,0:T(8,128)} %constant.9.clone.refs_10_) | copy-start | bytes 98308
  52.3 11.5 %collective-permute-start.6 = (bf16[2,192,384]{2,1,0:T(8,128)(2,1)S(1)}, bf16[2,192,384]{2,1,0:T(8,128)(2,1)S(1)}, u32[]{:S(2)}, u32[]{:S(2)}) collective-permute-start(bf16[2,192,384]{2,1,0:T(8,128)(2,1)S(1)} %pad_maximum_fusion.5), channel_id=1, source_target_pairs={{0,4},{1,5},{2,6},{3,7},{4,0},{5,1},{6,2},{7,3},{8,12},{10,14},{11... | collective-permute-start | bytes 884744 | tf_op jit(solution)/shard_map/ppermute | solution.py:66
  53.7 14.1 %collective-permute-start.7 = (bf16[2,192,384]{2,1,0:T(8,128)(2,1)S(1)}, bf16[2,192,384]{2,1,0:T(8,128)(2,1)S(1)}, u32[]{:S(2)}, u32[]{:S(2)}) collective-permute-start(bf16[2,192,384]{2,1,0:T(8,128)(2,1)S(1)} %pad_maximum_fusion.6), channel_id=1, source_target_pairs={{0,16},{1,17},{2,18},{7,23},{8,24},{9,25},{10,26},{11,27},{13,29},... | collective-permute-start | bytes 884744 | tf_op jit(solution)/shard_map/ppermute | solution.py:66
  61.9 12.7 %collective-permute-start.8 = (bf16[2,192,384]{2,1,0:T(8,128)(2,1)S(1)}, bf16[2,192,384]{2,1,0:T(8,128)(2,1)S(1)}, u32[]{:S(2)}, u32[]{:S(2)}) collective-permute-start(bf16[2,192,384]{2,1,0:T(8,128)(2,1)S(1)} %pad_maximum_fusion.7), channel_id=1, source_target_pairs={{3,23},{4,16},{5,17},{6,18},{9,29},{11,31},{12,24},{13,25},{14,26}... | collective-permute-start | bytes 884744 | tf_op jit(solution)/shard_map/ppermute | solution.py:66
  75.1 22.7 %collective-permute-start.9 = (bf16[4,384,256]{2,1,0:T(8,128)(2,1)S(1)}, bf16[4,384,256]{2,1,0:T(8,128)(2,1)S(1)}, u32[]{:S(2)}, u32[]{:S(2)}) collective-permute-start(bf16[4,384,256]{2,1,0:T(8,128)(2,1)S(1)} %get-tuple-element.37), channel_id=1, source_target_pairs={{0,2},{1,7},{2,0},{3,5},{4,6},{5,3},{6,4},{7,1},{8,10},{9,15},{10,... | collective-permute-start | bytes 2359304 | tf_op jit(solution)/shard_map/ppermute | solution.py:90
  77.9 20.0 %collective-permute-start.10 = (bf16[4,384,256]{2,1,0:T(8,128)(2,1)S(1)}, bf16[4,384,256]{2,1,0:T(8,128)(2,1)S(1)}, u32[]{:S(2)}, u32[]{:S(2)}) collective-permute-start(bf16[4,384,256]{2,1,0:T(8,128)(2,1)S(1)} %get-tuple-element.38), channel_id=1, source_target_pairs={{0,32},{1,33},{2,34},{3,35},{4,36},{5,37},{6,38},{7,39},{8,40},{9,... | collective-permute-start | bytes 2359304 | tf_op jit(solution)/shard_map/ppermute | solution.py:90
  79.8 34.2 %collective-permute-start.11 = (bf16[4,384,256]{2,1,0:T(8,128)(2,1)S(1)}, bf16[4,384,256]{2,1,0:T(8,128)(2,1)S(1)}, u32[]{:S(2)}, u32[]{:S(2)}) collective-permute-start(bf16[4,384,256]{2,1,0:T(8,128)(2,1)S(1)} %get-tuple-element.46), channel_id=1, source_target_pairs={{0,8},{1,25},{2,10},{3,27},{4,12},{5,29},{6,14},{7,31},{8,0},{9,17... | collective-permute-start | bytes 2359304 | tf_op jit(solution)/shard_map/ppermute | solution.py:90
  98.0 17.4 %collective-permute-start.13 = (bf16[4,384,256]{2,1,0:T(8,128)(2,1)S(1)}, bf16[4,384,256]{2,1,0:T(8,128)(2,1)S(1)}, u32[]{:S(2)}, u32[]{:S(2)}) collective-permute-start(bf16[4,384,256]{2,1,0:T(8,128)(2,1)S(1)} %pad_maximum_fusion), channel_id=1, source_target_pairs={{0,8},{1,25},{2,10},{3,27},{4,12},{5,29},{6,14},{7,31},{8,0},{9,17... | collective-permute-start | bytes 2359304 | tf_op jit(solution)/shard_map/ppermute | solution.py:90
  103.9 11.6 %collective-permute-start.12 = (bf16[2,384,256]{2,1,0:T(8,128)(2,1)S(1)}, bf16[2,384,256]{2,1,0:T(8,128)(2,1)S(1)}, u32[]{:S(2)}, u32[]{:S(2)}) collective-permute-start(bf16[2,384,256]{2,1,0:T(8,128)(2,1)S(1)} %pad_maximum_fusion.1), channel_id=1, source_target_pairs={{0,2},{1,7},{2,0},{3,5},{4,6},{5,3},{6,4},{7,1},{8,10},{9,15},{10,... | collective-permute-start | bytes 1179656 | tf_op jit(solution)/shard_map/ppermute | solution.py:90
  106.7 8.8 %collective-permute-start.14 = (bf16[1,384,256]{2,1,0:T(8,128)(2,1)S(1)}, bf16[1,384,256]{2,1,0:T(8,128)(2,1)S(1)}, u32[]{:S(2)}, u32[]{:S(2)}) collective-permute-start(bf16[1,384,256]{2,1,0:T(8,128)(2,1)S(1)} %get-tuple-element.57), channel_id=1, source_target_pairs={{0,10},{1,31},{2,8},{3,29},{4,14},{5,27},{6,12},{7,25},{8,2},{9,23... | collective-permute-start | bytes 589832 | tf_op jit(solution)/shard_map/ppermute | solution.py:90
  120.4 43.9 %collective-permute-start.20 = (bf16[2,192,128]{2,1,0:T(8,128)(2,1)S(1)}, bf16[2,192,128]{2,1,0:T(8,128)(2,1)S(1)}, u32[]{:S(2)}, u32[]{:S(2)}) collective-permute-start(bf16[2,192,128]{2,1,0:T(8,128)(2,1)S(1)} %get-tuple-element.53), channel_id=1, source_target_pairs={{0,64},{1,65},{2,66},{3,67},{4,68},{5,69},{6,70},{7,71},{8,72},{9,... | collective-permute-start | bytes 294920 | tf_op jit(solution)/shard_map/ppermute | solution.py:76
  136.8 11.2 %collective-permute-start.16 = (bf16[6,192,128]{2,1,0:T(8,128)(2,1)S(1)}, bf16[6,192,128]{2,1,0:T(8,128)(2,1)S(1)}, u32[]{:S(2)}, u32[]{:S(2)}) collective-permute-start(bf16[6,192,128]{2,1,0:T(8,128)(2,1)S(1)} %get-tuple-element.52), channel_id=1, source_target_pairs={{0,64},{1,65},{2,66},{3,67},{4,68},{5,69},{6,70},{7,71},{8,72},{9,... | collective-permute-start | bytes 884744 | tf_op jit(solution)/shard_map/ppermute | solution.py:76
  140.1 28.7 %collective-permute-start.22 = (bf16[384,3072]{1,0:T(8,128)(2,1)S(1)}, bf16[384,3072]{1,0:T(8,128)(2,1)S(1)}, u32[]{:S(2)}, u32[]{:S(2)}) collective-permute-start(bf16[384,3072]{1,0:T(8,128)(2,1)S(1)} %collective-permute-done.15.refs_10_), channel_id=1, source_target_pairs={{0,1},{1,0},{2,3},{3,2},{4,5},{5,4},{6,7},{7,6},{8,9},{9,8},{10,11... | collective-permute-start | bytes 7077896 | tf_op jit(solution)/shard_map/ppermute | solution.py:85
  148.1 20.7 %copy-start.5 = (f32[3072]{0:T(1024)S(1)}, f32[3072]{0:T(1024)}, u32[]{:S(2)}) copy-start(f32[3072]{0:T(1024)} %param.17) | copy-start | bytes 36868
  148.1 9.9 %collective-permute-start.17 = (bf16[4,192,128]{2,1,0:T(8,128)(2,1)S(1)}, bf16[4,192,128]{2,1,0:T(8,128)(2,1)S(1)}, u32[]{:S(2)}, u32[]{:S(2)}) collective-permute-start(bf16[4,192,128]{2,1,0:T(8,128)(2,1)S(1)} %pad_maximum_fusion.8), channel_id=1, source_target_pairs={{0,4},{1,5},{2,6},{3,7},{4,0},{5,1},{6,2},{7,3},{8,12},{9,13},{10,... | collective-permute-start | bytes 589832 | tf_op jit(solution)/shard_map/ppermute | solution.py:71
  149.5 8.6 %collective-permute-start.18 = (bf16[4,192,128]{2,1,0:T(8,128)(2,1)S(1)}, bf16[4,192,128]{2,1,0:T(8,128)(2,1)S(1)}, u32[]{:S(2)}, u32[]{:S(2)}) collective-permute-start(bf16[4,192,128]{2,1,0:T(8,128)(2,1)S(1)} %pad_maximum_fusion.9), channel_id=1, source_target_pairs={{0,16},{1,17},{2,18},{3,19},{4,20},{5,21},{6,22},{7,23},{8,24},{9,... | collective-permute-start | bytes 589832 | tf_op jit(solution)/shard_map/ppermute | solution.py:71
  154.0 10.3 %collective-permute-start.19 = (bf16[4,192,128]{2,1,0:T(8,128)(2,1)S(1)}, bf16[4,192,128]{2,1,0:T(8,128)(2,1)S(1)}, u32[]{:S(2)}, u32[]{:S(2)}) collective-permute-start(bf16[4,192,128]{2,1,0:T(8,128)(2,1)S(1)} %pad_maximum_fusion.10), channel_id=1, source_target_pairs={{0,20},{1,21},{2,22},{3,23},{4,16},{5,17},{6,18},{7,19},{8,28},{9,... | collective-permute-start | bytes 589832 | tf_op jit(solution)/shard_map/ppermute | solution.py:71
  164.5 4.3 %collective-permute-start.21 = (bf16[8,192,128]{2,1,0:T(8,128)(2,1)S(1)}, bf16[8,192,128]{2,1,0:T(8,128)(2,1)S(1)}, u32[]{:S(2)}, u32[]{:S(2)}) collective-permute-start(bf16[8,192,128]{2,1,0:T(8,128)(2,1)S(1)} %slice_dynamic-update-slice_fusion), channel_id=1, source_target_pairs={{0,1},{1,0},{2,3},{3,2},{4,5},{5,4},{6,7},{7,6},{8,9},{9,8},{10,11... | collective-permute-start | bytes 1179656 | tf_op jit(solution)/shard_map/ppermute | solution.py:85
  (6 other events, 18.1 us)

commit v5 on v4

--- a/solution.py
+++ b/solution.py
@@ -429,50 +429,50 @@
     s = s_ref[0]
     mine = s & 1
 
-    @pl.when(pl.program_id(0) == 0)
-    def _():
-        for p in range(4):
-            for core, pieces in (
-                (mine, (same[p].at[0], cross[p].at[0])),
-                (1 - mine, (core_ref.at[p], core_ref.at[4 + p])),
-            ):
-                slot = slot_of(s, core, p)
-                far_ref = xc_ref if core is mine else xd_ref
-
-                @pl.when(slot < 3)
-                def _(core=core, slot=slot, pieces=pieces, far_ref=far_ref):
-                    x_ref[:, pl.ds(pl.multiple_of((core * 3 + slot) * HD, HD), HD)] = pieces[0][...]
-                    far_ref[:, pl.ds(pl.multiple_of(slot * HD, HD), HD)] = pieces[1][...]
-
-    def dot(x, w):
-        return jnp.dot(x[...], w[...], preferred_element_type=jnp.float32)
-
-    near = dot(x_ref, w_ref).astype(jnp.bfloat16).astype(jnp.float32)
-    far = (dot(xc_ref, wc_ref) + dot(xd_ref, wd_ref)).astype(jnp.bfloat16).astype(jnp.float32)
-    out_ref[...] = (gate_ref[...] * (near + far)).astype(jnp.bfloat16)
+    for p in range(4):
+        for core, pieces in (
+            (mine, (same[p].at[0], cross[p].at[0])),
+            (1 - mine, (core_ref.at[p], core_ref.at[4 + p])),
+        ):
+            slot = slot_of(s, core, p)
+            far_ref = xc_ref if core is mine else xd_ref
+
+            @pl.when(slot < 3)
+            def _(core=core, slot=slot, pieces=pieces, far_ref=far_ref):
+                x_ref[:, pl.ds(pl.multiple_of((core * 3 + slot) * HD, HD), HD)] = pieces[0][...]
+                far_ref[:, pl.ds(pl.multiple_of(slot * HD, HD), HD)] = pieces[1][...]
+
+    cols = 1024
+
+    def one_part(n, _):
+        at = pl.ds(pl.multiple_of(n * cols, cols), cols)
+
+        def dot(x, w):
+            return jnp.dot(x[...], w[:, at], preferred_element_type=jnp.float32)
+
+        near = dot(x_ref, w_ref).astype(jnp.bfloat16).astype(jnp.float32)
+        far = (dot(xc_ref, wc_ref) + dot(xd_ref, wd_ref)).astype(jnp.bfloat16).astype(jnp.float32)
+        out_ref[:, at] = (gate_ref[:, at] * (near + far)).astype(jnp.bfloat16)
+        return 0
+
+    lax.fori_loop(0, out_ref.shape[1] // cols, one_part, 0)
 
 
 def output(slab_at, same, cross, core, weight, weight_c, weight_d, gate):
     inner, width = weight.shape
     half = TILE // 2
-    cols = 1024
-    by_col = lambda rows: pl.BlockSpec((rows, cols), lambda n, s_ref: (0, n))
+    vmem = pl.BlockSpec(memory_space=pltpu.VMEM)
     return pl.pallas_call(
         output_kernel,
         out_shape=jax.ShapeDtypeStruct((half, width), jnp.bfloat16),
-        grid_spec=pltpu.PrefetchScalarGridSpec(
-            num_scalar_prefetch=1,
-            grid=(width // cols,),
-            in_specs=[whole((1, half, HD))] * 8
-            + [whole((8, half, HD)), by_col(inner), by_col(inner // 2), by_col(inner // 2), by_col(1)],
-            out_specs=by_col(half),
-            scratch_shapes=[
-                pltpu.VMEM((half, inner), jnp.bfloat16),
-                pltpu.VMEM((half, inner // 2), jnp.bfloat16),
-                pltpu.VMEM((half, inner // 2), jnp.bfloat16),
-            ],
-        ),
-        compiler_params=pltpu.CompilerParams(vmem_limit_bytes=10 << 20),
+        in_specs=[pl.BlockSpec(memory_space=pltpu.SMEM)] + [vmem] * 13,
+        out_specs=vmem,
+        scratch_shapes=[
+            pltpu.VMEM((half, inner), jnp.bfloat16),
+            pltpu.VMEM((half, inner // 2), jnp.bfloat16),
+            pltpu.VMEM((half, inner // 2), jnp.bfloat16),
+        ],
+        compiler_params=pltpu.CompilerParams(vmem_limit_bytes=20 << 20),
         name="output",
     )(slab_at, *same, *cross, core, weight, weight_c, weight_d, gate)
 

time: 174 us -> 174 us (level)
  no operation moved by 1% of the time
where the time goes in v5:
time: 174 us; the launch traced here: 173 us
  starting transfers between devices  73.6 us (42%)
  Pallas kernels  51.4 us (30%)
  waiting for transfers between devices  38.4 us (22%)
  local copies, waits for them, and re-layouts  8.25 us (5%)
    ppermute x6, starting transfers between devices, to_block(): return lax.ppermute(value, 'slab', pairs)  21.9 us
    ppermute x6, starting transfers between devices, to_chip(): return lax.ppermute(value, 'slab', pairs)  19.9 us
    pallas_call x2, Pallas kernels, attend_halo(): pl.pallas_call(lambda *refs: halo_kernel(first, *refs), out_shape=[jax.Sh...  17.9 us
    pallas_call x2, Pallas kernels, attend_own(): pl.pallas_call(lambda *refs: own_kernel(first, *refs), out_shape=[state,...  16.6 us
    ppermute x1, waiting for transfers between devices, to_group(): return lax.ppermute(value, 'heads', [(0, 1), (1, 0)])  13.7 us
    pallas_call x4, Pallas kernels, project(): pl.pallas_call(lambda *refs: project_kernel(other, *refs), out_shape=jax....  11 us
    ppermute x6, waiting for transfers between devices, to_chip(): return lax.ppermute(value, 'slab', pairs)  10.7 us
    ppermute x3, starting transfers between devices, from_chip(): return lax.ppermute(value, 'slab', pairs)  9.83 us
  transfers between devices with their start and end apart: 23, of which 7 were waited for; matrix products, arithmetic and copies ran while one was open for 1% of the time, Pallas kernels for 25%

profile of v5, /device:TPU:17, one launch (start us, length us, event | category | flops | bytes accessed | tf_op | source)
XLA Modules:
  0.0 172.8 jit_solution(2312530257759424922)
XLA Ops:
  4.0 3.7 %collective-permute-start.4 = (bf16[192,3072]{1,0:T(8,128)(2,1)S(1)}, bf16[192,3072]{1,0:T(8,128)(2,1)S(1)}, u32[]{:S(2)}, u32[]{:S(2)}) collective-permute-start(bf16[192,3072]{1,0:T(8,128)(2,1)S(1)} %modulate.1.refs_1_), channel_id=1, source_target_pairs={{0,64},{64,0},{1,65},{65,1},{2,66},{66,2},{3,67},{67,3},{4,68},{68... | collective-permute-start | bytes 3538952 | tf_op jit(solution)/shard_map/ppermute | solution.py:94
  7.8 5.0 %copy-done = bf16[3072,2304]{1,0:T(8,128)(2,1)S(1)} copy-done((bf16[3072,2304]{1,0:T(8,128)(2,1)S(1)}, bf16[3072,2304]{1,0:T(8,128)(2,1)}, u32[]{:S(2)}) %copy-start) | copy-done | bytes 14155800
  12.8 2.7 %shard_map.101 = bf16[4,208,384]{2,1,0:T(8,128)(2,1)S(1)} custom-call(s32[1]{0:T(128)} %bitcast.refs_0_.s_ref, bf16[192,3072]{1,0:T(8,128)(2,1)S(1)} %modulate.1.refs_1_, bf16[3072,2304]{1,0:T(8,128)(2,1)S(1)} %copy-done, f32[1,128]{1,0:T(1,128)S(1)} %bitcast.16, f32[1,128]{1,0:T(1,128)S(1)} %bitcast.20, bf16[16,384]{1,0:T(8,128)(2,1)S(1)} %pad.7.refs_5_), custom_call_target="tpu_custom_call" | custom-call | tf_op jit(solution)/shard_map/pallas_call | solution.py:167
  16.6 2.7 %shard_map.100.refs_0_ = bf16[4,208,384]{2,1,0:T(8,128)(2,1)S(1)} custom-call(s32[1]{0:T(128)} %bitcast.refs_0_.s_ref, bf16[192,3072]{1,0:T(8,128)(2,1)S(1)} %modulate.1.refs_1_, bf16[3072,2304]{1,0:T(8,128)(2,1)S(1)} %copy-done, f32[1,128]{1,0:T(1,128)S(1)} %bitcast.17, f32[1,128]{1,0:T(1,128)S(1)} %bitcast.21, bf16[16,384]{1,0:T(8,128)(2,1)S(1)} %pad.7.refs_5_), custom_call_target="tpu_custom_call" | custom-call | tf_op jit(solution)/shard_map/pallas_call | solution.py:167
  19.7 13.7 %collective-permute-done.4.refs_1_ = bf16[192,3072]{1,0:T(8,128)(2,1)S(1)} collective-permute-done((bf16[192,3072]{1,0:T(8,128)(2,1)S(1)}, bf16[192,3072]{1,0:T(8,128)(2,1)S(1)}, u32[]{:S(2)}, u32[]{:S(2)}) %collective-permute-start.4) | collective-permute-done | bytes 1179680 | tf_op jit(solution)/shard_map/ppermute | solution.py:94
  33.4 2.8 %shard_map.103 = bf16[4,192,384]{2,1,0:T(8,128)(2,1)S(1)} custom-call(s32[1]{0:T(128)} %bitcast.refs_0_.s_ref, bf16[192,3072]{1,0:T(8,128)(2,1)S(1)} %collective-permute-done.4.refs_1_, bf16[3072,2304]{1,0:T(8,128)(2,1)S(1)} %bitcast.10, f32[1,128]{1,0:T(1,128)S(1)} %bitcast.18, f32[1,128]{1,0:T(1,128)S(1)} %bitcast.22, bf16[16,384]{1,0:T(8,128)(2,1)S(1)} %pad.7.refs_5_), custom_call_target="tpu_custom_call" | custom-call | tf_op jit(solution)/shard_map/pallas_call | solution.py:167
  38.9 5.3 %collective-permute-start.2 = (bf16[2,208,384]{2,1,0:T(8,128)(2,1)S(1)}, bf16[2,208,384]{2,1,0:T(8,128)(2,1)S(1)}, u32[]{:S(2)}, u32[]{:S(2)}) collective-permute-start(bf16[2,208,384]{2,1,0:T(8,128)(2,1)S(1)} %pad_maximum_fusion.3), channel_id=1, source_target_pairs={{0,16},{1,17},{2,18},{7,23},{8,24},{9,25},{10,26},{11,27},{13,29},... | collective-permute-start | bytes 958472 | tf_op jit(solution)/shard_map/ppermute | solution.py:66
  44.3 1.9 %collective-permute-start.3 = (bf16[2,208,384]{2,1,0:T(8,128)(2,1)S(1)}, bf16[2,208,384]{2,1,0:T(8,128)(2,1)S(1)}, u32[]{:S(2)}, u32[]{:S(2)}) collective-permute-start(bf16[2,208,384]{2,1,0:T(8,128)(2,1)S(1)} %pad_maximum_fusion.4), channel_id=1, source_target_pairs={{3,23},{4,16},{5,17},{6,18},{9,29},{11,31},{12,24},{13,25},{14,26}... | collective-permute-start | bytes 958472 | tf_op jit(solution)/shard_map/ppermute | solution.py:66
  46.2 3.2 %collective-permute-start.15 = (bf16[384,3072]{1,0:T(8,128)(2,1)S(1)}, bf16[384,3072]{1,0:T(8,128)(2,1)S(1)}, u32[]{:S(2)}, u32[]{:S(2)}) collective-permute-start(bf16[384,3072]{1,0:T(8,128)(2,1)S(1)} %weight_part.1), channel_id=1, source_target_pairs={{0,96},{1,97},{2,98},{3,99},{4,100},{5,101},{6,102},{7,103},{8,104... | collective-permute-start | bytes 7077896 | tf_op jit(solution)/shard_map/ppermute | solution.py:81
  49.4 2.7 %shard_map.102.refs_5_ = bf16[4,192,384]{2,1,0:T(8,128)(2,1)S(1)} custom-call(s32[1]{0:T(128)} %bitcast.refs_0_.s_ref, bf16[192,3072]{1,0:T(8,128)(2,1)S(1)} %collective-permute-done.4.refs_1_, bf16[3072,2304]{1,0:T(8,128)(2,1)S(1)} %bitcast.10, f32[1,128]{1,0:T(1,128)S(1)} %bitcast.19, f32[1,128]{1,0:T(1,128)S(1)} %bitcast.23, bf16[16,384]{1,0:T(8,128)(2,1)S(1)} %pad.7.refs_5_), custom_call_target="tpu_custom_call" | custom-call | tf_op jit(solution)/shard_map/pallas_call | solution.py:167
  53.7 8.2 %collective-permute-start.7 = (bf16[2,192,384]{2,1,0:T(8,128)(2,1)S(1)}, bf16[2,192,384]{2,1,0:T(8,128)(2,1)S(1)}, u32[]{:S(2)}, u32[]{:S(2)}) collective-permute-start(bf16[2,192,384]{2,1,0:T(8,128)(2,1)S(1)} %pad_maximum_fusion.6), channel_id=1, source_target_pairs={{0,16},{1,17},{2,18},{7,23},{8,24},{9,25},{10,26},{11,27},{13,29},... | collective-permute-start | bytes 884744 | tf_op jit(solution)/shard_map/ppermute | solution.py:66
  61.9 1.9 %collective-permute-start.8 = (bf16[2,192,384]{2,1,0:T(8,128)(2,1)S(1)}, bf16[2,192,384]{2,1,0:T(8,128)(2,1)S(1)}, u32[]{:S(2)}, u32[]{:S(2)}) collective-permute-start(bf16[2,192,384]{2,1,0:T(8,128)(2,1)S(1)} %pad_maximum_fusion.7), channel_id=1, source_target_pairs={{3,23},{4,16},{5,17},{6,18},{9,29},{11,31},{12,24},{13,25},{14,26}... | collective-permute-start | bytes 884744 | tf_op jit(solution)/shard_map/ppermute | solution.py:66
  63.9 4.0 %collective-permute-done.7.refs_8_ = bf16[2,192,384]{2,1,0:T(8,128)(2,1)S(1)} collective-permute-done((bf16[2,192,384]{2,1,0:T(8,128)(2,1)S(1)}, bf16[2,192,384]{2,1,0:T(8,128)(2,1)S(1)}, u32[]{:S(2)}, u32[]{:S(2)}) %collective-permute-start.7) | collective-permute-done | bytes 294944 | tf_op jit(solution)/shard_map/ppermute | solution.py:66
  67.8 6.7 %collective-permute-done.8.refs_9_ = bf16[2,192,384]{2,1,0:T(8,128)(2,1)S(1)} collective-permute-done((bf16[2,192,384]{2,1,0:T(8,128)(2,1)S(1)}, bf16[2,192,384]{2,1,0:T(8,128)(2,1)S(1)}, u32[]{:S(2)}, u32[]{:S(2)}) %collective-permute-start.8) | collective-permute-done | bytes 294944 | tf_op jit(solution)/shard_map/ppermute | solution.py:66
  75.1 2.7 %collective-permute-start.9 = (bf16[4,384,256]{2,1,0:T(8,128)(2,1)S(1)}, bf16[4,384,256]{2,1,0:T(8,128)(2,1)S(1)}, u32[]{:S(2)}, u32[]{:S(2)}) collective-permute-start(bf16[4,384,256]{2,1,0:T(8,128)(2,1)S(1)} %get-tuple-element.37), channel_id=1, source_target_pairs={{0,2},{1,7},{2,0},{3,5},{4,6},{5,3},{6,4},{7,1},{8,10},{9,15},{10,... | collective-permute-start | bytes 2359304 | tf_op jit(solution)/shard_map/ppermute | solution.py:90
  79.8 5.1 %collective-permute-start.11 = (bf16[4,384,256]{2,1,0:T(8,128)(2,1)S(1)}, bf16[4,384,256]{2,1,0:T(8,128)(2,1)S(1)}, u32[]{:S(2)}, u32[]{:S(2)}) collective-permute-start(bf16[4,384,256]{2,1,0:T(8,128)(2,1)S(1)} %get-tuple-element.46), channel_id=1, source_target_pairs={{0,8},{1,25},{2,10},{3,27},{4,12},{5,29},{6,14},{7,31},{8,0},{9,17... | collective-permute-start | bytes 2359304 | tf_op jit(solution)/shard_map/ppermute | solution.py:90
  84.9 12.9 %shard_map.104 = (f32[8,384,128]{2,1,0:T(8,128)S(1)}, f32[8,384,128]{2,1,0:T(8,128)S(1)}, f32[8,384,128]{2,1,0:T(8,128)S(1)}) custom-call(s32[8,128]{1,0:T(8,128)S(1)} %get-tuple-element.31.refs_0_.refs_1_, bf16[8,384,128]{2,1,0:T(8,128)(2,1)S(1)} %get-tuple-element.32.refs_1_.refs_2_, bf16[8,384,256]{2,1,0:T(8,128)(2,1)S(1)} %get-tuple-element.33.refs_2_), custom_call_target="tpu_custom_call" | custom-call | tf_op jit(solution)/shard_map/pallas_call | solution.py:352
  98.0 5.7 %collective-permute-start.13 = (bf16[4,384,256]{2,1,0:T(8,128)(2,1)S(1)}, bf16[4,384,256]{2,1,0:T(8,128)(2,1)S(1)}, u32[]{:S(2)}, u32[]{:S(2)}) collective-permute-start(bf16[4,384,256]{2,1,0:T(8,128)(2,1)S(1)} %pad_maximum_fusion), channel_id=1, source_target_pairs={{0,8},{1,25},{2,10},{3,27},{4,12},{5,29},{6,14},{7,31},{8,0},{9,17... | collective-permute-start | bytes 2359304 | tf_op jit(solution)/shard_map/ppermute | solution.py:90
  103.9 2.8 %collective-permute-start.12 = (bf16[2,384,256]{2,1,0:T(8,128)(2,1)S(1)}, bf16[2,384,256]{2,1,0:T(8,128)(2,1)S(1)}, u32[]{:S(2)}, u32[]{:S(2)}) collective-permute-start(bf16[2,384,256]{2,1,0:T(8,128)(2,1)S(1)} %pad_maximum_fusion.1), channel_id=1, source_target_pairs={{0,2},{1,7},{2,0},{3,5},{4,6},{5,3},{6,4},{7,1},{8,10},{9,15},{10,... | collective-permute-start | bytes 1179656 | tf_op jit(solution)/shard_map/ppermute | solution.py:90
  106.7 3.6 %collective-permute-start.14 = (bf16[1,384,256]{2,1,0:T(8,128)(2,1)S(1)}, bf16[1,384,256]{2,1,0:T(8,128)(2,1)S(1)}, u32[]{:S(2)}, u32[]{:S(2)}) collective-permute-start(bf16[1,384,256]{2,1,0:T(8,128)(2,1)S(1)} %get-tuple-element.57), channel_id=1, source_target_pairs={{0,10},{1,31},{2,8},{3,29},{4,14},{5,27},{6,12},{7,25},{8,2},{9,23... | collective-permute-start | bytes 589832 | tf_op jit(solution)/shard_map/ppermute | solution.py:90
  110.3 3.7 %shard_map.105 = (f32[8,384,128]{2,1,0:T(8,128)S(1)}, f32[8,384,128]{2,1,0:T(8,128)S(1)}, f32[8,384,128]{2,1,0:T(8,128)S(1)}) custom-call(s32[8,128]{1,0:T(8,128)S(1)} %get-tuple-element.31.refs_0_.refs_1_, bf16[8,384,128]{2,1,0:T(8,128)(2,1)S(1)} %get-tuple-element.32.refs_1_.refs_2_, ...), custom_call_target="tpu_custom_call", output_to_operand_aliasing={{0}: (3, {}), {1}: (4, {}), {2}: (5, {})} | custom-call | tf_op jit(solution)/shard_map/pallas_call | solution.py:352
  115.4 5.0 %shard_map.106 = (bf16[2,192,128]{2,1,0:T(8,128)(2,1)S(1)}, bf16[2,192,128]{2,1,0:T(8,128)(2,1)S(1)}) custom-call(s32[1]{0:T(128)} %bitcast.refs_0_.s_ref, s32[8,128]{1,0:T(8,128)S(1)} %get-tuple-element.31.refs_0_.refs_1_, bf16[8,384,128]{2,1,0:T(8,128)(2,1)S(1)} %get-tuple-element.32.refs_1_.refs_2_, f32[8,384,128]{2,1,0:T(8,128)S(1)} %get-tuple-element.42.refs_3_, ...), custom_call_target="tpu_custom_call" | custom-call | tf_op jit(solution)/shard_map/pallas_call | solution.py:404
  120.4 3.5 %collective-permute-start.20 = (bf16[2,192,128]{2,1,0:T(8,128)(2,1)S(1)}, bf16[2,192,128]{2,1,0:T(8,128)(2,1)S(1)}, u32[]{:S(2)}, u32[]{:S(2)}) collective-permute-start(bf16[2,192,128]{2,1,0:T(8,128)(2,1)S(1)} %get-tuple-element.53), channel_id=1, source_target_pairs={{0,64},{1,65},{2,66},{3,67},{4,68},{5,69},{6,70},{7,71},{8,72},{9,... | collective-permute-start | bytes 294920 | tf_op jit(solution)/shard_map/ppermute | solution.py:76
  123.9 12.9 %shard_map.107 = (bf16[6,192,128]{2,1,0:T(8,128)(2,1)S(1)}, bf16[6,192,128]{2,1,0:T(8,128)(2,1)S(1)}) custom-call(s32[1]{0:T(128)} %bitcast.refs_0_.s_ref, s32[8,128]{1,0:T(8,128)S(1)} %get-tuple-element.31.refs_0_.refs_1_, bf16[8,384,128]{2,1,0:T(8,128)(2,1)S(1)} %get-tuple-element.32.refs_1_.refs_2_, f32[8,384,128]{2,1,0:T(8,128)S(1)} %get-tuple-element.42.refs_3_, ...), custom_call_target="tpu_custom_call" | custom-call | tf_op jit(solution)/shard_map/pallas_call | solution.py:404
  136.8 3.3 %collective-permute-start.16 = (bf16[6,192,128]{2,1,0:T(8,128)(2,1)S(1)}, bf16[6,192,128]{2,1,0:T(8,128)(2,1)S(1)}, u32[]{:S(2)}, u32[]{:S(2)}) collective-permute-start(bf16[6,192,128]{2,1,0:T(8,128)(2,1)S(1)} %get-tuple-element.52), channel_id=1, source_target_pairs={{0,64},{1,65},{2,66},{3,67},{4,68},{5,69},{6,70},{7,71},{8,72},{9,... | collective-permute-start | bytes 884744 | tf_op jit(solution)/shard_map/ppermute | solution.py:76
  140.1 2.9 %collective-permute-start.22 = (bf16[384,3072]{1,0:T(8,128)(2,1)S(1)}, bf16[384,3072]{1,0:T(8,128)(2,1)S(1)}, u32[]{:S(2)}, u32[]{:S(2)}) collective-permute-start(bf16[384,3072]{1,0:T(8,128)(2,1)S(1)} %collective-permute-done.15.refs_10_), channel_id=1, source_target_pairs={{0,1},{1,0},{2,3},{3,2},{4,5},{5,4},{6,7},{7,6},{8,9},{9,8},{10,11... | collective-permute-start | bytes 7077896 | tf_op jit(solution)/shard_map/ppermute | solution.py:85
  143.1 5.0 %collective-permute-done.16 = bf16[6,192,128]{2,1,0:T(8,128)(2,1)S(1)} collective-permute-done((bf16[6,192,128]{2,1,0:T(8,128)(2,1)S(1)}, bf16[6,192,128]{2,1,0:T(8,128)(2,1)S(1)}, u32[]{:S(2)}, u32[]{:S(2)}) %collective-permute-start.16) | collective-permute-done | bytes 294944 | tf_op jit(solution)/shard_map/ppermute | solution.py:76
  149.5 4.6 %collective-permute-start.18 = (bf16[4,192,128]{2,1,0:T(8,128)(2,1)S(1)}, bf16[4,192,128]{2,1,0:T(8,128)(2,1)S(1)}, u32[]{:S(2)}, u32[]{:S(2)}) collective-permute-start(bf16[4,192,128]{2,1,0:T(8,128)(2,1)S(1)} %pad_maximum_fusion.9), channel_id=1, source_target_pairs={{0,16},{1,17},{2,18},{3,19},{4,20},{5,21},{6,22},{7,23},{8,24},{9,... | collective-permute-start | bytes 589832 | tf_op jit(solution)/shard_map/ppermute | solution.py:71
  154.0 4.0 %collective-permute-start.19 = (bf16[4,192,128]{2,1,0:T(8,128)(2,1)S(1)}, bf16[4,192,128]{2,1,0:T(8,128)(2,1)S(1)}, u32[]{:S(2)}, u32[]{:S(2)}) collective-permute-start(bf16[4,192,128]{2,1,0:T(8,128)(2,1)S(1)} %pad_maximum_fusion.10), channel_id=1, source_target_pairs={{0,20},{1,21},{2,22},{3,23},{4,16},{5,17},{6,18},{7,19},{8,28},{9,... | collective-permute-start | bytes 589832 | tf_op jit(solution)/shard_map/ppermute | solution.py:71
  158.1 6.3 %collective-permute-done.19 = bf16[4,192,128]{2,1,0:T(8,128)(2,1)S(1)} collective-permute-done((bf16[4,192,128]{2,1,0:T(8,128)(2,1)S(1)}, bf16[4,192,128]{2,1,0:T(8,128)(2,1)S(1)}, u32[]{:S(2)}, u32[]{:S(2)}) %collective-permute-start.19) | collective-permute-done | bytes 196640 | tf_op jit(solution)/shard_map/ppermute | solution.py:71
  164.5 3.0 %collective-permute-start.21 = (bf16[8,192,128]{2,1,0:T(8,128)(2,1)S(1)}, bf16[8,192,128]{2,1,0:T(8,128)(2,1)S(1)}, u32[]{:S(2)}, u32[]{:S(2)}) collective-permute-start(bf16[8,192,128]{2,1,0:T(8,128)(2,1)S(1)} %slice_dynamic-update-slice_fusion), channel_id=1, source_target_pairs={{0,1},{1,0},{2,3},{3,2},{4,5},{5,4},{6,7},{7,6},{8,9},{9,8},{10,11... | collective-permute-start | bytes 1179656 | tf_op jit(solution)/shard_map/ppermute | solution.py:85
  168.8 4.0 %output.1 = bf16[192,3072]{1,0:T(8,128)(2,1)} custom-call(s32[1]{0:T(128)} %bitcast.refs_0_.s_ref, bf16[2,192,128]{2,1,0:T(8,128)(2,1)S(1)} %get-tuple-element.50.refs_0_, bf16[2,192,128]{2,1,0:T(8,128)(2,1)S(1)} %get-tuple-element.82.refs_1_, bf16[2,192,128]{2,1,0:T(8,128)(2,1)S(1)} %get-tuple-element.80.refs_2_, ...), custom_call_target="tpu_custom_call" | custom-call | tf_op jit(solution)/shard_map/output/pallas_call | solution.py:465
  (92 shorter events, 16.6 us)
Async XLA Ops:
  0.0 7.7 %copy-start.8 = (s32[1,27]{1,0:T(1,128)S(1)}, s32[1,27]{1,0:T(1,128)}, u32[]{:S(2)}) copy-start(s32[1,27]{1,0:T(1,128)} %param.18) | copy-start | bytes 328
  0.0 7.7 %copy-start.7 = (f32[128]{0:T(128)S(1)}, f32[128]{0:T(128)}, u32[]{:S(2)}) copy-start(f32[128]{0:T(128)} %param.14) | copy-start | bytes 1540
  0.0 7.7 %copy-start.6 = (f32[128]{0:T(128)S(1)}, f32[128]{0:T(128)}, u32[]{:S(2)}) copy-start(f32[128]{0:T(128)} %param.13) | copy-start | bytes 1540
  4.0 29.3 %collective-permute-start.4 = (bf16[192,3072]{1,0:T(8,128)(2,1)S(1)}, bf16[192,3072]{1,0:T(8,128)(2,1)S(1)}, u32[]{:S(2)}, u32[]{:S(2)}) collective-permute-start(bf16[192,3072]{1,0:T(8,128)(2,1)S(1)} %modulate.1.refs_1_), channel_id=1, source_target_pairs={{0,64},{64,0},{1,65},{65,1},{2,66},{66,2},{3,67},{67,3},{4,68},{68... | collective-permute-start | bytes 3538952 | tf_op jit(solution)/shard_map/ppermute | solution.py:94
  12.8 20.6 %slice-start = ((s8[14155776]{0:T(1024)(128)(4,1)}), s8[4194304]{0:T(1024)(128)(4,1)S(1)}, s32[]{:S(2)}) async-start(s8[14155776]{0:T(1024)(128)(4,1)} %bitcast.9), calls=%async_computation | async-start | bytes 8388608
  12.8 20.6 %slice-start.1 = ((s8[14155776]{0:T(1024)(128)(4,1)}), s8[4194304]{0:T(1024)(128)(4,1)S(1)}, s32[]{:S(2)}) async-start(s8[14155776]{0:T(1024)(128)(4,1)} %bitcast.9), calls=%async_computation.1 | async-start | bytes 8388608
  15.5 17.9 %slice-start.2 = ((s8[14155776]{0:T(1024)(128)(4,1)}), s8[4194304]{0:T(1024)(128)(4,1)S(1)}, s32[]{:S(2)}) async-start(s8[14155776]{0:T(1024)(128)(4,1)} %bitcast.9), calls=%async_computation.2 | async-start | bytes 8388608
  15.5 17.8 %slice-start.3 = ((s8[14155776]{0:T(1024)(128)(4,1)}), s8[1572864]{0:T(1024)(128)(4,1)S(1)}, s32[]{:S(2)}) async-start(s8[14155776]{0:T(1024)(128)(4,1)} %bitcast.9), calls=%async_computation.3 | async-start | bytes 3145728
  15.5 4.0 %collective-permute-start = (bf16[4,208,384]{2,1,0:T(8,128)(2,1)S(1)}, bf16[4,208,384]{2,1,0:T(8,128)(2,1)S(1)}, u32[]{:S(2)}, u32[]{:S(2)}) collective-permute-start(bf16[4,208,384]{2,1,0:T(8,128)(2,1)S(1)} %shard_map.101), channel_id=1, source_target_pairs={{0,1},{1,0},{2,3},{3,2},{4,5},{5,4},{6,7},{7,6},{8,9},{9,8},{10,11... | collective-permute-start | bytes 1916936 | tf_op jit(solution)/shard_map/ppermute | solution.py:85
  36.2 16.0 %collective-permute-start.5 = (bf16[4,192,384]{2,1,0:T(8,128)(2,1)S(1)}, bf16[4,192,384]{2,1,0:T(8,128)(2,1)S(1)}, u32[]{:S(2)}, u32[]{:S(2)}) collective-permute-start(bf16[4,192,384]{2,1,0:T(8,128)(2,1)S(1)} %shard_map.103), channel_id=1, source_target_pairs={{0,1},{1,0},{2,3},{3,2},{4,5},{5,4},{6,7},{7,6},{8,9},{9,8},{10,11... | collective-permute-start | bytes 1769480 | tf_op jit(solution)/shard_map/ppermute | solution.py:85
  37.5 16.2 %collective-permute-start.1 = (bf16[2,208,384]{2,1,0:T(8,128)(2,1)S(1)}, bf16[2,208,384]{2,1,0:T(8,128)(2,1)S(1)}, u32[]{:S(2)}, u32[]{:S(2)}) collective-permute-start(bf16[2,208,384]{2,1,0:T(8,128)(2,1)S(1)} %pad_maximum_fusion.2), channel_id=1, source_target_pairs={{0,4},{1,5},{2,6},{3,7},{4,0},{5,1},{6,2},{7,3},{8,12},{10,14},{11... | collective-permute-start | bytes 958472 | tf_op jit(solution)/shard_map/ppermute | solution.py:66
  38.9 23.0 %collective-permute-start.2 = (bf16[2,208,384]{2,1,0:T(8,128)(2,1)S(1)}, bf16[2,208,384]{2,1,0:T(8,128)(2,1)S(1)}, u32[]{:S(2)}, u32[]{:S(2)}) collective-permute-start(bf16[2,208,384]{2,1,0:T(8,128)(2,1)S(1)} %pad_maximum_fusion.3), channel_id=1, source_target_pairs={{0,16},{1,17},{2,18},{7,23},{8,24},{9,25},{10,26},{11,27},{13,29},... | collective-permute-start | bytes 958472 | tf_op jit(solution)/shard_map/ppermute | solution.py:66
  44.3 19.6 %collective-permute-start.3 = (bf16[2,208,384]{2,1,0:T(8,128)(2,1)S(1)}, bf16[2,208,384]{2,1,0:T(8,128)(2,1)S(1)}, u32[]{:S(2)}, u32[]{:S(2)}) collective-permute-start(bf16[2,208,384]{2,1,0:T(8,128)(2,1)S(1)} %pad_maximum_fusion.4), channel_id=1, source_target_pairs={{3,23},{4,16},{5,17},{6,18},{9,29},{11,31},{12,24},{13,25},{14,26}... | collective-permute-start | bytes 958472 | tf_op jit(solution)/shard_map/ppermute | solution.py:66
  46.2 74.2 %collective-permute-start.15 = (bf16[384,3072]{1,0:T(8,128)(2,1)S(1)}, bf16[384,3072]{1,0:T(8,128)(2,1)S(1)}, u32[]{:S(2)}, u32[]{:S(2)}) collective-permute-start(bf16[384,3072]{1,0:T(8,128)(2,1)S(1)} %weight_part.1), channel_id=1, source_target_pairs={{0,96},{1,97},{2,98},{3,99},{4,100},{5,101},{6,102},{7,103},{8,104... | collective-permute-start | bytes 7077896 | tf_op jit(solution)/shard_map/ppermute | solution.py:81
  52.1 22.4 %copy-start.2 = (s32[8,8,128]{2,1,0:T(8,128)S(1)}, s32[8,8,128]{2,1,0:T(8,128)}, u32[]{:S(2)}) copy-start(s32[8,8,128]{2,1,0:T(8,128)} %constant.9.clone.refs_10_) | copy-start | bytes 98308
  52.3 11.5 %collective-permute-start.6 = (bf16[2,192,384]{2,1,0:T(8,128)(2,1)S(1)}, bf16[2,192,384]{2,1,0:T(8,128)(2,1)S(1)}, u32[]{:S(2)}, u32[]{:S(2)}) collective-permute-start(bf16[2,192,384]{2,1,0:T(8,128)(2,1)S(1)} %pad_maximum_fusion.5), channel_id=1, source_target_pairs={{0,4},{1,5},{2,6},{3,7},{4,0},{5,1},{6,2},{7,3},{8,12},{10,14},{11... | collective-permute-start | bytes 884744 | tf_op jit(solution)/shard_map/ppermute | solution.py:66
  53.7 14.1 %collective-permute-start.7 = (bf16[2,192,384]{2,1,0:T(8,128)(2,1)S(1)}, bf16[2,192,384]{2,1,0:T(8,128)(2,1)S(1)}, u32[]{:S(2)}, u32[]{:S(2)}) collective-permute-start(bf16[2,192,384]{2,1,0:T(8,128)(2,1)S(1)} %pad_maximum_fusion.6), channel_id=1, source_target_pairs={{0,16},{1,17},{2,18},{7,23},{8,24},{9,25},{10,26},{11,27},{13,29},... | collective-permute-start | bytes 884744 | tf_op jit(solution)/shard_map/ppermute | solution.py:66
  61.9 12.7 %collective-permute-start.8 = (bf16[2,192,384]{2,1,0:T(8,128)(2,1)S(1)}, bf16[2,192,384]{2,1,0:T(8,128)(2,1)S(1)}, u32[]{:S(2)}, u32[]{:S(2)}) collective-permute-start(bf16[2,192,384]{2,1,0:T(8,128)(2,1)S(1)} %pad_maximum_fusion.7), channel_id=1, source_target_pairs={{3,23},{4,16},{5,17},{6,18},{9,29},{11,31},{12,24},{13,25},{14,26}... | collective-permute-start | bytes 884744 | tf_op jit(solution)/shard_map/ppermute | solution.py:66
  75.1 22.7 %collective-permute-start.9 = (bf16[4,384,256]{2,1,0:T(8,128)(2,1)S(1)}, bf16[4,384,256]{2,1,0:T(8,128)(2,1)S(1)}, u32[]{:S(2)}, u32[]{:S(2)}) collective-permute-start(bf16[4,384,256]{2,1,0:T(8,128)(2,1)S(1)} %get-tuple-element.37), channel_id=1, source_target_pairs={{0,2},{1,7},{2,0},{3,5},{4,6},{5,3},{6,4},{7,1},{8,10},{9,15},{10,... | collective-permute-start | bytes 2359304 | tf_op jit(solution)/shard_map/ppermute | solution.py:90
  77.9 20.0 %collective-permute-start.10 = (bf16[4,384,256]{2,1,0:T(8,128)(2,1)S(1)}, bf16[4,384,256]{2,1,0:T(8,128)(2,1)S(1)}, u32[]{:S(2)}, u32[]{:S(2)}) collective-permute-start(bf16[4,384,256]{2,1,0:T(8,128)(2,1)S(1)} %get-tuple-element.38), channel_id=1, source_target_pairs={{0,32},{1,33},{2,34},{3,35},{4,36},{5,37},{6,38},{7,39},{8,40},{9,... | collective-permute-start | bytes 2359304 | tf_op jit(solution)/shard_map/ppermute | solution.py:90
  79.8 34.2 %collective-permute-start.11 = (bf16[4,384,256]{2,1,0:T(8,128)(2,1)S(1)}, bf16[4,384,256]{2,1,0:T(8,128)(2,1)S(1)}, u32[]{:S(2)}, u32[]{:S(2)}) collective-permute-start(bf16[4,384,256]{2,1,0:T(8,128)(2,1)S(1)} %get-tuple-element.46), channel_id=1, source_target_pairs={{0,8},{1,25},{2,10},{3,27},{4,12},{5,29},{6,14},{7,31},{8,0},{9,17... | collective-permute-start | bytes 2359304 | tf_op jit(solution)/shard_map/ppermute | solution.py:90
  98.0 17.4 %collective-permute-start.13 = (bf16[4,384,256]{2,1,0:T(8,128)(2,1)S(1)}, bf16[4,384,256]{2,1,0:T(8,128)(2,1)S(1)}, u32[]{:S(2)}, u32[]{:S(2)}) collective-permute-start(bf16[4,384,256]{2,1,0:T(8,128)(2,1)S(1)} %pad_maximum_fusion), channel_id=1, source_target_pairs={{0,8},{1,25},{2,10},{3,27},{4,12},{5,29},{6,14},{7,31},{8,0},{9,17... | collective-permute-start | bytes 2359304 | tf_op jit(solution)/shard_map/ppermute | solution.py:90
  103.9 11.6 %collective-permute-start.12 = (bf16[2,384,256]{2,1,0:T(8,128)(2,1)S(1)}, bf16[2,384,256]{2,1,0:T(8,128)(2,1)S(1)}, u32[]{:S(2)}, u32[]{:S(2)}) collective-permute-start(bf16[2,384,256]{2,1,0:T(8,128)(2,1)S(1)} %pad_maximum_fusion.1), channel_id=1, source_target_pairs={{0,2},{1,7},{2,0},{3,5},{4,6},{5,3},{6,4},{7,1},{8,10},{9,15},{10,... | collective-permute-start | bytes 1179656 | tf_op jit(solution)/shard_map/ppermute | solution.py:90
  106.7 8.8 %collective-permute-start.14 = (bf16[1,384,256]{2,1,0:T(8,128)(2,1)S(1)}, bf16[1,384,256]{2,1,0:T(8,128)(2,1)S(1)}, u32[]{:S(2)}, u32[]{:S(2)}) collective-permute-start(bf16[1,384,256]{2,1,0:T(8,128)(2,1)S(1)} %get-tuple-element.57), channel_id=1, source_target_pairs={{0,10},{1,31},{2,8},{3,29},{4,14},{5,27},{6,12},{7,25},{8,2},{9,23... | collective-permute-start | bytes 589832 | tf_op jit(solution)/shard_map/ppermute | solution.py:90
  120.4 43.9 %collective-permute-start.20 = (bf16[2,192,128]{2,1,0:T(8,128)(2,1)S(1)}, bf16[2,192,128]{2,1,0:T(8,128)(2,1)S(1)}, u32[]{:S(2)}, u32[]{:S(2)}) collective-permute-start(bf16[2,192,128]{2,1,0:T(8,128)(2,1)S(1)} %get-tuple-element.53), channel_id=1, source_target_pairs={{0,64},{1,65},{2,66},{3,67},{4,68},{5,69},{6,70},{7,71},{8,72},{9,... | collective-permute-start | bytes 294920 | tf_op jit(solution)/shard_map/ppermute | solution.py:76
  136.8 11.2 %collective-permute-start.16 = (bf16[6,192,128]{2,1,0:T(8,128)(2,1)S(1)}, bf16[6,192,128]{2,1,0:T(8,128)(2,1)S(1)}, u32[]{:S(2)}, u32[]{:S(2)}) collective-permute-start(bf16[6,192,128]{2,1,0:T(8,128)(2,1)S(1)} %get-tuple-element.52), channel_id=1, source_target_pairs={{0,64},{1,65},{2,66},{3,67},{4,68},{5,69},{6,70},{7,71},{8,72},{9,... | collective-permute-start | bytes 884744 | tf_op jit(solution)/shard_map/ppermute | solution.py:76
  140.1 28.7 %collective-permute-start.22 = (bf16[384,3072]{1,0:T(8,128)(2,1)S(1)}, bf16[384,3072]{1,0:T(8,128)(2,1)S(1)}, u32[]{:S(2)}, u32[]{:S(2)}) collective-permute-start(bf16[384,3072]{1,0:T(8,128)(2,1)S(1)} %collective-permute-done.15.refs_10_), channel_id=1, source_target_pairs={{0,1},{1,0},{2,3},{3,2},{4,5},{5,4},{6,7},{7,6},{8,9},{9,8},{10,11... | collective-permute-start | bytes 7077896 | tf_op jit(solution)/shard_map/ppermute | solution.py:85
  148.1 20.7 %copy-start.5 = (f32[3072]{0:T(1024)S(1)}, f32[3072]{0:T(1024)}, u32[]{:S(2)}) copy-start(f32[3072]{0:T(1024)} %param.17) | copy-start | bytes 36868
  148.1 9.9 %collective-permute-start.17 = (bf16[4,192,128]{2,1,0:T(8,128)(2,1)S(1)}, bf16[4,192,128]{2,1,0:T(8,128)(2,1)S(1)}, u32[]{:S(2)}, u32[]{:S(2)}) collective-permute-start(bf16[4,192,128]{2,1,0:T(8,128)(2,1)S(1)} %pad_maximum_fusion.8), channel_id=1, source_target_pairs={{0,4},{1,5},{2,6},{3,7},{4,0},{5,1},{6,2},{7,3},{8,12},{9,13},{10,... | collective-permute-start | bytes 589832 | tf_op jit(solution)/shard_map/ppermute | solution.py:71
  149.5 8.6 %collective-permute-start.18 = (bf16[4,192,128]{2,1,0:T(8,128)(2,1)S(1)}, bf16[4,192,128]{2,1,0:T(8,128)(2,1)S(1)}, u32[]{:S(2)}, u32[]{:S(2)}) collective-permute-start(bf16[4,192,128]{2,1,0:T(8,128)(2,1)S(1)} %pad_maximum_fusion.9), channel_id=1, source_target_pairs={{0,16},{1,17},{2,18},{3,19},{4,20},{5,21},{6,22},{7,23},{8,24},{9,... | collective-permute-start | bytes 589832 | tf_op jit(solution)/shard_map/ppermute | solution.py:71
  154.0 10.3 %collective-permute-start.19 = (bf16[4,192,128]{2,1,0:T(8,128)(2,1)S(1)}, bf16[4,192,128]{2,1,0:T(8,128)(2,1)S(1)}, u32[]{:S(2)}, u32[]{:S(2)}) collective-permute-start(bf16[4,192,128]{2,1,0:T(8,128)(2,1)S(1)} %pad_maximum_fusion.10), channel_id=1, source_target_pairs={{0,20},{1,21},{2,22},{3,23},{4,16},{5,17},{6,18},{7,19},{8,28},{9,... | collective-permute-start | bytes 589832 | tf_op jit(solution)/shard_map/ppermute | solution.py:71
  164.5 4.3 %collective-permute-start.21 = (bf16[8,192,128]{2,1,0:T(8,128)(2,1)S(1)}, bf16[8,192,128]{2,1,0:T(8,128)(2,1)S(1)}, u32[]{:S(2)}, u32[]{:S(2)}) collective-permute-start(bf16[8,192,128]{2,1,0:T(8,128)(2,1)S(1)} %slice_dynamic-update-slice_fusion), channel_id=1, source_target_pairs={{0,1},{1,0},{2,3},{3,2},{4,5},{5,4},{6,7},{7,6},{8,9},{9,8},{10,11... | collective-permute-start | bytes 1179656 | tf_op jit(solution)/shard_map/ppermute | solution.py:85
  (6 other events, 18.1 us)
